TPU v7x, 128 devices: a whole 4x4x4 slice. The times are simulated.
128 devices in a mesh: gx: 16 (over y, z), gy: 8 (over x, core).
Axes of the slice: x: 4, y: 4, z: 4, core: 2. Of those that a mesh axis runs over, the one named last changes fastest.
Arguments:
- features: bfloat16 [2048, 512, 128], P('gx', 'gy'), may hold values from -6 to 6
- cotangent: bfloat16 [2048, 512, 128], P('gx', 'gy'), may hold values from -31 to 31
- kernel: float32 [7, 7, 128], replicated, may hold values from -0.875 to 0.875
- kernel_bias: float32 [128], replicated, may hold values from -3 to 3
- norm_gain: float32 [128], replicated, may hold values from 0.1 to 1.9
- norm_shift: float32 [128], replicated, may hold values from -3 to 3
- w_up: bfloat16 [128, 512], replicated, may hold values from -0.5 to 0.5
- b_up: float32 [512], replicated, may hold values from -3 to 3
- w_down: bfloat16 [512, 128], replicated, may hold values from -0.25 to 0.25
- b_down: float32 [128], replicated, may hold values from -3 to 3
- layer_scale: float32 [128], replicated, may hold values from 0.3 to 3
Outputs:
- d_features: bfloat16 [2048, 512, 128], P('gx', 'gy')
- d_kernel: float32 [7, 7, 128], replicated
- d_kernel_bias: float32 [128], replicated
- d_norm_gain: float32 [128], replicated
- d_norm_shift: float32 [128], replicated
- d_w_up: float32 [128, 512], replicated
- d_b_up: float32 [512], replicated
- d_w_down: float32 [512, 128], replicated
- d_b_down: float32 [128], replicated
- d_layer_scale: float32 [128], replicated
All inputs are finite; a program needn't handle non-finite values.
Results may differ from a plain program's by a relative error of at most 0.0072.
Values may be sent and summed in bfloat16 or wider, within the bound.
No kernel may reach another device: no remote copies, remote signals or barrier semaphores. Data moves between devices by JAX's collectives and lax.ppermute only.
A program may use at most 64 MiB of HBM per device.

v0:
```python
import math

import jax
import jax.numpy as jnp
from jax import lax
from jax.sharding import PartitionSpec as P

EPSILON = 1e-06


def extended(cells, sides, width):
    for axis, dim in sides:
        count = lax.axis_size(axis)
        head = lax.slice_in_dim(cells, 0, width, axis=dim)
        tail = lax.slice_in_dim(cells, cells.shape[dim] - width, cells.shape[dim], axis=dim)
        cells = jnp.concatenate(
            [
                lax.ppermute(tail, axis, [(i, (i + 1) % count) for i in range(count)]),
                cells,
                lax.ppermute(head, axis, [((i + 1) % count, i) for i in range(count)]),
            ],
            axis=dim,
        )
    return cells


def gelu_pair(hidden):
    erf_part = jax.scipy.special.erf(hidden * 0.7071067811865476)
    value = 0.5 * hidden * (1.0 + erf_part)
    slope_value = (
        0.5 * (1.0 + erf_part) + hidden * jnp.exp(-0.5 * hidden * hidden) * 0.3989422804014327
    )
    return (value, slope_value)


def product(spec, left, right):
    return jnp.einsum(spec, left, right, preferred_element_type=jnp.float32)


def depthwise(padded, kernel, row_count, col_count):
    tap_count = kernel.shape[0]
    accum = jnp.zeros((row_count, col_count, kernel.shape[2]), jnp.float32)
    for row_tap in range(tap_count):
        for col_tap in range(tap_count):
            window = padded[row_tap : row_tap + row_count, col_tap : col_tap + col_count]
            accum = accum + window.astype(jnp.float32) * kernel[row_tap, col_tap]
    return accum


def spread_back(padded, kernel, row_count, col_count):
    tap_count = kernel.shape[0]
    edge_cells = tap_count - 1
    accum = jnp.zeros((row_count, col_count, kernel.shape[2]), jnp.float32)
    for row_tap in range(tap_count):
        for col_tap in range(tap_count):
            window = padded[
                edge_cells - row_tap : edge_cells - row_tap + row_count,
                edge_cells - col_tap : edge_cells - col_tap + col_count,
            ]
            accum = accum + window * kernel[row_tap, col_tap]
    return accum


def kernel_grad(slopes_in, padded, tap_count):
    row_count, col_count = (slopes_in.shape[0], slopes_in.shape[1])
    rows_out = []
    for row_tap in range(tap_count):
        line = []
        for col_tap in range(tap_count):
            window = padded[row_tap : row_tap + row_count, col_tap : col_tap + col_count].astype(
                jnp.float32
            )
            line.append(jnp.sum(slopes_in * window, axis=(0, 1)))
        rows_out.append(jnp.stack(line, 0))
    return jnp.stack(rows_out, 0)


def mask_edges(padded, width):
    col_total = padded.shape[1]
    inner_cols = col_total - 2 * width
    grid_cols = inner_cols * lax.axis_size("gy")
    col_place = lax.axis_index("gy") * inner_cols + lax.iota(jnp.int32, col_total) - width
    keep_mask = (col_place >= 0) & (col_place < grid_cols)
    return jnp.where(keep_mask[None, :, None], padded, jnp.zeros((), padded.dtype))


def layer_back(conv_out, cotan, norm_gain, norm_shift, w_up, b_up, w_down, b_down, layer_scale):
    chan_mean = jnp.mean(conv_out, axis=-1, keepdims=True)
    centred = conv_out - chan_mean
    inv_std = lax.rsqrt(jnp.mean(centred * centred, axis=-1, keepdims=True) + EPSILON)
    normed = centred * inv_std
    normal_out = (normed * norm_gain + norm_shift).astype(jnp.bfloat16)
    hidden = product("rwc,ce->rwe", normal_out, w_up) + b_up
    active, gelu_slope = gelu_pair(hidden)
    active = active.astype(jnp.bfloat16)
    output = product("rwe,ec->rwc", active, w_down) + b_down
    cot_float = cotan.astype(jnp.float32)
    d_output = (cot_float * layer_scale).astype(jnp.bfloat16)
    d_active = product("rwc,ec->rwe", d_output, w_down)
    d_hidden = (d_active * gelu_slope).astype(jnp.bfloat16)
    d_normal = product("rwe,ce->rwc", d_hidden, w_up)
    d_normed = d_normal * norm_gain
    first_mean = jnp.mean(d_normed, axis=-1, keepdims=True)
    second_mean = jnp.mean(d_normed * normed, axis=-1, keepdims=True)
    d_conv = inv_std * (d_normed - first_mean - normed * second_mean)
    d_gain = jnp.sum(d_normal * normed, axis=(0, 1))
    d_shift = jnp.sum(d_normal, axis=(0, 1))
    d_wup = product("rwc,rwe->ce", normal_out, d_hidden)
    d_bup = jnp.sum(d_hidden.astype(jnp.float32), axis=(0, 1))
    d_wdown = product("rwe,rwc->ec", active, d_output)
    d_bdown = jnp.sum(d_output.astype(jnp.float32), axis=(0, 1))
    d_lscale = jnp.sum(cot_float * output, axis=(0, 1))
    return (d_conv, (d_gain, d_shift, d_wup, d_bup, d_wdown, d_bdown, d_lscale))


def local(
    features,
    cotangent,
    kernel,
    kernel_bias,
    norm_gain,
    norm_shift,
    w_up,
    b_up,
    w_down,
    b_down,
    layer_scale,
):
    tap_count = kernel.shape[0]
    reach_cells = tap_count // 2
    row_count, col_count = (features.shape[0], features.shape[1])
    padded_x = mask_edges(extended(features, (("gx", 0), ("gy", 1)), reach_cells), reach_cells)
    conv_out = depthwise(padded_x, kernel, row_count, col_count) + kernel_bias
    d_conv, layer_grads = layer_back(
        conv_out, cotangent, norm_gain, norm_shift, w_up, b_up, w_down, b_down, layer_scale
    )
    d_kern = kernel_grad(d_conv, padded_x, tap_count)
    d_kbias = jnp.sum(d_conv, axis=(0, 1))
    padded_slope = mask_edges(extended(d_conv, (("gx", 0), ("gy", 1)), reach_cells), reach_cells)
    spread = spread_back(padded_slope, kernel, row_count, col_count)
    d_features = (cotangent.astype(jnp.float32) + spread).astype(jnp.bfloat16)
    d_gain, d_shift, d_wup, d_bup, d_wdown, d_bdown, d_lscale = layer_grads
    summed = lax.psum(
        (d_kern, d_kbias, d_gain, d_shift, d_wup, d_bup, d_wdown, d_bdown, d_lscale), ("gx", "gy")
    )
    factor = 1.0 / math.sqrt(row_count * col_count * lax.axis_size("gx") * lax.axis_size("gy"))
    return (d_features,) + tuple((entry * factor for entry in summed))


def solution(mesh):
    placed = (P("gx", "gy", None), P("gx", "gy", None), P(), P(), P(), P(), P(), P(), P(), P(), P())
    return jax.shard_map(
        local,
        mesh=mesh,
        in_specs=placed,
        out_specs=(P("gx", "gy", None), P(), P(), P(), P(), P(), P(), P(), P(), P()),
        check_vma=False,
    )
```

profile of v0, /device:TPU:1, one launch (start us, length us, event | category | flops | bytes accessed | tf_op | source)
XLA Modules:
  0.0 487.0 jit_solution(8291468814353680774)
XLA Ops:
  7.3 3.1 copy.22
  10.4 2.5 collective-permute-start
  13.0 5.2 %collective-permute-start.1 = (bf16[3,64,128]{2,0,1:T(4,128)(2,1)S(1)}, bf16[3,64,128]{2,0,1:T(4,128)(2,1)S(1)}, u32[]{:S(2)}, u32[]{:S(2)}) collective-permute-start(bf16[3,64,128]{2,0,1:T(4,128)(2,1)S(1)} %get-tuple-element.93), channel_id=1, source_target_pairs={{8,0},{16,8},{24,16},{32,24},{40,32},{48,40},{56,48},{64,56},{72,6... | collective-permute-start | bytes 147464 | tf_op jit(solution)/shard_map/ppermute | solution.py:20
  19.5 2.6 collective-permute-start.2
  23.9 2.4 collective-permute-done.3
  26.3 2.9 maximum_select_fusion.1
  29.2 33.0 %fusion.163 = (f32[128,64]{0,1:T(8,128)S(1)}, f32[128,64,128]{2,0,1:T(8,128)S(1)}) fusion(f32[128]{0:T(128)S(1)} %copy-done.11, f32[128]{0:T(128)S(1)} %get-tuple-element.141, bf16[134,70,128]{2,0,1:T(8,128)(2,1)S(1)} %maximum_select_fusion.1, f32[128]{0:T(128)S(1)} %get-tuple-element.142, f32[128]{0:T(128)S(1)} %get-tuple-element.95, ...), kind=kLoop, calls=%fused_computation.403 | loop fusion | flops 155181056 | bytes 107013120 | tf_op jit(solution)/shard_map/reduce_sum | solution.py:88
  62.3 2.7 multiply_reduce_fusion.2
  65.1 8.6 %multiply_convert_fusion = (bf16[128,64,512]{2,0,1:T(8,128)(2,1)}, f32[128,64,512]{2,0,1:T(8,128)S(1)}) fusion(f32[512]{0:T(512)S(1)} %copy-done.9, bf16[128,512]{1,0:T(8,128)(2,1)S(1)} %copy-done, f32[128,64,128]{2,0,1:T(8,128)S(1)} %get-tuple-element.85, f32[128]{0:T(128)S(1)} %copy-done.8, f32[128]{0:T(128)S(1)} %copy-done.7, ...), kind=kOutput, calls=%fused_computation.7 | convolution fusion | flops 1104150528 | bytes 29559808 | tf_op jit(solution)/shard_map/rwc,ce->rwe/dot_general | solution.py:37
  73.7 10.6 %convert_reduce_fusion = (f32[512]{0:T(512)S(1)}, bf16[128,64,512]{2,0,1:T(8,128)(2,1)S(1)}) fusion(f32[128,64,512]{2,0,1:T(8,128)S(1)} %get-tuple-element.147, f32[512]{0:T(512)S(1)} %copy-done.9, bf16[512,128]{1,0:T(8,128)(2,1)S(1)} %copy-done.12, f32[128]{0:T(128)S(1)} %copy-done.10, bf16[128,64,128]{2,1,0:T(8,128)(2,1)S(1)} %copy-done.4), kind=kOutput, calls=%fused_computation.8 | convolution fusion | flops 1131412992 | bytes 27398656 | tf_op jit(solution)/shard_map/rwc,ec->rwe/dot_general | solution.py:37
  84.3 4.2 convolution_bitcast_fusion.1
  88.4 4.8 multiply_reduce_fusion
  93.2 13.4 %fusion.102 = (f32[128]{0:T(128)S(1)}, f32[128]{0:T(128)S(1)}, f32[128]{0:T(128)S(1)}, f32[128]{0:T(128)S(1)}, f32[128]{0:T(128)S(1)}, /*index=5*/f32[128]{0:T(1...) fusion(bf16[134,70,128]{2,0,1:T(8,128)(2,1)S(1)} %maximum_selec, ...), kind=kLoop, calls=%fused_computation.208 | loop fusion | flops 63960832 | bytes 50472448 | tf_op jit(solution)/shard_map/reduce_sum | solution.py:73
  106.6 11.0 %fusion.84 = (f32[128]{0:T(128)S(1)}, f32[128]{0:T(128)S(1)}, f32[128]{0:T(128)S(1)}, f32[128]{0:T(128)S(1)}, f32[128]{0:T(128)S(1)}, /*index=5*/f32[128]{0:T(12...) fusion(f32[128,64,128]{2,0,1:T(8,128)S(1)} %get-tuple-element.8, ...), kind=kLoop, calls=%fused_computation.190 | loop fusion | flops 56620800 | bytes 41952256 | tf_op jit(solution)/shard_map/reduce_sum | solution.py:73
  117.7 8.3 %fusion.43 = (f32[128]{0:T(128)S(1)}, f32[128]{0:T(128)S(1)}, f32[128]{0:T(128)S(1)}, f32[128]{0:T(128)S(1)}, f32[128]{0:T(128)S(1)}, /*index=5*/f32[128]{0:T(12...) fusion(f32[128,64,128]{2,0,1:T(8,128)S(1)} %get-tuple-element.8, ...), kind=kLoop, calls=%fused_computation.149 | loop fusion | flops 41941248 | bytes 31464448 | tf_op jit(solution)/shard_map/reduce_sum | solution.py:73
  126.1 4.3 convolution_bitcast_fusion
  130.4 6.2 %fusion.105 = f32[128]{0:T(128)S(1)} fusion(bf16[128,64,512]{2,0,1:T(8,128)(2,1)} %get-tuple-element.146, f32[128]{0:T(128)S(1)} %copy-done.13, bf16[128,64,128]{2,1,0:T(8,128)(2,1)S(1)} %copy-done.5, bf16[512,128]{1,0:T(8,128)(2,1)S(1)} %copy-done.12), kind=kOutput, calls=%fused_computation.211 | convolution fusion | flops 1077936000 | bytes 10617856 | tf_op jit(solution)/shard_map/rwe,ec->rwc/dot_general | solution.py:37
  136.9 67.9 %all-reduce = (f32[7,7,128]{2,1,0:T(8,128)S(1)}, f32[128]{0:T(128)S(1)}, f32[128]{0:T(128)S(1)}, f32[128]{0:T(128)S(1)}, f32[512]{0:T(512)S(1)}, /*index=5*/f32[128]{0:T(128)S(1)}, f32[128]{0:T(128)S(1)}) all-reduce(f32[7,7,128]{2,1,0:T(8,128)S(1)} %constant_dynamic-update-slice_fusion, ...), channel_id=1, replica_groups=mesh['gx'=16,'gy'=8] {'gx','gy'}, use_global_device_ids=true, to_apply=%region_53.54 | all-reduce | flops 7424 | bytes 59392 | tf_op jit(solution)/shard_map/psum | solution.py:143
  208.1 4.8 collective-permute-start.5
  213.4 1.8 collective-permute-done.4
  218.7 136.7 %all-reduce.4.cloned.1.call-done = (f32[128,512]{1,0:T(8,128)}, f32[512,128]{1,0:T(8,128)}) async-done(((f32[128,512]{1,0:T(8,128)}, f32[512,128]{1,0:T(8,128)}), (f32[128,512]{1,0:T(8,128)}, f32[512,128]{1,0:T(8,128)})) %all-reduce.4.cloned.1.call-update) | async-done | bytes 524304 | tf_op jit(solution)/shard_map/psum | solution.py:143
  358.7 5.5 %maximum_select_fusion = f32[134,70,128]{2,0,1:T(8,128)} fusion(f32[134,3,128]{2,0,1:T(8,128)S(1)} %collective-permute-done.7, f32[3,64,128]{2,0,1:T(4,128)S(1)} %collective-permute-done.5, f32[128,64,128]{2,0,1:T(8,128)} %copy-done.2, f32[3,64,128]{2,0,1:T(4,128)S(1)} %collective-permute-done.4, f32[134,3,128]{2,0,1:T(8,128)S(1)} %collective-permute-done.6, ...), kind=kLoop, calls=%fused_computation.111 | loop fusion | flops 6003200 | bytes 9605190 | tf_op jit(solution)/shard_map/jit(_where)/select_n | solution.py:84
  364.2 111.4 %fusion.104 = bf16[128,64,128]{2,0,1:T(8,128)(2,1)} fusion(f32[134,70,128]{2,0,1:T(8,128)} %maximum_select_fusion, f32[128]{0:T(128)S(1)} %get-tuple-element.141, f32[128]{0:T(128)S(1)} %get-tuple-element.142, f32[128]{0:T(128)S(1)} %get-tuple-element.95, f32[128]{0:T(128)S(1)} %get-tuple-element.96, f32[128]{0:T(128)S(1)} %get-tuple-element.97, ...), kind=kLoop, calls=%fused_computation.210 | loop fusion | flops 104857600 | bytes 209740288 | tf_op jit(solution)/shard_map/convert_element_type | solution.py:141
  475.6 4.3 copy.27
  (80 shorter events, 14.1 us)
Async XLA Ops:
  7.2 57.8 %copy-start = (bf16[128,512]{1,0:T(8,128)(2,1)S(1)}, bf16[128,512]{1,0:T(8,128)(2,1)}, u32[]{:S(2)}) copy-start(bf16[128,512]{1,0:T(8,128)(2,1)} %param.17) | copy-start | bytes 393220
  7.2 10.9 %copy-start.6 = (f32[7,7,128]{2,1,0:T(8,128)S(1)}, f32[7,7,128]{2,1,0:T(8,128)}, u32[]{:S(2)}) copy-start(f32[7,7,128]{2,1,0:T(8,128)} %param.13) | copy-start | bytes 75268
  7.2 11.0 %copy-start.10 = (f32[128]{0:T(128)S(1)}, f32[128]{0:T(128)}, u32[]{:S(2)}) copy-start(f32[128]{0:T(128)} %param.21) | copy-start | bytes 1540
  7.2 348.1 %all-reduce.4.cloned.1.call-start = ((), (), s32[]{:S(2)}) async-start(), calls=%async_computation | async-start | bytes 1048576 | tf_op jit(solution)/shard_map/psum | solution.py:143
  7.3 10.9 %copy-start.3 = (bf16[128,64,128]{2,1,0:T(8,128)(2,1)S(1)}, bf16[128,64,128]{2,1,0:T(8,128)(2,1)}, u32[]{:S(2)}) copy-start(bf16[128,64,128]{2,1,0:T(8,128)(2,1)} %param.12) | copy-start | bytes 6291460
  10.4 8.9 %collective-permute-start = (bf16[3,64,128]{2,0,1:T(4,128)(2,1)S(1)}, bf16[3,64,128]{2,0,1:T(4,128)(2,1)S(1)}, u32[]{:S(2)}, u32[]{:S(2)}) collective-permute-start(bf16[3,64,128]{2,0,1:T(4,128)(2,1)S(1)} %get-tuple-element.92), channel_id=1, source_target_pairs={{0,8},{8,16},{16,24},{24,32},{32,40},{40,48},{48,56},{56,64},{64,7... | collective-permute-start | bytes 147464 | tf_op jit(solution)/shard_map/ppermute | solution.py:18
  13.0 6.5 %collective-permute-start.1 = (bf16[3,64,128]{2,0,1:T(4,128)(2,1)S(1)}, bf16[3,64,128]{2,0,1:T(4,128)(2,1)S(1)}, u32[]{:S(2)}, u32[]{:S(2)}) collective-permute-start(bf16[3,64,128]{2,0,1:T(4,128)(2,1)S(1)} %get-tuple-element.93), channel_id=1, source_target_pairs={{8,0},{16,8},{24,16},{32,24},{40,32},{48,40},{56,48},{64,56},{72,6... | collective-permute-start | bytes 147464 | tf_op jit(solution)/shard_map/ppermute | solution.py:20
  19.3 9.9 %copy-start.11 = (f32[128]{0:T(128)S(1)}, f32[128]{0:T(128)}, u32[]{:S(2)}) copy-start(f32[128]{0:T(128)} %param.14) | copy-start | bytes 1540
  19.5 4.3 collective-permute-start.2
  22.2 4.1 collective-permute-start.3
  62.2 2.8 copy-start.7
  62.2 2.8 copy-start.8
  65.0 8.7 %copy-start.4 = (bf16[128,64,128]{2,1,0:T(8,128)(2,1)S(1)}, bf16[128,64,128]{2,1,0:T(8,128)(2,1)}, u32[]{:S(2)}) copy-start(bf16[128,64,128]{2,1,0:T(8,128)(2,1)} %param.12) | copy-start | bytes 6291460
  65.0 8.7 %copy-start.12 = (bf16[512,128]{1,0:T(8,128)(2,1)S(1)}, bf16[512,128]{1,0:T(8,128)(2,1)}, u32[]{:S(2)}) copy-start(bf16[512,128]{1,0:T(8,128)(2,1)} %param.19) | copy-start | bytes 393220
  93.2 32.8 %slice-start = ((s8[8388608]{0:T(1024)(128)(4,1)}), s8[4194304]{0:T(1024)(128)(4,1)S(1)}, s32[]{:S(2)}) async-start(s8[8388608]{0:T(1024)(128)(4,1)} %bitcast.185), calls=%async_computation.1 | async-start | bytes 8388608
  106.6 19.3 %copy-start.2 = (f32[128,64,128]{2,0,1:T(8,128)}, f32[128,64,128]{2,0,1:T(8,128)S(1)}, u32[]{:S(2)}) copy-start(f32[128,64,128]{2,0,1:T(8,128)S(1)} %get-tuple-element.83) | copy-start | bytes 12582916
  106.6 19.4 %slice-start.1 = ((s8[8388608]{0:T(1024)(128)(4,1)}), s8[4194304]{0:T(1024)(128)(4,1)S(1)}, s32[]{:S(2)}) async-start(s8[8388608]{0:T(1024)(128)(4,1)} %bitcast.185), calls=%async_computation.2 | async-start | bytes 8388608
  117.7 8.4 %copy-start.5 = (bf16[128,64,128]{2,1,0:T(8,128)(2,1)S(1)}, bf16[128,64,128]{2,1,0:T(8,128)(2,1)}, u32[]{:S(2)}) copy-start(bf16[128,64,128]{2,1,0:T(8,128)(2,1)} %param.12) | copy-start | bytes 6291460
  126.1 4.4 copy-start.13
  208.1 7.1 %collective-permute-start.4 = (f32[3,64,128]{2,0,1:T(4,128)S(1)}, f32[3,64,128]{2,0,1:T(4,128)S(1)}, u32[]{:S(2)}, u32[]{:S(2)}) collective-permute-start(f32[3,64,128]{2,0,1:T(4,128)S(1)} %get-tuple-element.88), channel_id=1, source_target_pairs={{0,8},{8,16},{16,24},{24,32},{32,40},{40,48},{48,56},{56,64},{64,7... | collective-permute-start | bytes 294920 | tf_op jit(solution)/shard_map/ppermute | solution.py:18
  208.1 7.1 %collective-permute-start.5 = (f32[3,64,128]{2,0,1:T(4,128)S(1)}, f32[3,64,128]{2,0,1:T(4,128)S(1)}, u32[]{:S(2)}, u32[]{:S(2)}) collective-permute-start(f32[3,64,128]{2,0,1:T(4,128)S(1)} %get-tuple-element.89), channel_id=1, source_target_pairs={{8,0},{16,8},{24,16},{32,24},{40,32},{48,40},{56,48},{64,56},{72,6... | collective-permute-start | bytes 294920 | tf_op jit(solution)/shard_map/ppermute | solution.py:20
  216.3 142.4 %collective-permute-start.6 = (f32[134,3,128]{2,0,1:T(8,128)S(1)}, f32[134,3,128]{2,0,1:T(8,128)S(1)}, u32[]{:S(2)}, u32[]{:S(2)}) collective-permute-start(f32[134,3,128]{2,0,1:T(8,128)S(1)} %get-tuple-element.86), channel_id=1, source_target_pairs={{0,1},{1,2},{2,3},{3,4},{4,5},{5,6},{6,7},{7,0},{8,9},{9,10},{10,1... | collective-permute-start | bytes 617480 | tf_op jit(solution)/shard_map/ppermute | solution.py:18
  217.8 140.9 %collective-permute-start.7 = (f32[134,3,128]{2,0,1:T(8,128)S(1)}, f32[134,3,128]{2,0,1:T(8,128)S(1)}, u32[]{:S(2)}, u32[]{:S(2)}) collective-permute-start(f32[134,3,128]{2,0,1:T(8,128)S(1)} %get-tuple-element.87), channel_id=1, source_target_pairs={{1,0},{2,1},{3,2},{4,3},{5,4},{6,5},{7,6},{0,7},{9,8},{10,9},{11,1... | collective-permute-start | bytes 617480 | tf_op jit(solution)/shard_map/ppermute | solution.py:20
  364.2 115.7 %copy-start.1 = (bf16[128,512]{1,0:T(8,128)(2,1)S(1)}, bf16[128,512]{1,0:T(8,128)(2,1)}, u32[]{:S(2)}) copy-start(bf16[128,512]{1,0:T(8,128)(2,1)} %param.17) | copy-start | bytes 393220
  (1 other events, 2.8 us)
Sparse Core Ops, SparseCore 0:
  213.0 142.2 all-reduce.3
where the time goes:
time: 490 us; the launch traced here: 487 us
  other arithmetic  198 us (40%)
  waiting for transfers between devices  143 us (29%)
  blocking collectives  67.9 us (14%)
  matrix products  38.7 us (8%)
  starting transfers between devices  17.5 us (4%)
  between operations  14.7 us (3%)
  local copies, waits for them, and re-layouts  7.79 us (2%)
    psum x1, waiting for transfers between devices, local(): lax.psum((d_kern, d_kbias, d_gain, d_shift, d_wup, d_bup, d_wdown, d_bdow...  137 us
    convert_element_type x1, other arithmetic, local(): d_features = (cotangent.astype(jnp.float32) + spread).astype(jnp.bfloat16)  111 us
    psum x1, blocking collectives, local(): lax.psum((d_kern, d_kbias, d_gain, d_shift, d_wup, d_bup, d_wdown, d_bdow...  67.9 us
    dot_general x6, matrix products, product(): return jnp.einsum(spec, left, right, preferred_element_type=jnp.float32)  38.7 us
    reduce_sum x1, other arithmetic, layer_back(): chan_mean = jnp.mean(conv_out, axis=-1, keepdims=True)  33 us
    reduce_sum x3, other arithmetic, kernel_grad(): line.append(jnp.sum(slopes_in * window, axis=(0, 1)))  32.7 us
    ppermute x4, starting transfers between devices, extended(): lax.ppermute(head, axis, [((i + 1) % count, i) for i in range(count)])  10.8 us
  transfers between devices with their start and end apart: 9, of which 5 were waited for; matrix products, arithmetic and copies ran while one was open for 1% of the time, Pallas kernels for 0%

commit v1 on v0

v1 whole, which is shorter than its diff:
```python
import functools
import math

import jax
import jax.numpy as jnp
from jax import lax
from jax.experimental import pallas as pl
from jax.experimental.pallas import tpu as pltpu
from jax.sharding import PartitionSpec as P

EPSILON = 1e-06
REACH = 3
TAPS = 7
PAIRS = 4
OFF = 8
GRANT = 58 * 2**20


def shifted(cells, axis, step, cyclic):
    count = lax.axis_size(axis)
    pairs = [(i, (i + step) % count) for i in range(count) if cyclic or 0 <= i + step < count]
    return lax.ppermute(cells, axis, pairs)


def halo(cells):
    rows, cols = cells.shape[0], cells.shape[1]
    top = shifted(cells[rows - REACH :], "gx", 1, True)
    bottom = shifted(cells[:REACH], "gx", -1, True)

    def edge(start):
        cut = [part[:, start : start + REACH] for part in (top, cells, bottom)]
        return jnp.concatenate(cut, axis=0)

    left = shifted(edge(cols - REACH), "gy", 1, False)
    right = shifted(edge(0), "gy", -1, False)
    return top, bottom, left, right


def fill_padded(own, top, bottom, left, right, pad_ref):
    rows, cols = own.shape[0], own.shape[1]
    inner = pl.ds(OFF, cols)
    pad_ref[0:REACH, inner, :] = top[...].astype(jnp.float32)
    pad_ref[REACH + rows : 2 * REACH + rows, inner, :] = bottom[...].astype(jnp.float32)

    def body(r, carry):
        pad_ref[REACH + r, inner, :] = own[r].astype(jnp.float32)
        return carry

    lax.fori_loop(0, rows, body, 0, unroll=4)

    def sides(r, carry):
        pad_ref[r, OFF - REACH : OFF, :] = left[r].astype(jnp.float32)
        pad_ref[r, OFF + cols : OFF + cols + REACH, :] = right[r].astype(jnp.float32)
        return carry

    lax.fori_loop(0, rows + 2 * REACH, sides, 0, unroll=2)


def fill_pairs(pad_ref, pair_ref):
    half = pair_ref.shape[1] // pad_ref.shape[0]

    def body(r, carry):
        for m in range(PAIRS):
            for p in range(2):
                start = OFF - REACH + 2 * m + p
                cells = pad_ref[r, pl.ds(start, half, stride=2), :]
                pair_ref[m, pl.ds(pl.multiple_of(r * half, half), half), p * 128 : p * 128 + 128] = (
                    cells.astype(jnp.bfloat16)
                )
        return carry

    lax.fori_loop(0, pad_ref.shape[0], body, 0, unroll=2)


def fill_weights(kern_ref, w_ref, flip):
    width = kern_ref.shape[2]
    row = lax.broadcasted_iota(jnp.int32, (width, width), 0)
    col = lax.broadcasted_iota(jnp.int32, (width, width), 1)
    eye = row == col
    for a in range(TAPS):
        for m in range(PAIRS):
            for p in range(2):
                for q in range(2):
                    b = 2 * m + p - q
                    base = ((a * PAIRS + m) * 2 + p) * width
                    if 0 <= b < TAPS:
                        tap = (
                            kern_ref[TAPS - 1 - a, pl.ds(TAPS - 1 - b, 1), :]
                            if flip
                            else kern_ref[a, pl.ds(b, 1), :]
                        )
                        block = jnp.where(eye, jnp.broadcast_to(tap, (width, width)), 0.0)
                    else:
                        block = jnp.zeros((width, width), jnp.float32)
                    w_ref[base : base + width, q * width : (q + 1) * width] = block.astype(
                        jnp.bfloat16
                    )


def conv_pairs(pair_ref, w_ref, row0, row_count, half):
    lhs = jnp.concatenate(
        [
            pair_ref[m, pl.ds(pl.multiple_of((row0 + a) * half, half), row_count * half), :]
            for a in range(TAPS)
            for m in range(PAIRS)
        ],
        axis=1,
    )
    return jnp.dot(lhs, w_ref[...], preferred_element_type=jnp.float32)


def dot(left, right, dims):
    return lax.dot_general(left, right, (dims, ((), ())), preferred_element_type=jnp.float32)


def fold(values):
    return jnp.sum(values.reshape(-1, 8, values.shape[-1]), axis=0)


def layer_kernel(
    block_rows,
    own,
    top,
    bottom,
    left,
    right,
    cot_ref,
    kern_ref,
    kbias_ref,
    gain_ref,
    shift_ref,
    wup_ref,
    bup_ref,
    wdown_ref,
    scale_ref,
    dconv_ref,
    dwup_ref,
    dgt_ref,
    sums_ref,
    dbup_ref,
    pad_ref,
    pair_ref,
    w_ref,
    cell_ref,
):
    step = pl.program_id(0)
    half = own.shape[1] // 2
    count = block_rows * half

    @pl.when(step == 0)
    def _():
        fill_weights(kern_ref, w_ref, False)
        fill_padded(own, top, bottom, left, right, pad_ref)
        fill_pairs(pad_ref, pair_ref)
        dwup_ref[...] = jnp.zeros_like(dwup_ref)
        dgt_ref[...] = jnp.zeros_like(dgt_ref)
        sums_ref[...] = jnp.zeros_like(sums_ref)
        dbup_ref[...] = jnp.zeros_like(dbup_ref)

    conv = conv_pairs(pair_ref, w_ref, step * block_rows, block_rows, half)
    conv = jnp.concatenate([conv[:, :128], conv[:, 128:]], axis=0) + kbias_ref[...]
    gain = gain_ref[...]
    centred = conv - jnp.mean(conv, axis=-1, keepdims=True)
    inv_std = lax.rsqrt(jnp.mean(centred * centred, axis=-1, keepdims=True) + EPSILON)
    normed = centred * inv_std
    normal = (normed * gain + shift_ref[...]).astype(jnp.bfloat16)
    hidden = dot(normal, wup_ref[...], ((1,), (0,))) + bup_ref[...]
    cdf = 0.5 * (1.0 + lax.erf(hidden * 0.7071067811865476))
    active = (hidden * cdf).astype(jnp.bfloat16)
    slope = cdf + hidden * jnp.exp(-0.5 * hidden * hidden) * 0.3989422804014327
    cell_ref[...] = cot_ref[...].astype(jnp.float32)
    cot = jnp.concatenate([cell_ref[pl.ds(q, count, stride=2), :] for q in range(2)], axis=0)
    d_output = (cot * scale_ref[...]).astype(jnp.bfloat16)
    d_hidden = (dot(d_output, wdown_ref[...], ((1,), (1,))) * slope).astype(jnp.bfloat16)
    d_normal = dot(d_hidden, wup_ref[...], ((1,), (1,)))
    d_normed = d_normal * gain
    first = jnp.mean(d_normed, axis=-1, keepdims=True)
    second = jnp.mean(d_normed * normed, axis=-1, keepdims=True)
    d_conv = inv_std * (d_normed - first - normed * second)
    sums_ref[0] += fold(d_conv)
    sums_ref[1] += fold(d_normal * normed)
    sums_ref[2] += fold(d_normal)
    sums_ref[3] += fold(cot)
    dbup_ref[...] += fold(d_hidden.astype(jnp.float32))
    dwup_ref[...] += dot(normal, d_hidden, ((0,), (0,)))
    dgt_ref[...] += dot(cot.astype(jnp.bfloat16), active, ((0,), (0,)))
    for q in range(2):
        cell_ref[pl.ds(q, count, stride=2), :] = d_conv[q * count : (q + 1) * count]
    dconv_ref[...] = cell_ref[...].astype(jnp.bfloat16)


def layer(x, sides, cotangent, kernel, kbias, gain, shift, wup, bup, wdown, scale):
    rows, cols, width = x.shape
    hidden = wup.shape[1]
    block_rows = 8
    block = block_rows * cols
    whole = lambda a: pl.BlockSpec(a.shape, lambda i: (0,) * a.ndim)
    row = lambda a: a.reshape(1, -1)
    consts = (kernel, row(kbias), row(gain), row(shift), wup, row(bup), wdown, row(scale))
    padded = rows + 2 * REACH
    cells = pl.BlockSpec((block, width), lambda i: (i, 0))
    full = lambda *shape: pl.BlockSpec(shape, lambda i: (0,) * len(shape))
    f32 = jnp.float32
    return pl.pallas_call(
        functools.partial(layer_kernel, block_rows),
        grid=(rows // block_rows,),
        in_specs=[whole(x)]
        + [whole(s) for s in sides]
        + [cells]
        + [whole(c) for c in consts],
        out_specs=[
            cells,
            full(width, hidden),
            full(width, hidden),
            full(4, 8, width),
            full(8, hidden),
        ],
        out_shape=[
            jax.ShapeDtypeStruct((rows * cols, width), jnp.bfloat16),
            jax.ShapeDtypeStruct((width, hidden), f32),
            jax.ShapeDtypeStruct((width, hidden), f32),
            jax.ShapeDtypeStruct((4, 8, width), f32),
            jax.ShapeDtypeStruct((8, hidden), f32),
        ],
        scratch_shapes=[
            pltpu.VMEM((padded, cols + 2 * OFF, width), f32),
            pltpu.VMEM((PAIRS, padded * cols // 2, 2 * width), jnp.bfloat16),
            pltpu.VMEM((TAPS * PAIRS * 2 * width, 2 * width), jnp.bfloat16),
            pltpu.VMEM((block, width), f32),
        ],
        compiler_params=pltpu.CompilerParams(vmem_limit_bytes=GRANT),
        name="layer",
    )(x, *sides, cotangent.reshape(rows * cols, width), *consts)


def tap_kernel(own, top, bottom, left, right, dconv_ref, out_ref, pad_ref, grad_ref):
    rows, cols = own.shape[0], own.shape[1]
    edge = TAPS - 1
    fill_padded(own, top, bottom, left, right, pad_ref)
    grad_ref[0:edge] = jnp.zeros((edge,) + grad_ref.shape[1:], jnp.float32)
    grad_ref[edge + rows :] = jnp.zeros((edge,) + grad_ref.shape[1:], jnp.float32)

    def copy(r, carry):
        grad_ref[edge + r] = dconv_ref[pl.ds(pl.multiple_of(r * cols, cols), cols), :].astype(
            jnp.float32
        )
        return carry

    lax.fori_loop(0, rows, copy, 0, unroll=4)
    for b in range(TAPS):

        def body(i, sums):
            r = 2 * i
            sums = list(sums)
            for s in range(cols // 8):
                grads = [grad_ref[r + k, 8 * s : 8 * s + 8, :] for k in range(TAPS + 1)]
                start = OFF - REACH + b + 8 * s
                cells = [pad_ref[r + u, start : start + 8, :] for u in range(2)]
                for a in range(TAPS):
                    sums[a] = sums[a] + (
                        cells[0] * grads[edge - a] + cells[1] * grads[TAPS - a]
                    )
            return tuple(sums)

        zero = jnp.zeros((8, own.shape[2]), jnp.float32)
        sums = lax.fori_loop(0, (rows + edge) // 2, body, (zero,) * TAPS)
        for a in range(TAPS):
            out_ref[a, b] = sums[a]


def tap_grads(x, sides, dconv):
    rows, cols, width = x.shape
    padded = rows + 2 * REACH
    return pl.pallas_call(
        tap_kernel,
        out_shape=jax.ShapeDtypeStruct((TAPS, TAPS, 8, width), jnp.float32),
        scratch_shapes=[
            pltpu.VMEM((padded, cols + 2 * OFF, width), jnp.float32),
            pltpu.VMEM((rows + 2 * TAPS - 2, cols, width), jnp.float32),
        ],
        compiler_params=pltpu.CompilerParams(vmem_limit_bytes=GRANT),
        cost_estimate=pl.CostEstimate(
            flops=2 * TAPS * TAPS * x.size, bytes_accessed=4 * x.size, transcendentals=0
        ),
        name="taps",
    )(x, *sides, dconv)


def spread_kernel(
    block_rows, own, top, bottom, left, right, cot_ref, kern_ref, out_ref, pad_ref, pair_ref, w_ref, cell_ref
):
    step = pl.program_id(0)
    half = own.shape[1] // 2
    count = block_rows * half

    @pl.when(step == 0)
    def _():
        fill_weights(kern_ref, w_ref, True)
        fill_padded(own, top, bottom, left, right, pad_ref)
        fill_pairs(pad_ref, pair_ref)

    conv = conv_pairs(pair_ref, w_ref, step * block_rows, block_rows, half)
    for q in range(2):
        cell_ref[pl.ds(q, count, stride=2), :] = conv[:, q * 128 : q * 128 + 128]
    out_ref[...] = (cell_ref[...] + cot_ref[...].astype(jnp.float32)).astype(jnp.bfloat16)


def spread(dconv, sides, cotangent, kernel):
    rows, cols, width = dconv.shape
    block_rows = 16
    block = block_rows * cols
    padded = rows + 2 * REACH
    whole = lambda a: pl.BlockSpec(a.shape, lambda i: (0,) * a.ndim)
    cells = pl.BlockSpec((block, width), lambda i: (i, 0))
    return pl.pallas_call(
        functools.partial(spread_kernel, block_rows),
        grid=(rows // block_rows,),
        in_specs=[whole(dconv)] + [whole(s) for s in sides] + [cells, whole(kernel)],
        out_specs=cells,
        out_shape=jax.ShapeDtypeStruct((rows * cols, width), jnp.bfloat16),
        scratch_shapes=[
            pltpu.VMEM((padded, cols + 2 * OFF, width), jnp.float32),
            pltpu.VMEM((PAIRS, padded * cols // 2, 2 * width), jnp.bfloat16),
            pltpu.VMEM((TAPS * PAIRS * 2 * width, 2 * width), jnp.bfloat16),
            pltpu.VMEM((block, width), jnp.float32),
        ],
        compiler_params=pltpu.CompilerParams(vmem_limit_bytes=GRANT),
        name="spread",
    )(dconv, *sides, cotangent.reshape(rows * cols, width), kernel).reshape(rows, cols, width)


def total(parts):
    axes = ("gx", "gy")
    share = lax.all_to_all(parts, axes, split_axis=0, concat_axis=0, tiled=True)
    share = jnp.sum(share.astype(jnp.float32), axis=0).astype(parts.dtype)
    copies = jnp.broadcast_to(share[None], parts.shape)
    return lax.all_to_all(copies, axes, split_axis=0, concat_axis=0, tiled=True)


def local(
    features, cotangent, kernel, kernel_bias, norm_gain, norm_shift, w_up, b_up, w_down, b_down, layer_scale
):
    rows, cols, width = features.shape
    hidden = w_up.shape[1]
    devices = lax.axis_size("gx") * lax.axis_size("gy")
    x_sides = halo(features)
    dconv, d_wup, d_gt, sums, d_bup = layer(
        features, x_sides, cotangent, kernel, kernel_bias, norm_gain, norm_shift, w_up, b_up, w_down, layer_scale
    )
    d_sides = halo(dconv.reshape(rows, cols, width))
    d_kern = tap_grads(features, x_sides, dconv)
    d_features = spread(dconv.reshape(rows, cols, width), d_sides, cotangent, kernel)

    lanes = hidden // width
    small = jnp.concatenate(
        [
            jnp.sum(d_kern, axis=2).reshape(TAPS * TAPS, width),
            jnp.sum(sums, axis=1),
            jnp.sum(d_bup, axis=0).reshape(lanes, width),
        ],
        axis=0,
    )
    small = jnp.pad(small, ((0, devices - small.shape[0]), (0, 0)))
    parts = jnp.concatenate(
        [d_wup.reshape(width, lanes, width), d_gt.reshape(width, lanes, width), small[:, None]], axis=1
    )
    parts = jnp.pad(parts, ((0, 0), (0, 16 - parts.shape[1]), (0, 0))).astype(jnp.bfloat16)
    summed = total(parts).astype(jnp.float32)
    factor = 1.0 / math.sqrt(rows * cols * devices)
    summed = summed * factor
    g_wup = summed[:, :lanes].reshape(width, hidden)
    g_gt = summed[:, lanes : 2 * lanes].reshape(width, hidden)
    small = summed[:, 2 * lanes]
    taps = TAPS * TAPS
    cot_sum = small[taps + 3]
    g_lscale = jnp.sum(w_down.astype(jnp.float32).T * g_gt, axis=1) + b_down * cot_sum
    return (
        d_features,
        small[:taps].reshape(TAPS, TAPS, width),
        small[taps],
        small[taps + 1],
        small[taps + 2],
        g_wup,
        small[taps + 4 : taps + 4 + lanes].reshape(hidden),
        (g_gt * layer_scale[:, None]).T,
        layer_scale * cot_sum,
        g_lscale,
    )


def solution(mesh):
    placed = (P("gx", "gy", None), P("gx", "gy", None), P(), P(), P(), P(), P(), P(), P(), P(), P())
    return jax.shard_map(
        local,
        mesh=mesh,
        in_specs=placed,
        out_specs=(P("gx", "gy", None), P(), P(), P(), P(), P(), P(), P(), P(), P()),
        check_vma=False,
    )
```

time: 490 us -> 169 us (0.34)
  other arithmetic: 198 us -> 4.07 us
  waiting for transfers between devices: 143 us -> 20.2 us
  Pallas kernels: 0 us -> 100 us
  blocking collectives: 67.9 us -> 0 us
  matrix products: 38.7 us -> 0 us
  starting transfers between devices: 17.5 us -> 33.6 us
  between operations: 14.7 us -> 0.95 us
    psum x1 -> x0, waiting for transfers between devices: 137 us -> none  [local(): lax.psum((d_kern, d_kbias, d_gain, d_shift, d_wup, d_bup, d_wdown, d_bdow...]
    convert_element_type x1 -> x0, other arithmetic: 111 us -> none  [local(): d_features = (cotangent.astype(jnp.float32) + spread).astype(jnp.bfloat16)]
    pallas_call x0 -> x3, Pallas kernels: none -> 100 us  [the longest x1 56.5 us: layer(): pl.pallas_call(functools.partial(layer_kernel, block_rows), grid=(rows //...]
    psum x1 -> x0, blocking collectives: 67.9 us -> none  [local(): lax.psum((d_kern, d_kbias, d_gain, d_shift, d_wup, d_bup, d_wdown, d_bdow...]
    reduce_sum x6 -> x5, other arithmetic: 69.5 us -> 1.9 us  [the longest x1 0.99 us: local(): jnp.sum(d_kern, axis=2).reshape(TAPS * TAPS, width)]
    dot_general x6 -> x0, matrix products: 38.7 us -> none  [product(): return jnp.einsum(spec, left, right, preferred_element_type=jnp.float32)]
    ppermute x8, waiting for transfers between devices: 6.05 us -> 16.4 us  [shifted(): return lax.ppermute(cells, axis, pairs)]
    select_n x2 -> x0, other arithmetic: 8.43 us -> none  [mask_edges(): jnp.where(keep_mask[None, :, None], padded, jnp.zeros((), padded.dtype))]
  transfers between devices with their start and end apart: 9 -> 10, of which waited for: 5 -> 6; matrix products, arithmetic and copies ran while one was open for 1% -> 3% of each run, Pallas kernels for 0% -> 13%
where the time goes in v1:
time: 169 us; the launch traced here: 168 us
  Pallas kernels  100 us (59%)
  starting transfers between devices  33.6 us (20%)
  waiting for transfers between devices  20.2 us (12%)
  local copies, waits for them, and re-layouts  9.04 us (5%)
  other arithmetic  4.07 us (2%)
    pallas_call x1, Pallas kernels, layer(): pl.pallas_call(functools.partial(layer_kernel, block_rows), grid=(rows //...  56.5 us
    ppermute x8, starting transfers between devices, shifted(): return lax.ppermute(cells, axis, pairs)  25.3 us
    pallas_call x1, Pallas kernels, spread(): pl.pallas_call(functools.partial(spread_kernel, block_rows), grid=(rows /...  22.7 us
    pallas_call x1, Pallas kernels, tap_grads(): pl.pallas_call(tap_kernel, out_shape=jax.ShapeDtypeStruct((TAPS, TAPS, 8,...  21.3 us
    ppermute x8, waiting for transfers between devices, shifted(): return lax.ppermute(cells, axis, pairs)  16.4 us
    all_to_all x1, starting transfers between devices, total(): return lax.all_to_all(copies, axes, split_axis=0, concat_axis=0, tiled=True)  4.6 us
    all_to_all x1, waiting for transfers between devices, total(): share = lax.all_to_all(parts, axes, split_axis=0, concat_axis=0, tiled=True)  3.77 us
    all_to_all x1, starting transfers between devices, total(): share = lax.all_to_all(parts, axes, split_axis=0, concat_axis=0, tiled=True)  3.7 us
  transfers between devices with their start and end apart: 10, of which 6 were waited for; matrix products, arithmetic and copies ran while one was open for 3% of the time, Pallas kernels for 13%

profile of v1, /device:TPU:1, one launch (start us, length us, event | category | flops | bytes accessed | tf_op | source)
XLA Modules:
  0.0 168.2 jit_solution(14001276516605543403)
XLA Ops:
  0.6 0.8 fusion.16
  1.5 7.1 %collective-permute-start.1 = (bf16[3,64,128]{2,1,0:T(8,128)(2,1)S(1)}, bf16[3,64,128]{2,1,0:T(8,128)(2,1)S(1)}, u32[]{:S(2)}, u32[]{:S(2)}) collective-permute-start(bf16[3,64,128]{2,1,0:T(8,128)(2,1)S(1)} %get-tuple-element.26), channel_id=1, source_target_pairs={{0,120},{8,0},{16,8},{24,16},{32,24},{40,32},{48,40},{56,48},{64,5... | collective-permute-start | bytes 147464 | tf_op jit(solution)/shard_map/ppermute | solution.py:22
  8.6 1.1 fusion.15
  9.7 5.1 %collective-permute-done.top = bf16[3,64,128]{2,1,0:T(8,128)(2,1)S(1)} collective-permute-done((bf16[3,64,128]{2,1,0:T(8,128)(2,1)S(1)}, bf16[3,64,128]{2,1,0:T(8,128)(2,1)S(1)}, u32[]{:S(2)}, u32[]{:S(2)}) %collective-permute-start) | collective-permute-done | bytes 49184 | tf_op jit(solution)/shard_map/ppermute | solution.py:22
  14.9 5.1 %collective-permute-start.2 = (bf16[134,3,128]{2,1,0:T(4,128)(2,1)S(1)}, bf16[134,3,128]{2,1,0:T(4,128)(2,1)S(1)}, u32[]{:S(2)}, u32[]{:S(2)}) collective-permute-start(bf16[134,3,128]{2,1,0:T(4,128)(2,1)S(1)} %pad_maximum_fusion), channel_id=1, source_target_pairs={{0,1},{1,2},{2,3},{3,4},{4,5},{5,6},{6,7},{8,9},{9,10},{10,11},{11... | collective-permute-start | bytes 308744 | tf_op jit(solution)/shard_map/ppermute | solution.py:22
  20.2 1.9 %collective-permute-start.3 = (bf16[134,3,128]{2,1,0:T(4,128)(2,1)S(1)}, bf16[134,3,128]{2,1,0:T(4,128)(2,1)S(1)}, u32[]{:S(2)}, u32[]{:S(2)}) collective-permute-start(bf16[134,3,128]{2,1,0:T(4,128)(2,1)S(1)} %pad_maximum_fusion.1), channel_id=1, source_target_pairs={{1,0},{2,1},{3,2},{4,3},{5,4},{6,5},{7,6},{9,8},{10,9},{11,10},{12... | collective-permute-start | bytes 308744 | tf_op jit(solution)/shard_map/ppermute | solution.py:22
  22.1 4.4 %collective-permute-done.3.right = bf16[134,3,128]{2,1,0:T(4,128)(2,1)S(1)} collective-permute-done((bf16[134,3,128]{2,1,0:T(4,128)(2,1)S(1)}, bf16[134,3,128]{2,1,0:T(4,128)(2,1)S(1)}, u32[]{:S(2)}, u32[]{:S(2)}) %collective-permute-start.3) | collective-permute-done | bytes 102944 | tf_op jit(solution)/shard_map/ppermute | solution.py:22
  27.2 56.5 %layer.1 = (bf16[8192,128]{1,0:T(8,128)(2,1)}, f32[128,512]{1,0:T(8,128)}, f32[128,512]{1,0:T(8,128)}, f32[4,8,128]{2,1,0:T(8,128)}, f32[8,512]{1,0:T(8,128)}) custom-call(bf16[128,64,128]{2,1,0:T(8,128)(2,1)} %own.3, bf16[3,64,128]{2,1,0:T(8,128)(2,1)} %copy-done.6, bf16[3,64,128]{2,1,0:T(8,128)(2,1)} %copy-done.5, bf16[134,3,128]{2,1,0:T(4,128)(2,1)} %copy-done, ...), custom_call_target="tpu_custom_call" | custom-call | tf_op jit(solution)/shard_map/layer/pallas_call | solution.py:204
  83.7 21.3 %taps.1 = f32[7,7,8,128]{3,2,1,0:T(8,128)} custom-call(bf16[128,64,128]{2,1,0:T(8,128)(2,1)} %own.3, bf16[3,64,128]{2,1,0:T(8,128)(2,1)} %copy-done.6, bf16[3,64,128]{2,1,0:T(8,128)(2,1)} %copy-done.5, bf16[134,3,128]{2,1,0:T(4,128)(2,1)} %copy-done, bf16[134,3,128]{2,1,0:T(4,128)(2,1)} %copy-done.1, bf16[8192,128]{1,0:T(8,128)(2,1)} %get-tuple-element.15.dconv_ref), custom_call_target="tpu_custom_call" | custom-call | flops 102760448 | bytes 4194304 | tf_op jit(solution)/shard_map/taps/pallas_call | solution.py:274
  105.0 1.0 reduce_sum.48
  106.3 1.1 fusion.4
  107.4 3.7 %all-to-all-start = ((bf16[128,16,128]{2,1,0:T(8,128)(2,1)}), bf16[128,16,128]{2,1,0:T(8,128)(2,1)S(1)}, u32[]{:S(2)}, u32[]{:S(2)}) async-start(bf16[128,16,128]{2,1,0:T(8,128)(2,1)} %fusion.4), calls=%async_computation | async-start | bytes 1048576 | tf_op jit(solution)/shard_map/all_to_all | solution.py:334
  112.0 1.5 collective-permute-start.4
  113.5 4.1 %collective-permute-start.5 = (bf16[3,64,128]{2,1,0:T(8,128)(2,1)S(1)}, bf16[3,64,128]{2,1,0:T(8,128)(2,1)S(1)}, u32[]{:S(2)}, u32[]{:S(2)}) collective-permute-start(bf16[3,64,128]{2,1,0:T(8,128)(2,1)S(1)} %bitcast.48), channel_id=1, source_target_pairs={{0,120},{8,0},{16,8},{24,16},{32,24},{40,32},{48,40},{56,48},{64,5... | collective-permute-start | bytes 147464 | tf_op jit(solution)/shard_map/ppermute | solution.py:22
  117.7 1.1 fusion.13
  118.8 2.2 %collective-permute-done.4.top = bf16[3,64,128]{2,1,0:T(8,128)(2,1)S(1)} collective-permute-done((bf16[3,64,128]{2,1,0:T(8,128)(2,1)S(1)}, bf16[3,64,128]{2,1,0:T(8,128)(2,1)S(1)}, u32[]{:S(2)}, u32[]{:S(2)}) %collective-permute-start.4) | collective-permute-done | bytes 49184 | tf_op jit(solution)/shard_map/ppermute | solution.py:22
  121.0 3.8 %all-to-all-done = bf16[128,16,128]{2,1,0:T(8,128)(2,1)S(1)} async-done(((bf16[128,16,128]{2,1,0:T(8,128)(2,1)}), bf16[128,16,128]{2,1,0:T(8,128)(2,1)S(1)}, u32[]{:S(2)}, u32[]{:S(2)}) %all-to-all-start) | async-done | bytes 524320 | tf_op jit(solution)/shard_map/all_to_all | solution.py:334
  124.9 0.9 broadcast_in_dim.12
  125.8 4.6 %all-to-all-start.1 = ((bf16[128,16,128]{2,1,0:T(8,128)(2,1)}), bf16[128,16,128]{2,1,0:T(8,128)(2,1)S(1)}, u32[]{:S(2)}, u32[]{:S(2)}) async-start(bf16[128,16,128]{2,1,0:T(8,128)(2,1)} %broadcast_in_dim.12), calls=%async_computation.1 | async-start | bytes 1048576 | tf_op jit(solution)/shard_map/all_to_all | solution.py:337
  130.5 3.5 %collective-permute-start.6 = (bf16[134,3,128]{2,1,0:T(4,128)(2,1)S(1)}, bf16[134,3,128]{2,1,0:T(4,128)(2,1)S(1)}, u32[]{:S(2)}, u32[]{:S(2)}) collective-permute-start(bf16[134,3,128]{2,1,0:T(4,128)(2,1)S(1)} %pad_maximum_fusion.2), channel_id=1, source_target_pairs={{0,1},{1,2},{2,3},{3,4},{4,5},{5,6},{6,7},{8,9},{9,10},{10,11},{11... | collective-permute-start | bytes 308744 | tf_op jit(solution)/shard_map/ppermute | solution.py:22
  134.2 1.9 %collective-permute-start.7 = (bf16[134,3,128]{2,1,0:T(4,128)(2,1)S(1)}, bf16[134,3,128]{2,1,0:T(4,128)(2,1)S(1)}, u32[]{:S(2)}, u32[]{:S(2)}) collective-permute-start(bf16[134,3,128]{2,1,0:T(4,128)(2,1)S(1)} %pad_maximum_fusion.3), channel_id=1, source_target_pairs={{1,0},{2,1},{3,2},{4,3},{5,4},{6,5},{7,6},{9,8},{10,9},{11,10},{12... | collective-permute-start | bytes 308744 | tf_op jit(solution)/shard_map/ppermute | solution.py:22
  136.1 1.2 collective-permute-done.6.left
  137.3 3.5 %collective-permute-done.7.right = bf16[134,3,128]{2,1,0:T(4,128)(2,1)S(1)} collective-permute-done((bf16[134,3,128]{2,1,0:T(4,128)(2,1)S(1)}, bf16[134,3,128]{2,1,0:T(4,128)(2,1)S(1)}, u32[]{:S(2)}, u32[]{:S(2)}) %collective-permute-start.7) | collective-permute-done | bytes 102944 | tf_op jit(solution)/shard_map/ppermute | solution.py:22
  141.5 22.7 %spread.1 = bf16[8192,128]{1,0:T(8,128)(2,1)} custom-call(bf16[128,64,128]{2,1,0:T(8,128)(2,1)} %bitcast.41, bf16[3,64,128]{2,1,0:T(8,128)(2,1)} %copy-done.9, bf16[3,64,128]{2,1,0:T(8,128)(2,1)} %copy-done.10, bf16[134,3,128]{2,1,0:T(4,128)(2,1)} %copy-done.7, bf16[134,3,128]{2,1,0:T(4,128)(2,1)} %copy-done.8, bf16[8192,128]{1,0:T(8,128)(2,1)} %bitcast.43, ...), custom_call_target="tpu_custom_call" | custom-call | tf_op jit(solution)/shard_map/spread/pallas_call | solution.py:315
  (64 shorter events, 7.1 us)
Async XLA Ops:
  1.5 8.3 %collective-permute-start.1 = (bf16[3,64,128]{2,1,0:T(8,128)(2,1)S(1)}, bf16[3,64,128]{2,1,0:T(8,128)(2,1)S(1)}, u32[]{:S(2)}, u32[]{:S(2)}) collective-permute-start(bf16[3,64,128]{2,1,0:T(8,128)(2,1)S(1)} %get-tuple-element.26), channel_id=1, source_target_pairs={{0,120},{8,0},{16,8},{24,16},{32,24},{40,32},{48,40},{56,48},{64,5... | collective-permute-start | bytes 147464 | tf_op jit(solution)/shard_map/ppermute | solution.py:22
  8.6 6.3 %collective-permute-start = (bf16[3,64,128]{2,1,0:T(8,128)(2,1)S(1)}, bf16[3,64,128]{2,1,0:T(8,128)(2,1)S(1)}, u32[]{:S(2)}, u32[]{:S(2)}) collective-permute-start(bf16[3,64,128]{2,1,0:T(8,128)(2,1)S(1)} %get-tuple-element.27), channel_id=1, source_target_pairs={{0,8},{8,16},{16,24},{24,32},{32,40},{40,48},{48,56},{56,64},{64,7... | collective-permute-start | bytes 147464 | tf_op jit(solution)/shard_map/ppermute | solution.py:22
  9.7 16.8 %copy-start.5 = (bf16[3,64,128]{2,1,0:T(8,128)(2,1)}, bf16[3,64,128]{2,1,0:T(8,128)(2,1)S(1)}, u32[]{:S(2)}) copy-start(bf16[3,64,128]{2,1,0:T(8,128)(2,1)S(1)} %collective-permute-done.1.bottom) | copy-start | bytes 147460
  14.8 11.7 %copy-start.6 = (bf16[3,64,128]{2,1,0:T(8,128)(2,1)}, bf16[3,64,128]{2,1,0:T(8,128)(2,1)S(1)}, u32[]{:S(2)}) copy-start(bf16[3,64,128]{2,1,0:T(8,128)(2,1)S(1)} %collective-permute-done.top) | copy-start | bytes 147460
  14.9 7.2 %collective-permute-start.2 = (bf16[134,3,128]{2,1,0:T(4,128)(2,1)S(1)}, bf16[134,3,128]{2,1,0:T(4,128)(2,1)S(1)}, u32[]{:S(2)}, u32[]{:S(2)}) collective-permute-start(bf16[134,3,128]{2,1,0:T(4,128)(2,1)S(1)} %pad_maximum_fusion), channel_id=1, source_target_pairs={{0,1},{1,2},{2,3},{3,4},{4,5},{5,6},{6,7},{8,9},{9,10},{10,11},{11... | collective-permute-start | bytes 308744 | tf_op jit(solution)/shard_map/ppermute | solution.py:22
  20.2 6.4 %collective-permute-start.3 = (bf16[134,3,128]{2,1,0:T(4,128)(2,1)S(1)}, bf16[134,3,128]{2,1,0:T(4,128)(2,1)S(1)}, u32[]{:S(2)}, u32[]{:S(2)}) collective-permute-start(bf16[134,3,128]{2,1,0:T(4,128)(2,1)S(1)} %pad_maximum_fusion.1), channel_id=1, source_target_pairs={{1,0},{2,1},{3,2},{4,3},{5,4},{6,5},{7,6},{9,8},{10,9},{11,10},{12... | collective-permute-start | bytes 308744 | tf_op jit(solution)/shard_map/ppermute | solution.py:22
  22.1 4.4 %copy-start = (bf16[134,3,128]{2,1,0:T(4,128)(2,1)}, bf16[134,3,128]{2,1,0:T(4,128)(2,1)S(1)}, u32[]{:S(2)}) copy-start(bf16[134,3,128]{2,1,0:T(4,128)(2,1)S(1)} %collective-permute-done.2.left) | copy-start | bytes 308740
  83.7 22.3 %copy-start.4 = (f32[128,512]{1,0:T(8,128)S(1)}, f32[128,512]{1,0:T(8,128)}, u32[]{:S(2)}) copy-start(f32[128,512]{1,0:T(8,128)} %get-tuple-element.16) | copy-start | bytes 786436
  83.7 22.4 %copy-start.12 = (f32[4,8,128]{2,1,0:T(8,128)S(1)}, f32[4,8,128]{2,1,0:T(8,128)}, u32[]{:S(2)}) copy-start(f32[4,8,128]{2,1,0:T(8,128)} %get-tuple-element.18) | copy-start | bytes 49156
  83.7 22.4 %copy-start.11 = (f32[8,512]{1,0:T(8,128)S(1)}, f32[8,512]{1,0:T(8,128)}, u32[]{:S(2)}) copy-start(f32[8,512]{1,0:T(8,128)} %get-tuple-element.19) | copy-start | bytes 49156
  83.7 22.5 %copy-start.3 = (f32[128,512]{1,0:T(8,128)S(1)}, f32[128,512]{1,0:T(8,128)}, u32[]{:S(2)}) copy-start(f32[128,512]{1,0:T(8,128)} %get-tuple-element.17) | copy-start | bytes 786436
  107.4 17.3 %all-to-all-start = ((bf16[128,16,128]{2,1,0:T(8,128)(2,1)}), bf16[128,16,128]{2,1,0:T(8,128)(2,1)S(1)}, u32[]{:S(2)}, u32[]{:S(2)}) async-start(bf16[128,16,128]{2,1,0:T(8,128)(2,1)} %fusion.4), calls=%async_computation | async-start | bytes 1048576 | tf_op jit(solution)/shard_map/all_to_all | solution.py:334
  112.0 9.0 %collective-permute-start.4 = (bf16[3,64,128]{2,1,0:T(8,128)(2,1)S(1)}, bf16[3,64,128]{2,1,0:T(8,128)(2,1)S(1)}, u32[]{:S(2)}, u32[]{:S(2)}) collective-permute-start(bf16[3,64,128]{2,1,0:T(8,128)(2,1)S(1)} %bitcast.49), channel_id=1, source_target_pairs={{0,8},{8,16},{16,24},{24,32},{32,40},{40,48},{48,56},{56,64},{64,7... | collective-permute-start | bytes 147464 | tf_op jit(solution)/shard_map/ppermute | solution.py:22
  113.5 16.8 %collective-permute-start.5 = (bf16[3,64,128]{2,1,0:T(8,128)(2,1)S(1)}, bf16[3,64,128]{2,1,0:T(8,128)(2,1)S(1)}, u32[]{:S(2)}, u32[]{:S(2)}) collective-permute-start(bf16[3,64,128]{2,1,0:T(8,128)(2,1)S(1)} %bitcast.48), channel_id=1, source_target_pairs={{0,120},{8,0},{16,8},{24,16},{32,24},{40,32},{48,40},{56,48},{64,5... | collective-permute-start | bytes 147464 | tf_op jit(solution)/shard_map/ppermute | solution.py:22
  121.0 19.9 %copy-start.9 = (bf16[3,64,128]{2,1,0:T(8,128)(2,1)}, bf16[3,64,128]{2,1,0:T(8,128)(2,1)S(1)}, u32[]{:S(2)}) copy-start(bf16[3,64,128]{2,1,0:T(8,128)(2,1)S(1)} %collective-permute-done.4.top) | copy-start | bytes 147460
  125.8 38.4 %all-to-all-start.1 = ((bf16[128,16,128]{2,1,0:T(8,128)(2,1)}), bf16[128,16,128]{2,1,0:T(8,128)(2,1)S(1)}, u32[]{:S(2)}, u32[]{:S(2)}) async-start(bf16[128,16,128]{2,1,0:T(8,128)(2,1)} %broadcast_in_dim.12), calls=%async_computation.1 | async-start | bytes 1048576 | tf_op jit(solution)/shard_map/all_to_all | solution.py:337
  130.4 10.4 %copy-start.10 = (bf16[3,64,128]{2,1,0:T(8,128)(2,1)}, bf16[3,64,128]{2,1,0:T(8,128)(2,1)S(1)}, u32[]{:S(2)}) copy-start(bf16[3,64,128]{2,1,0:T(8,128)(2,1)S(1)} %collective-permute-done.5.bottom) | copy-start | bytes 147460
  130.5 6.8 %collective-permute-start.6 = (bf16[134,3,128]{2,1,0:T(4,128)(2,1)S(1)}, bf16[134,3,128]{2,1,0:T(4,128)(2,1)S(1)}, u32[]{:S(2)}, u32[]{:S(2)}) collective-permute-start(bf16[134,3,128]{2,1,0:T(4,128)(2,1)S(1)} %pad_maximum_fusion.2), channel_id=1, source_target_pairs={{0,1},{1,2},{2,3},{3,4},{4,5},{5,6},{6,7},{8,9},{9,10},{10,11},{11... | collective-permute-start | bytes 308744 | tf_op jit(solution)/shard_map/ppermute | solution.py:22
  134.2 6.6 %collective-permute-start.7 = (bf16[134,3,128]{2,1,0:T(4,128)(2,1)S(1)}, bf16[134,3,128]{2,1,0:T(4,128)(2,1)S(1)}, u32[]{:S(2)}, u32[]{:S(2)}) collective-permute-start(bf16[134,3,128]{2,1,0:T(4,128)(2,1)S(1)} %pad_maximum_fusion.3), channel_id=1, source_target_pairs={{1,0},{2,1},{3,2},{4,3},{5,4},{6,5},{7,6},{9,8},{10,9},{11,10},{12... | collective-permute-start | bytes 308744 | tf_op jit(solution)/shard_map/ppermute | solution.py:22
  137.3 3.5 %copy-start.7 = (bf16[134,3,128]{2,1,0:T(4,128)(2,1)}, bf16[134,3,128]{2,1,0:T(4,128)(2,1)S(1)}, u32[]{:S(2)}) copy-start(bf16[134,3,128]{2,1,0:T(4,128)(2,1)S(1)} %collective-permute-done.6.left) | copy-start | bytes 308740
  140.8 0.7 copy-start.8
  164.2 2.8 %copy-start.2 = (bf16[512,128]{1,0:T(8,128)(2,1)S(1)}, bf16[512,128]{1,0:T(8,128)(2,1)}, u32[]{:S(2)}) copy-start(bf16[512,128]{1,0:T(8,128)(2,1)} %wdown_ref.1) | copy-start | bytes 393220
  164.2 2.8 %copy-start.13 = (f32[128]{0:T(128)S(1)}, f32[128]{0:T(128)}, u32[]{:S(2)}) copy-start(f32[128]{0:T(128)} %param.21) | copy-start | bytes 1540
  164.2 3.6 %copy-start.14 = (f32[128]{0:T(128)S(1)}, f32[128]{0:T(128)}, u32[]{:S(2)}) copy-start(f32[128]{0:T(128)} %param.20) | copy-start | bytes 1540
  (1 other events, 0.6 us)

commit v2 on v1

--- a/solution.py
+++ b/solution.py
@@ -14,6 +14,8 @@
 PAIRS = 4
 OFF = 8
 GRANT = 58 * 2**20
+LANES = 4
+SHARE = 16
 
 
 def shifted(cells, axis, step, cyclic):
@@ -117,6 +119,22 @@
     return jnp.sum(values.reshape(-1, 8, values.shape[-1]), axis=0)
 
 
+def tap_sums(pad_ref, cell_ref, row0, row_count, cols):
+    sums = {}
+    for b in range(TAPS):
+        for a in range(TAPS):
+            sums[a, b] = jnp.zeros((8, 128), jnp.float32)
+        for s in range(0, cols, 8):
+            grads = [cell_ref[r * cols + s : r * cols + s + 8, :] for r in range(row_count)]
+            for reached in range(row_count + TAPS - 1):
+                start = OFF - REACH + b + s
+                cells = pad_ref[row0 + reached, start : start + 8, :]
+                for a in range(TAPS):
+                    if 0 <= reached - a < row_count:
+                        sums[a, b] = sums[a, b] + cells * grads[reached - a]
+    return sums
+
+
 def layer_kernel(
     block_rows,
     own,
@@ -134,17 +152,22 @@
     wdown_ref,
     scale_ref,
     dconv_ref,
+    parts_ref,
     dwup_ref,
     dgt_ref,
     sums_ref,
     dbup_ref,
+    dkern_ref,
+    stage_ref,
     pad_ref,
     pair_ref,
     w_ref,
     cell_ref,
+    conv_ref,
 ):
     step = pl.program_id(0)
-    half = own.shape[1] // 2
+    cols = own.shape[1]
+    half = cols // 2
     count = block_rows * half
 
     @pl.when(step == 0)
@@ -156,8 +179,10 @@
         dgt_ref[...] = jnp.zeros_like(dgt_ref)
         sums_ref[...] = jnp.zeros_like(sums_ref)
         dbup_ref[...] = jnp.zeros_like(dbup_ref)
-
-    conv = conv_pairs(pair_ref, w_ref, step * block_rows, block_rows, half)
+        dkern_ref[...] = jnp.zeros_like(dkern_ref)
+        conv_ref[...] = conv_pairs(pair_ref, w_ref, 0, block_rows, half)
+
+    conv = conv_ref[...]
     conv = jnp.concatenate([conv[:, :128], conv[:, 128:]], axis=0) + kbias_ref[...]
     gain = gain_ref[...]
     centred = conv - jnp.mean(conv, axis=-1, keepdims=True)
@@ -187,12 +212,33 @@
     for q in range(2):
         cell_ref[pl.ds(q, count, stride=2), :] = d_conv[q * count : (q + 1) * count]
     dconv_ref[...] = cell_ref[...].astype(jnp.bfloat16)
+    following = jnp.minimum(step + 1, pl.num_programs(0) - 1)
+    conv = conv_pairs(pair_ref, w_ref, following * block_rows, block_rows, half)
+    taps = tap_sums(pad_ref, cell_ref, step * block_rows, block_rows, cols)
+    conv_ref[...] = conv
+    for (a, b), value in taps.items():
+        dkern_ref[a, b] += value
+
+    @pl.when(step == pl.num_programs(0) - 1)
+    def _():
+        stage_ref[...] = jnp.zeros_like(stage_ref)
+        for k in range(LANES):
+            lanes = slice(k * 128, k * 128 + 128)
+            stage_ref[pl.ds(k, 128, stride=SHARE), :] = dwup_ref[:, lanes]
+            stage_ref[pl.ds(LANES + k, 128, stride=SHARE), :] = dgt_ref[:, lanes]
+        small = [dkern_ref[a, b] for a in range(TAPS) for b in range(TAPS)]
+        small += [sums_ref[k] for k in range(4)]
+        small += [dbup_ref[:, k * 128 : k * 128 + 128] for k in range(LANES)]
+        for i, value in enumerate(small):
+            at = i * SHARE + 2 * LANES
+            stage_ref[at : at + 1, :] = jnp.sum(value, axis=0, keepdims=True)
+        parts_ref[...] = stage_ref[...].astype(jnp.bfloat16)
 
 
 def layer(x, sides, cotangent, kernel, kbias, gain, shift, wup, bup, wdown, scale):
     rows, cols, width = x.shape
     hidden = wup.shape[1]
-    block_rows = 8
+    block_rows = 16
     block = block_rows * cols
     whole = lambda a: pl.BlockSpec(a.shape, lambda i: (0,) * a.ndim)
     row = lambda a: a.reshape(1, -1)
@@ -208,82 +254,27 @@
         + [whole(s) for s in sides]
         + [cells]
         + [whole(c) for c in consts],
-        out_specs=[
-            cells,
-            full(width, hidden),
-            full(width, hidden),
-            full(4, 8, width),
-            full(8, hidden),
-        ],
+        out_specs=[cells, full(width * SHARE, width)],
         out_shape=[
             jax.ShapeDtypeStruct((rows * cols, width), jnp.bfloat16),
-            jax.ShapeDtypeStruct((width, hidden), f32),
-            jax.ShapeDtypeStruct((width, hidden), f32),
-            jax.ShapeDtypeStruct((4, 8, width), f32),
-            jax.ShapeDtypeStruct((8, hidden), f32),
+            jax.ShapeDtypeStruct((width * SHARE, width), jnp.bfloat16),
         ],
         scratch_shapes=[
+            pltpu.VMEM((width, hidden), f32),
+            pltpu.VMEM((width, hidden), f32),
+            pltpu.VMEM((4, 8, width), f32),
+            pltpu.VMEM((8, hidden), f32),
+            pltpu.VMEM((TAPS, TAPS, 8, width), f32),
+            pltpu.VMEM((width * SHARE, width), f32),
             pltpu.VMEM((padded, cols + 2 * OFF, width), f32),
             pltpu.VMEM((PAIRS, padded * cols // 2, 2 * width), jnp.bfloat16),
             pltpu.VMEM((TAPS * PAIRS * 2 * width, 2 * width), jnp.bfloat16),
             pltpu.VMEM((block, width), f32),
+            pltpu.VMEM((block // 2, 2 * width), f32),
         ],
         compiler_params=pltpu.CompilerParams(vmem_limit_bytes=GRANT),
         name="layer",
     )(x, *sides, cotangent.reshape(rows * cols, width), *consts)
-
-
-def tap_kernel(own, top, bottom, left, right, dconv_ref, out_ref, pad_ref, grad_ref):
-    rows, cols = own.shape[0], own.shape[1]
-    edge = TAPS - 1
-    fill_padded(own, top, bottom, left, right, pad_ref)
-    grad_ref[0:edge] = jnp.zeros((edge,) + grad_ref.shape[1:], jnp.float32)
-    grad_ref[edge + rows :] = jnp.zeros((edge,) + grad_ref.shape[1:], jnp.float32)
-
-    def copy(r, carry):
-        grad_ref[edge + r] = dconv_ref[pl.ds(pl.multiple_of(r * cols, cols), cols), :].astype(
-            jnp.float32
-        )
-        return carry
-
-    lax.fori_loop(0, rows, copy, 0, unroll=4)
-    for b in range(TAPS):
-
-        def body(i, sums):
-            r = 2 * i
-            sums = list(sums)
-            for s in range(cols // 8):
-                grads = [grad_ref[r + k, 8 * s : 8 * s + 8, :] for k in range(TAPS + 1)]
-                start = OFF - REACH + b + 8 * s
-                cells = [pad_ref[r + u, start : start + 8, :] for u in range(2)]
-                for a in range(TAPS):
-                    sums[a] = sums[a] + (
-                        cells[0] * grads[edge - a] + cells[1] * grads[TAPS - a]
-                    )
-            return tuple(sums)
-
-        zero = jnp.zeros((8, own.shape[2]), jnp.float32)
-        sums = lax.fori_loop(0, (rows + edge) // 2, body, (zero,) * TAPS)
-        for a in range(TAPS):
-            out_ref[a, b] = sums[a]
-
-
-def tap_grads(x, sides, dconv):
-    rows, cols, width = x.shape
-    padded = rows + 2 * REACH
-    return pl.pallas_call(
-        tap_kernel,
-        out_shape=jax.ShapeDtypeStruct((TAPS, TAPS, 8, width), jnp.float32),
-        scratch_shapes=[
-            pltpu.VMEM((padded, cols + 2 * OFF, width), jnp.float32),
-            pltpu.VMEM((rows + 2 * TAPS - 2, cols, width), jnp.float32),
-        ],
-        compiler_params=pltpu.CompilerParams(vmem_limit_bytes=GRANT),
-        cost_estimate=pl.CostEstimate(
-            flops=2 * TAPS * TAPS * x.size, bytes_accessed=4 * x.size, transcendentals=0
-        ),
-        name="taps",
-    )(x, *sides, dconv)
 
 
 def spread_kernel(
@@ -337,55 +328,88 @@
     return lax.all_to_all(copies, axes, split_axis=0, concat_axis=0, tiled=True)
 
 
+def finish_kernel(
+    factor,
+    summed_ref,
+    wdown_ref,
+    bdown_ref,
+    scale_ref,
+    dkern_ref,
+    dkbias_ref,
+    dgain_ref,
+    dshift_ref,
+    dwup_ref,
+    dbup_ref,
+    dwdown_ref,
+    dbdown_ref,
+    dscale_ref,
+    stage_ref,
+):
+    stage_ref[...] = summed_ref[...].astype(jnp.float32) * factor
+    scale = scale_ref[...]
+
+    def small(i):
+        at = i * SHARE + 2 * LANES
+        return stage_ref[at : at + 1, :]
+
+    for a in range(TAPS):
+        for b in range(TAPS):
+            dkern_ref[a, b : b + 1, :] = small(a * TAPS + b)
+    first = TAPS * TAPS
+    dkbias_ref[...] = small(first)
+    dgain_ref[...] = small(first + 1)
+    dshift_ref[...] = small(first + 2)
+    cot_sum = small(first + 3)
+    dscale = bdown_ref[...] * cot_sum
+    for k in range(LANES):
+        lanes = slice(k * 128, k * 128 + 128)
+        dbup_ref[:, lanes] = small(first + 4 + k)
+        dwup_ref[:, lanes] = stage_ref[pl.ds(k, 128, stride=SHARE), :]
+        product = stage_ref[pl.ds(LANES + k, 128, stride=SHARE), :].T
+        dwdown_ref[lanes, :] = product * scale
+        weights = wdown_ref[lanes, :].astype(jnp.float32)
+        dscale = dscale + jnp.sum(product * weights, axis=0, keepdims=True)
+    dbdown_ref[...] = cot_sum * scale
+    dscale_ref[...] = dscale
+
+
+def finish(summed, w_down, b_down, layer_scale, factor):
+    hidden, width = w_down.shape
+    shapes = [(TAPS, TAPS, width)] + [(1, width)] * 3 + [(width, hidden), (1, hidden), (hidden, width)]
+    shapes += [(1, width)] * 2
+    row = lambda a: a.reshape(1, -1)
+    return pl.pallas_call(
+        functools.partial(finish_kernel, factor),
+        out_shape=[jax.ShapeDtypeStruct(shape, jnp.float32) for shape in shapes],
+        scratch_shapes=[pltpu.VMEM(summed.shape, jnp.float32)],
+        name="finish",
+    )(summed, w_down, row(b_down), row(layer_scale))
+
+
 def local(
     features, cotangent, kernel, kernel_bias, norm_gain, norm_shift, w_up, b_up, w_down, b_down, layer_scale
 ):
     rows, cols, width = features.shape
-    hidden = w_up.shape[1]
     devices = lax.axis_size("gx") * lax.axis_size("gy")
-    x_sides = halo(features)
-    dconv, d_wup, d_gt, sums, d_bup = layer(
-        features, x_sides, cotangent, kernel, kernel_bias, norm_gain, norm_shift, w_up, b_up, w_down, layer_scale
+    dconv, parts = layer(
+        features,
+        halo(features),
+        cotangent,
+        kernel,
+        kernel_bias,
+        norm_gain,
+        norm_shift,
+        w_up,
+        b_up,
+        w_down,
+        layer_scale,
     )
-    d_sides = halo(dconv.reshape(rows, cols, width))
-    d_kern = tap_grads(features, x_sides, dconv)
-    d_features = spread(dconv.reshape(rows, cols, width), d_sides, cotangent, kernel)
-
-    lanes = hidden // width
-    small = jnp.concatenate(
-        [
-            jnp.sum(d_kern, axis=2).reshape(TAPS * TAPS, width),
-            jnp.sum(sums, axis=1),
-            jnp.sum(d_bup, axis=0).reshape(lanes, width),
-        ],
-        axis=0,
-    )
-    small = jnp.pad(small, ((0, devices - small.shape[0]), (0, 0)))
-    parts = jnp.concatenate(
-        [d_wup.reshape(width, lanes, width), d_gt.reshape(width, lanes, width), small[:, None]], axis=1
-    )
-    parts = jnp.pad(parts, ((0, 0), (0, 16 - parts.shape[1]), (0, 0))).astype(jnp.bfloat16)
-    summed = total(parts).astype(jnp.float32)
+    dconv = dconv.reshape(rows, cols, width)
+    d_features = spread(dconv, halo(dconv), cotangent, kernel)
+    summed = total(parts.reshape(devices, SHARE, width)).reshape(devices * SHARE, width)
     factor = 1.0 / math.sqrt(rows * cols * devices)
-    summed = summed * factor
-    g_wup = summed[:, :lanes].reshape(width, hidden)
-    g_gt = summed[:, lanes : 2 * lanes].reshape(width, hidden)
-    small = summed[:, 2 * lanes]
-    taps = TAPS * TAPS
-    cot_sum = small[taps + 3]
-    g_lscale = jnp.sum(w_down.astype(jnp.float32).T * g_gt, axis=1) + b_down * cot_sum
-    return (
-        d_features,
-        small[:taps].reshape(TAPS, TAPS, width),
-        small[taps],
-        small[taps + 1],
-        small[taps + 2],
-        g_wup,
-        small[taps + 4 : taps + 4 + lanes].reshape(hidden),
-        (g_gt * layer_scale[:, None]).T,
-        layer_scale * cot_sum,
-        g_lscale,
-    )
+    grads = finish(summed, w_down, b_down, layer_scale, factor)
+    return (d_features,) + tuple(g.reshape(-1) if g.shape[0] == 1 else g for g in grads)
 
 
 def solution(mesh):

time: 169 us -> 153 us (0.905)
  Pallas kernels: 100 us -> 90.7 us
  other arithmetic: 4.07 us -> 0.56 us
  local copies, waits for them, and re-layouts: 9.04 us -> 6.99 us
    pallas_call x1, Pallas kernels: 21.3 us -> 2.17 us  [finish(): pl.pallas_call(functools.partial(finish_kernel, factor), out_shape=[jax.S...]
    pallas_call x1, Pallas kernels: 56.5 us -> 65.8 us  [layer(): pl.pallas_call(functools.partial(layer_kernel, block_rows), grid=(rows //...]
    reduce_sum x4 -> x0, other arithmetic: 1.76 us -> none  [the longest x1 0.99 us: local(): jnp.sum(d_kern, axis=2).reshape(TAPS * TAPS, width)]
  transfers between devices with their start and end apart: 10 -> 10, of which waited for: 6 -> 6; matrix products, arithmetic and copies ran while one was open for 3% -> 3% of each run, Pallas kernels for 13% -> 15%
where the time goes in v2:
time: 153 us
  Pallas kernels  90.7 us (59%)
  starting transfers between devices  33.6 us (22%)
  waiting for transfers between devices  20.2 us (13%)
  local copies, waits for them, and re-layouts  6.99 us (5%)
    pallas_call x1, Pallas kernels, layer(): pl.pallas_call(functools.partial(layer_kernel, block_rows), grid=(rows //...  65.8 us
    ppermute x8, starting transfers between devices, shifted(): return lax.ppermute(cells, axis, pairs)  25.3 us
    pallas_call x1, Pallas kernels, spread(): pl.pallas_call(functools.partial(spread_kernel, block_rows), grid=(rows /...  22.7 us
    ppermute x8, waiting for transfers between devices, shifted(): return lax.ppermute(cells, axis, pairs)  16.4 us
    all_to_all x1, starting transfers between devices, total(): return lax.all_to_all(copies, axes, split_axis=0, concat_axis=0, tiled=True)  4.6 us
    all_to_all x1, waiting for transfers between devices, total(): share = lax.all_to_all(parts, axes, split_axis=0, concat_axis=0, tiled=True)  3.77 us
    all_to_all x1, starting transfers between devices, total(): share = lax.all_to_all(parts, axes, split_axis=0, concat_axis=0, tiled=True)  3.71 us
  transfers between devices with their start and end apart: 10, of which 6 were waited for; matrix products, arithmetic and copies ran while one was open for 3% of the time, Pallas kernels for 15%

profile of v2, /device:TPU:1, one launch (start us, length us, event | category | flops | bytes accessed | tf_op | source)
XLA Modules:
  0.0 152.7 jit_solution(14711360057110640552)
XLA Ops:
  0.6 0.8 fusion.3
  1.5 7.1 %collective-permute-start.1 = (bf16[3,64,128]{2,1,0:T(8,128)(2,1)S(1)}, bf16[3,64,128]{2,1,0:T(8,128)(2,1)S(1)}, u32[]{:S(2)}, u32[]{:S(2)}) collective-permute-start(bf16[3,64,128]{2,1,0:T(8,128)(2,1)S(1)} %get-tuple-element.38), channel_id=1, source_target_pairs={{0,120},{8,0},{16,8},{24,16},{32,24},{40,32},{48,40},{56,48},{64,5... | collective-permute-start | bytes 147464 | tf_op jit(solution)/shard_map/ppermute | solution.py:24
  8.6 1.1 fusion.2
  9.7 5.1 %collective-permute-done.top = bf16[3,64,128]{2,1,0:T(8,128)(2,1)S(1)} collective-permute-done((bf16[3,64,128]{2,1,0:T(8,128)(2,1)S(1)}, bf16[3,64,128]{2,1,0:T(8,128)(2,1)S(1)}, u32[]{:S(2)}, u32[]{:S(2)}) %collective-permute-start) | collective-permute-done | bytes 49184 | tf_op jit(solution)/shard_map/ppermute | solution.py:24
  14.9 5.1 %collective-permute-start.2 = (bf16[134,3,128]{2,1,0:T(4,128)(2,1)S(1)}, bf16[134,3,128]{2,1,0:T(4,128)(2,1)S(1)}, u32[]{:S(2)}, u32[]{:S(2)}) collective-permute-start(bf16[134,3,128]{2,1,0:T(4,128)(2,1)S(1)} %pad_maximum_fusion), channel_id=1, source_target_pairs={{0,1},{1,2},{2,3},{3,4},{4,5},{5,6},{6,7},{8,9},{9,10},{10,11},{11... | collective-permute-start | bytes 308744 | tf_op jit(solution)/shard_map/ppermute | solution.py:24
  20.2 1.9 %collective-permute-start.3 = (bf16[134,3,128]{2,1,0:T(4,128)(2,1)S(1)}, bf16[134,3,128]{2,1,0:T(4,128)(2,1)S(1)}, u32[]{:S(2)}, u32[]{:S(2)}) collective-permute-start(bf16[134,3,128]{2,1,0:T(4,128)(2,1)S(1)} %pad_maximum_fusion.1), channel_id=1, source_target_pairs={{1,0},{2,1},{3,2},{4,3},{5,4},{6,5},{7,6},{9,8},{10,9},{11,10},{12... | collective-permute-start | bytes 308744 | tf_op jit(solution)/shard_map/ppermute | solution.py:24
  22.1 4.4 %collective-permute-done.3.right = bf16[134,3,128]{2,1,0:T(4,128)(2,1)S(1)} collective-permute-done((bf16[134,3,128]{2,1,0:T(4,128)(2,1)S(1)}, bf16[134,3,128]{2,1,0:T(4,128)(2,1)S(1)}, u32[]{:S(2)}, u32[]{:S(2)}) %collective-permute-start.3) | collective-permute-done | bytes 102944 | tf_op jit(solution)/shard_map/ppermute | solution.py:24
  27.2 65.8 %layer.1 = (bf16[8192,128]{1,0:T(8,128)(2,1)}, bf16[2048,128]{1,0:T(8,128)(2,1)}) custom-call(bf16[128,64,128]{2,1,0:T(8,128)(2,1)} %own.1, bf16[3,64,128]{2,1,0:T(8,128)(2,1)} %copy-done.8, bf16[3,64,128]{2,1,0:T(8,128)(2,1)} %copy-done.7, bf16[134,3,128]{2,1,0:T(4,128)(2,1)} %copy-done.3, bf16[134,3,128]{2,1,0:T(4,128)(2,1)} %copy-done.4, ...), custom_call_target="tpu_custom_call" | custom-call | tf_op jit(solution)/shard_map/layer/pallas_call | solution.py:250
  93.0 3.7 %all-to-all-start = ((bf16[128,16,128]{2,1,0:T(8,128)(2,1)}), bf16[128,16,128]{2,1,0:T(8,128)(2,1)S(1)}, u32[]{:S(2)}, u32[]{:S(2)}) async-start(bf16[128,16,128]{2,1,0:T(8,128)(2,1)} %bitcast.25), calls=%async_computation | async-start | bytes 1048576 | tf_op jit(solution)/shard_map/all_to_all | solution.py:325
  96.7 0.8 fusion.1
  97.5 1.5 %collective-permute-start.4 = (bf16[3,64,128]{2,1,0:T(8,128)(2,1)S(1)}, bf16[3,64,128]{2,1,0:T(8,128)(2,1)S(1)}, u32[]{:S(2)}, u32[]{:S(2)}) collective-permute-start(bf16[3,64,128]{2,1,0:T(8,128)(2,1)S(1)} %bitcast.27), channel_id=1, source_target_pairs={{0,8},{8,16},{16,24},{24,32},{32,40},{40,48},{48,56},{56,64},{64,7... | collective-permute-start | bytes 147464 | tf_op jit(solution)/shard_map/ppermute | solution.py:24
  99.1 4.1 %collective-permute-start.5 = (bf16[3,64,128]{2,1,0:T(8,128)(2,1)S(1)}, bf16[3,64,128]{2,1,0:T(8,128)(2,1)S(1)}, u32[]{:S(2)}, u32[]{:S(2)}) collective-permute-start(bf16[3,64,128]{2,1,0:T(8,128)(2,1)S(1)} %bitcast.26), channel_id=1, source_target_pairs={{0,120},{8,0},{16,8},{24,16},{32,24},{40,32},{48,40},{56,48},{64,5... | collective-permute-start | bytes 147464 | tf_op jit(solution)/shard_map/ppermute | solution.py:24
  103.2 1.1 fusion
  104.4 2.2 %collective-permute-done.4.top = bf16[3,64,128]{2,1,0:T(8,128)(2,1)S(1)} collective-permute-done((bf16[3,64,128]{2,1,0:T(8,128)(2,1)S(1)}, bf16[3,64,128]{2,1,0:T(8,128)(2,1)S(1)}, u32[]{:S(2)}, u32[]{:S(2)}) %collective-permute-start.4) | collective-permute-done | bytes 49184 | tf_op jit(solution)/shard_map/ppermute | solution.py:24
  106.5 3.8 %all-to-all-done = bf16[128,16,128]{2,1,0:T(8,128)(2,1)S(1)} async-done(((bf16[128,16,128]{2,1,0:T(8,128)(2,1)}), bf16[128,16,128]{2,1,0:T(8,128)(2,1)S(1)}, u32[]{:S(2)}, u32[]{:S(2)}) %all-to-all-start) | async-done | bytes 524320 | tf_op jit(solution)/shard_map/all_to_all | solution.py:325
  110.5 0.9 broadcast_in_dim.2
  111.3 4.6 %all-to-all-start.1 = ((bf16[128,16,128]{2,1,0:T(8,128)(2,1)}), bf16[128,16,128]{2,1,0:T(8,128)(2,1)S(1)}, u32[]{:S(2)}, u32[]{:S(2)}) async-start(bf16[128,16,128]{2,1,0:T(8,128)(2,1)} %broadcast_in_dim.2), calls=%async_computation.1 | async-start | bytes 1048576 | tf_op jit(solution)/shard_map/all_to_all | solution.py:328
  116.1 3.5 %collective-permute-start.6 = (bf16[134,3,128]{2,1,0:T(4,128)(2,1)S(1)}, bf16[134,3,128]{2,1,0:T(4,128)(2,1)S(1)}, u32[]{:S(2)}, u32[]{:S(2)}) collective-permute-start(bf16[134,3,128]{2,1,0:T(4,128)(2,1)S(1)} %pad_maximum_fusion.2), channel_id=1, source_target_pairs={{0,1},{1,2},{2,3},{3,4},{4,5},{5,6},{6,7},{8,9},{9,10},{10,11},{11... | collective-permute-start | bytes 308744 | tf_op jit(solution)/shard_map/ppermute | solution.py:24
  119.8 1.9 %collective-permute-start.7 = (bf16[134,3,128]{2,1,0:T(4,128)(2,1)S(1)}, bf16[134,3,128]{2,1,0:T(4,128)(2,1)S(1)}, u32[]{:S(2)}, u32[]{:S(2)}) collective-permute-start(bf16[134,3,128]{2,1,0:T(4,128)(2,1)S(1)} %pad_maximum_fusion.3), channel_id=1, source_target_pairs={{1,0},{2,1},{3,2},{4,3},{5,4},{6,5},{7,6},{9,8},{10,9},{11,10},{12... | collective-permute-start | bytes 308744 | tf_op jit(solution)/shard_map/ppermute | solution.py:24
  121.7 1.2 collective-permute-done.6.left
  122.9 3.5 %collective-permute-done.7.right = bf16[134,3,128]{2,1,0:T(4,128)(2,1)S(1)} collective-permute-done((bf16[134,3,128]{2,1,0:T(4,128)(2,1)S(1)}, bf16[134,3,128]{2,1,0:T(4,128)(2,1)S(1)}, u32[]{:S(2)}, u32[]{:S(2)}) %collective-permute-start.7) | collective-permute-done | bytes 102944 | tf_op jit(solution)/shard_map/ppermute | solution.py:24
  127.1 22.7 %spread.1 = bf16[8192,128]{1,0:T(8,128)(2,1)} custom-call(bf16[128,64,128]{2,1,0:T(8,128)(2,1)} %bitcast.22, bf16[3,64,128]{2,1,0:T(8,128)(2,1)} %copy-done.5, bf16[3,64,128]{2,1,0:T(8,128)(2,1)} %copy-done.6, bf16[134,3,128]{2,1,0:T(4,128)(2,1)} %copy-done.1, bf16[134,3,128]{2,1,0:T(4,128)(2,1)} %copy-done.2, bf16[8192,128]{1,0:T(8,128)(2,1)} %bitcast.20, ...), custom_call_target="tpu_custom_call" | custom-call | tf_op jit(solution)/shard_map/spread/pallas_call | solution.py:306
  149.7 0.8 copy-done
  150.6 2.2 %finish.1 = (f32[7,7,128]{2,1,0:T(8,128)}, f32[1,128]{1,0:T(1,128)}, f32[1,128]{1,0:T(1,128)}, f32[1,128]{1,0:T(1,128)}, f32[128,512]{1,0:T(8,128)}, /*index=5*/...) custom-call(bf16[2048,128]{1,0:T(8,128)(2,1)} %bitcast.23, bf16[512,128]{1,0:T(8,128)(2,1)} %wdown_ref.3, ...), custom_call_target="tpu_custom_call" | custom-call | tf_op jit(solution)/shard_map/finish/pallas_call | solution.py:381
  (31 shorter events, 2.0 us)
Async XLA Ops:
  1.5 8.3 %collective-permute-start.1 = (bf16[3,64,128]{2,1,0:T(8,128)(2,1)S(1)}, bf16[3,64,128]{2,1,0:T(8,128)(2,1)S(1)}, u32[]{:S(2)}, u32[]{:S(2)}) collective-permute-start(bf16[3,64,128]{2,1,0:T(8,128)(2,1)S(1)} %get-tuple-element.38), channel_id=1, source_target_pairs={{0,120},{8,0},{16,8},{24,16},{32,24},{40,32},{48,40},{56,48},{64,5... | collective-permute-start | bytes 147464 | tf_op jit(solution)/shard_map/ppermute | solution.py:24
  8.6 6.3 %collective-permute-start = (bf16[3,64,128]{2,1,0:T(8,128)(2,1)S(1)}, bf16[3,64,128]{2,1,0:T(8,128)(2,1)S(1)}, u32[]{:S(2)}, u32[]{:S(2)}) collective-permute-start(bf16[3,64,128]{2,1,0:T(8,128)(2,1)S(1)} %get-tuple-element.39), channel_id=1, source_target_pairs={{0,8},{8,16},{16,24},{24,32},{32,40},{40,48},{48,56},{56,64},{64,7... | collective-permute-start | bytes 147464 | tf_op jit(solution)/shard_map/ppermute | solution.py:24
  9.7 16.8 %copy-start.7 = (bf16[3,64,128]{2,1,0:T(8,128)(2,1)}, bf16[3,64,128]{2,1,0:T(8,128)(2,1)S(1)}, u32[]{:S(2)}) copy-start(bf16[3,64,128]{2,1,0:T(8,128)(2,1)S(1)} %collective-permute-done.1.bottom) | copy-start | bytes 147460
  14.8 11.7 %copy-start.8 = (bf16[3,64,128]{2,1,0:T(8,128)(2,1)}, bf16[3,64,128]{2,1,0:T(8,128)(2,1)S(1)}, u32[]{:S(2)}) copy-start(bf16[3,64,128]{2,1,0:T(8,128)(2,1)S(1)} %collective-permute-done.top) | copy-start | bytes 147460
  14.9 7.2 %collective-permute-start.2 = (bf16[134,3,128]{2,1,0:T(4,128)(2,1)S(1)}, bf16[134,3,128]{2,1,0:T(4,128)(2,1)S(1)}, u32[]{:S(2)}, u32[]{:S(2)}) collective-permute-start(bf16[134,3,128]{2,1,0:T(4,128)(2,1)S(1)} %pad_maximum_fusion), channel_id=1, source_target_pairs={{0,1},{1,2},{2,3},{3,4},{4,5},{5,6},{6,7},{8,9},{9,10},{10,11},{11... | collective-permute-start | bytes 308744 | tf_op jit(solution)/shard_map/ppermute | solution.py:24
  20.2 6.4 %collective-permute-start.3 = (bf16[134,3,128]{2,1,0:T(4,128)(2,1)S(1)}, bf16[134,3,128]{2,1,0:T(4,128)(2,1)S(1)}, u32[]{:S(2)}, u32[]{:S(2)}) collective-permute-start(bf16[134,3,128]{2,1,0:T(4,128)(2,1)S(1)} %pad_maximum_fusion.1), channel_id=1, source_target_pairs={{1,0},{2,1},{3,2},{4,3},{5,4},{6,5},{7,6},{9,8},{10,9},{11,10},{12... | collective-permute-start | bytes 308744 | tf_op jit(solution)/shard_map/ppermute | solution.py:24
  22.1 4.4 %copy-start.3 = (bf16[134,3,128]{2,1,0:T(4,128)(2,1)}, bf16[134,3,128]{2,1,0:T(4,128)(2,1)S(1)}, u32[]{:S(2)}) copy-start(bf16[134,3,128]{2,1,0:T(4,128)(2,1)S(1)} %collective-permute-done.2.left) | copy-start | bytes 308740
  26.5 0.7 copy-start.4
  93.0 17.3 %all-to-all-start = ((bf16[128,16,128]{2,1,0:T(8,128)(2,1)}), bf16[128,16,128]{2,1,0:T(8,128)(2,1)S(1)}, u32[]{:S(2)}, u32[]{:S(2)}) async-start(bf16[128,16,128]{2,1,0:T(8,128)(2,1)} %bitcast.25), calls=%async_computation | async-start | bytes 1048576 | tf_op jit(solution)/shard_map/all_to_all | solution.py:325
  97.5 9.0 %collective-permute-start.4 = (bf16[3,64,128]{2,1,0:T(8,128)(2,1)S(1)}, bf16[3,64,128]{2,1,0:T(8,128)(2,1)S(1)}, u32[]{:S(2)}, u32[]{:S(2)}) collective-permute-start(bf16[3,64,128]{2,1,0:T(8,128)(2,1)S(1)} %bitcast.27), channel_id=1, source_target_pairs={{0,8},{8,16},{16,24},{24,32},{32,40},{40,48},{48,56},{56,64},{64,7... | collective-permute-start | bytes 147464 | tf_op jit(solution)/shard_map/ppermute | solution.py:24
  99.1 16.9 %collective-permute-start.5 = (bf16[3,64,128]{2,1,0:T(8,128)(2,1)S(1)}, bf16[3,64,128]{2,1,0:T(8,128)(2,1)S(1)}, u32[]{:S(2)}, u32[]{:S(2)}) collective-permute-start(bf16[3,64,128]{2,1,0:T(8,128)(2,1)S(1)} %bitcast.26), channel_id=1, source_target_pairs={{0,120},{8,0},{16,8},{24,16},{32,24},{40,32},{48,40},{56,48},{64,5... | collective-permute-start | bytes 147464 | tf_op jit(solution)/shard_map/ppermute | solution.py:24
  106.5 19.9 %copy-start.5 = (bf16[3,64,128]{2,1,0:T(8,128)(2,1)}, bf16[3,64,128]{2,1,0:T(8,128)(2,1)S(1)}, u32[]{:S(2)}) copy-start(bf16[3,64,128]{2,1,0:T(8,128)(2,1)S(1)} %collective-permute-done.4.top) | copy-start | bytes 147460
  111.3 38.4 %all-to-all-start.1 = ((bf16[128,16,128]{2,1,0:T(8,128)(2,1)}), bf16[128,16,128]{2,1,0:T(8,128)(2,1)S(1)}, u32[]{:S(2)}, u32[]{:S(2)}) async-start(bf16[128,16,128]{2,1,0:T(8,128)(2,1)} %broadcast_in_dim.2), calls=%async_computation.1 | async-start | bytes 1048576 | tf_op jit(solution)/shard_map/all_to_all | solution.py:328
  116.0 10.4 %copy-start.6 = (bf16[3,64,128]{2,1,0:T(8,128)(2,1)}, bf16[3,64,128]{2,1,0:T(8,128)(2,1)S(1)}, u32[]{:S(2)}) copy-start(bf16[3,64,128]{2,1,0:T(8,128)(2,1)S(1)} %collective-permute-done.5.bottom) | copy-start | bytes 147460
  116.1 6.8 %collective-permute-start.6 = (bf16[134,3,128]{2,1,0:T(4,128)(2,1)S(1)}, bf16[134,3,128]{2,1,0:T(4,128)(2,1)S(1)}, u32[]{:S(2)}, u32[]{:S(2)}) collective-permute-start(bf16[134,3,128]{2,1,0:T(4,128)(2,1)S(1)} %pad_maximum_fusion.2), channel_id=1, source_target_pairs={{0,1},{1,2},{2,3},{3,4},{4,5},{5,6},{6,7},{8,9},{9,10},{10,11},{11... | collective-permute-start | bytes 308744 | tf_op jit(solution)/shard_map/ppermute | solution.py:24
  119.8 6.6 %collective-permute-start.7 = (bf16[134,3,128]{2,1,0:T(4,128)(2,1)S(1)}, bf16[134,3,128]{2,1,0:T(4,128)(2,1)S(1)}, u32[]{:S(2)}, u32[]{:S(2)}) collective-permute-start(bf16[134,3,128]{2,1,0:T(4,128)(2,1)S(1)} %pad_maximum_fusion.3), channel_id=1, source_target_pairs={{1,0},{2,1},{3,2},{4,3},{5,4},{6,5},{7,6},{9,8},{10,9},{11,10},{12... | collective-permute-start | bytes 308744 | tf_op jit(solution)/shard_map/ppermute | solution.py:24
  122.9 3.5 %copy-start.1 = (bf16[134,3,128]{2,1,0:T(4,128)(2,1)}, bf16[134,3,128]{2,1,0:T(4,128)(2,1)S(1)}, u32[]{:S(2)}) copy-start(bf16[134,3,128]{2,1,0:T(4,128)(2,1)S(1)} %collective-permute-done.6.left) | copy-start | bytes 308740
  126.4 0.7 copy-start.2
  149.7 0.8 copy-start

commit v3 on v2

--- a/solution.py
+++ b/solution.py
@@ -152,13 +152,11 @@
     wdown_ref,
     scale_ref,
     dconv_ref,
-    parts_ref,
     dwup_ref,
     dgt_ref,
     sums_ref,
     dbup_ref,
     dkern_ref,
-    stage_ref,
     pad_ref,
     pair_ref,
     w_ref,
@@ -219,21 +217,6 @@
     for (a, b), value in taps.items():
         dkern_ref[a, b] += value
 
-    @pl.when(step == pl.num_programs(0) - 1)
-    def _():
-        stage_ref[...] = jnp.zeros_like(stage_ref)
-        for k in range(LANES):
-            lanes = slice(k * 128, k * 128 + 128)
-            stage_ref[pl.ds(k, 128, stride=SHARE), :] = dwup_ref[:, lanes]
-            stage_ref[pl.ds(LANES + k, 128, stride=SHARE), :] = dgt_ref[:, lanes]
-        small = [dkern_ref[a, b] for a in range(TAPS) for b in range(TAPS)]
-        small += [sums_ref[k] for k in range(4)]
-        small += [dbup_ref[:, k * 128 : k * 128 + 128] for k in range(LANES)]
-        for i, value in enumerate(small):
-            at = i * SHARE + 2 * LANES
-            stage_ref[at : at + 1, :] = jnp.sum(value, axis=0, keepdims=True)
-        parts_ref[...] = stage_ref[...].astype(jnp.bfloat16)
-
 
 def layer(x, sides, cotangent, kernel, kbias, gain, shift, wup, bup, wdown, scale):
     rows, cols, width = x.shape
@@ -254,18 +237,23 @@
         + [whole(s) for s in sides]
         + [cells]
         + [whole(c) for c in consts],
-        out_specs=[cells, full(width * SHARE, width)],
+        out_specs=[
+            cells,
+            full(width, hidden),
+            full(width, hidden),
+            full(4, 8, width),
+            full(8, hidden),
+            full(TAPS, TAPS, 8, width),
+        ],
         out_shape=[
             jax.ShapeDtypeStruct((rows * cols, width), jnp.bfloat16),
-            jax.ShapeDtypeStruct((width * SHARE, width), jnp.bfloat16),
+            jax.ShapeDtypeStruct((width, hidden), f32),
+            jax.ShapeDtypeStruct((width, hidden), f32),
+            jax.ShapeDtypeStruct((4, 8, width), f32),
+            jax.ShapeDtypeStruct((8, hidden), f32),
+            jax.ShapeDtypeStruct((TAPS, TAPS, 8, width), f32),
         ],
         scratch_shapes=[
-            pltpu.VMEM((width, hidden), f32),
-            pltpu.VMEM((width, hidden), f32),
-            pltpu.VMEM((4, 8, width), f32),
-            pltpu.VMEM((8, hidden), f32),
-            pltpu.VMEM((TAPS, TAPS, 8, width), f32),
-            pltpu.VMEM((width * SHARE, width), f32),
             pltpu.VMEM((padded, cols + 2 * OFF, width), f32),
             pltpu.VMEM((PAIRS, padded * cols // 2, 2 * width), jnp.bfloat16),
             pltpu.VMEM((TAPS * PAIRS * 2 * width, 2 * width), jnp.bfloat16),
@@ -275,6 +263,31 @@
         compiler_params=pltpu.CompilerParams(vmem_limit_bytes=GRANT),
         name="layer",
     )(x, *sides, cotangent.reshape(rows * cols, width), *consts)
+
+
+def parts_kernel(dwup_ref, dgt_ref, sums_ref, dbup_ref, dkern_ref, parts_ref, stage_ref):
+    stage_ref[...] = jnp.zeros_like(stage_ref)
+    for k in range(LANES):
+        lanes = slice(k * 128, k * 128 + 128)
+        stage_ref[pl.ds(k, 128, stride=SHARE), :] = dwup_ref[:, lanes]
+        stage_ref[pl.ds(LANES + k, 128, stride=SHARE), :] = dgt_ref[:, lanes]
+    small = [dkern_ref[a, b] for a in range(TAPS) for b in range(TAPS)]
+    small += [sums_ref[k] for k in range(4)]
+    small += [dbup_ref[:, k * 128 : k * 128 + 128] for k in range(LANES)]
+    for i, value in enumerate(small):
+        at = i * SHARE + 2 * LANES
+        stage_ref[at : at + 1, :] = jnp.sum(value, axis=0, keepdims=True)
+    parts_ref[...] = stage_ref[...].astype(jnp.bfloat16)
+
+
+def shares(*sums):
+    width = sums[0].shape[0]
+    return pl.pallas_call(
+        parts_kernel,
+        out_shape=jax.ShapeDtypeStruct((width * SHARE, width), jnp.bfloat16),
+        scratch_shapes=[pltpu.VMEM((width * SHARE, width), jnp.float32)],
+        name="shares",
+    )(*sums)
 
 
 def spread_kernel(
@@ -391,7 +404,7 @@
 ):
     rows, cols, width = features.shape
     devices = lax.axis_size("gx") * lax.axis_size("gy")
-    dconv, parts = layer(
+    dconv, *sums = layer(
         features,
         halo(features),
         cotangent,
@@ -406,7 +419,7 @@
     )
     dconv = dconv.reshape(rows, cols, width)
     d_features = spread(dconv, halo(dconv), cotangent, kernel)
-    summed = total(parts.reshape(devices, SHARE, width)).reshape(devices * SHARE, width)
+    summed = total(shares(*sums).reshape(devices, SHARE, width)).reshape(devices * SHARE, width)
     factor = 1.0 / math.sqrt(rows * cols * devices)
     grads = finish(summed, w_down, b_down, layer_scale, factor)
     return (d_features,) + tuple(g.reshape(-1) if g.shape[0] == 1 else g for g in grads)

time: 153 us -> 138 us (0.902)
  Pallas kernels: 90.7 us -> 75.6 us
    pallas_call x1, Pallas kernels: 65.8 us -> 48.4 us  [layer(): pl.pallas_call(functools.partial(layer_kernel, block_rows), grid=(rows //...]
    pallas_call x0 -> x1, Pallas kernels: none -> 2.31 us  [shares(): pl.pallas_call(parts_kernel, out_shape=jax.ShapeDtypeStruct((width * SHAR...]
  transfers between devices with their start and end apart: 10 -> 10, of which waited for: 6 -> 6; matrix products, arithmetic and copies ran while one was open for 3% -> 3% of each run, Pallas kernels for 15% -> 16%
where the time goes in v3:
time: 138 us
  Pallas kernels  75.6 us (55%)
  starting transfers between devices  33.6 us (24%)
  waiting for transfers between devices  20.2 us (15%)
  local copies, waits for them, and re-layouts  6.99 us (5%)
    pallas_call x1, Pallas kernels, layer(): pl.pallas_call(functools.partial(layer_kernel, block_rows), grid=(rows //...  48.4 us
    ppermute x8, starting transfers between devices, shifted(): return lax.ppermute(cells, axis, pairs)  25.3 us
    pallas_call x1, Pallas kernels, spread(): pl.pallas_call(functools.partial(spread_kernel, block_rows), grid=(rows /...  22.7 us
    ppermute x8, waiting for transfers between devices, shifted(): return lax.ppermute(cells, axis, pairs)  16.4 us
    all_to_all x1, starting transfers between devices, total(): return lax.all_to_all(copies, axes, split_axis=0, concat_axis=0, tiled=True)  4.6 us
    all_to_all x1, waiting for transfers between devices, total(): share = lax.all_to_all(parts, axes, split_axis=0, concat_axis=0, tiled=True)  3.77 us
    all_to_all x1, starting transfers between devices, total(): share = lax.all_to_all(parts, axes, split_axis=0, concat_axis=0, tiled=True)  3.7 us
  transfers between devices with their start and end apart: 10, of which 6 were waited for; matrix products, arithmetic and copies ran while one was open for 3% of the time, Pallas kernels for 16%

profile of v3, /device:TPU:1, one launch (start us, length us, event | category | flops | bytes accessed | tf_op | source)
XLA Modules:
  0.0 137.6 jit_solution(8886330890375228454)
XLA Ops:
  0.6 0.8 fusion.3
  1.5 7.1 %collective-permute-start.1 = (bf16[3,64,128]{2,1,0:T(8,128)(2,1)S(1)}, bf16[3,64,128]{2,1,0:T(8,128)(2,1)S(1)}, u32[]{:S(2)}, u32[]{:S(2)}) collective-permute-start(bf16[3,64,128]{2,1,0:T(8,128)(2,1)S(1)} %get-tuple-element.46), channel_id=1, source_target_pairs={{0,120},{8,0},{16,8},{24,16},{32,24},{40,32},{48,40},{56,48},{64,5... | collective-permute-start | bytes 147464 | tf_op jit(solution)/shard_map/ppermute | solution.py:24
  8.6 1.1 fusion.2
  9.7 5.1 %collective-permute-done.top = bf16[3,64,128]{2,1,0:T(8,128)(2,1)S(1)} collective-permute-done((bf16[3,64,128]{2,1,0:T(8,128)(2,1)S(1)}, bf16[3,64,128]{2,1,0:T(8,128)(2,1)S(1)}, u32[]{:S(2)}, u32[]{:S(2)}) %collective-permute-start) | collective-permute-done | bytes 49184 | tf_op jit(solution)/shard_map/ppermute | solution.py:24
  14.9 5.1 %collective-permute-start.2 = (bf16[134,3,128]{2,1,0:T(4,128)(2,1)S(1)}, bf16[134,3,128]{2,1,0:T(4,128)(2,1)S(1)}, u32[]{:S(2)}, u32[]{:S(2)}) collective-permute-start(bf16[134,3,128]{2,1,0:T(4,128)(2,1)S(1)} %pad_maximum_fusion), channel_id=1, source_target_pairs={{0,1},{1,2},{2,3},{3,4},{4,5},{5,6},{6,7},{8,9},{9,10},{10,11},{11... | collective-permute-start | bytes 308744 | tf_op jit(solution)/shard_map/ppermute | solution.py:24
  20.2 1.9 %collective-permute-start.3 = (bf16[134,3,128]{2,1,0:T(4,128)(2,1)S(1)}, bf16[134,3,128]{2,1,0:T(4,128)(2,1)S(1)}, u32[]{:S(2)}, u32[]{:S(2)}) collective-permute-start(bf16[134,3,128]{2,1,0:T(4,128)(2,1)S(1)} %pad_maximum_fusion.1), channel_id=1, source_target_pairs={{1,0},{2,1},{3,2},{4,3},{5,4},{6,5},{7,6},{9,8},{10,9},{11,10},{12... | collective-permute-start | bytes 308744 | tf_op jit(solution)/shard_map/ppermute | solution.py:24
  22.1 4.4 %collective-permute-done.3.right = bf16[134,3,128]{2,1,0:T(4,128)(2,1)S(1)} collective-permute-done((bf16[134,3,128]{2,1,0:T(4,128)(2,1)S(1)}, bf16[134,3,128]{2,1,0:T(4,128)(2,1)S(1)}, u32[]{:S(2)}, u32[]{:S(2)}) %collective-permute-start.3) | collective-permute-done | bytes 102944 | tf_op jit(solution)/shard_map/ppermute | solution.py:24
  27.2 48.4 %layer.1 = (bf16[8192,128]{1,0:T(8,128)(2,1)}, f32[128,512]{1,0:T(8,128)}, f32[128,512]{1,0:T(8,128)}, f32[4,8,128]{2,1,0:T(8,128)}, f32[8,512]{1,0:T(8,128)}, /*index=5*/f32[7,7,8,128]{3,2,1,0:T(8,128)}) custom-call(bf16[128,64,128]{2,1,0:T(8,128)(2,1)} %own.1, bf16[3,64,128]{2,1,0:T(8,128)(2,1)} %copy-done.8, bf16[3,64,128]{2,1,0:T(8,128)(2,1)} %copy-done.7, ...), custom_call_target="tpu_custom_call" | custom-call | tf_op jit(solution)/shard_map/layer/pallas_call | solution.py:233
  75.6 2.3 %shares.1 = bf16[2048,128]{1,0:T(8,128)(2,1)} custom-call(f32[128,512]{1,0:T(8,128)} %get-tuple-element.26.dwup_ref, f32[128,512]{1,0:T(8,128)} %get-tuple-element.27.dgt_ref, f32[4,8,128]{2,1,0:T(8,128)} %get-tuple-element.28.sums_ref, f32[8,512]{1,0:T(8,128)} %get-tuple-element.29.dbup_ref, f32[7,7,8,128]{3,2,1,0:T(8,128)} %get-tuple-element.30.dkern_ref), custom_call_target="tpu_custom_call" | custom-call | tf_op jit(solution)/shard_map/shares/pallas_call | solution.py:285
  77.9 3.7 %all-to-all-start = ((bf16[128,16,128]{2,1,0:T(8,128)(2,1)}), bf16[128,16,128]{2,1,0:T(8,128)(2,1)S(1)}, u32[]{:S(2)}, u32[]{:S(2)}) async-start(bf16[128,16,128]{2,1,0:T(8,128)(2,1)} %bitcast.25), calls=%async_computation | async-start | bytes 1048576 | tf_op jit(solution)/shard_map/all_to_all | solution.py:338
  81.6 0.8 fusion.1
  82.4 1.5 %collective-permute-start.4 = (bf16[3,64,128]{2,1,0:T(8,128)(2,1)S(1)}, bf16[3,64,128]{2,1,0:T(8,128)(2,1)S(1)}, u32[]{:S(2)}, u32[]{:S(2)}) collective-permute-start(bf16[3,64,128]{2,1,0:T(8,128)(2,1)S(1)} %bitcast.27), channel_id=1, source_target_pairs={{0,8},{8,16},{16,24},{24,32},{32,40},{40,48},{48,56},{56,64},{64,7... | collective-permute-start | bytes 147464 | tf_op jit(solution)/shard_map/ppermute | solution.py:24
  84.0 4.1 %collective-permute-start.5 = (bf16[3,64,128]{2,1,0:T(8,128)(2,1)S(1)}, bf16[3,64,128]{2,1,0:T(8,128)(2,1)S(1)}, u32[]{:S(2)}, u32[]{:S(2)}) collective-permute-start(bf16[3,64,128]{2,1,0:T(8,128)(2,1)S(1)} %bitcast.26), channel_id=1, source_target_pairs={{0,120},{8,0},{16,8},{24,16},{32,24},{40,32},{48,40},{56,48},{64,5... | collective-permute-start | bytes 147464 | tf_op jit(solution)/shard_map/ppermute | solution.py:24
  88.1 1.1 fusion
  89.3 2.2 %collective-permute-done.4.top = bf16[3,64,128]{2,1,0:T(8,128)(2,1)S(1)} collective-permute-done((bf16[3,64,128]{2,1,0:T(8,128)(2,1)S(1)}, bf16[3,64,128]{2,1,0:T(8,128)(2,1)S(1)}, u32[]{:S(2)}, u32[]{:S(2)}) %collective-permute-start.4) | collective-permute-done | bytes 49184 | tf_op jit(solution)/shard_map/ppermute | solution.py:24
  91.5 3.8 %all-to-all-done = bf16[128,16,128]{2,1,0:T(8,128)(2,1)S(1)} async-done(((bf16[128,16,128]{2,1,0:T(8,128)(2,1)}), bf16[128,16,128]{2,1,0:T(8,128)(2,1)S(1)}, u32[]{:S(2)}, u32[]{:S(2)}) %all-to-all-start) | async-done | bytes 524320 | tf_op jit(solution)/shard_map/all_to_all | solution.py:338
  95.4 0.9 broadcast_in_dim.2
  96.2 4.6 %all-to-all-start.1 = ((bf16[128,16,128]{2,1,0:T(8,128)(2,1)}), bf16[128,16,128]{2,1,0:T(8,128)(2,1)S(1)}, u32[]{:S(2)}, u32[]{:S(2)}) async-start(bf16[128,16,128]{2,1,0:T(8,128)(2,1)} %broadcast_in_dim.2), calls=%async_computation.1 | async-start | bytes 1048576 | tf_op jit(solution)/shard_map/all_to_all | solution.py:341
  101.0 3.5 %collective-permute-start.6 = (bf16[134,3,128]{2,1,0:T(4,128)(2,1)S(1)}, bf16[134,3,128]{2,1,0:T(4,128)(2,1)S(1)}, u32[]{:S(2)}, u32[]{:S(2)}) collective-permute-start(bf16[134,3,128]{2,1,0:T(4,128)(2,1)S(1)} %pad_maximum_fusion.2), channel_id=1, source_target_pairs={{0,1},{1,2},{2,3},{3,4},{4,5},{5,6},{6,7},{8,9},{9,10},{10,11},{11... | collective-permute-start | bytes 308744 | tf_op jit(solution)/shard_map/ppermute | solution.py:24
  104.7 1.9 %collective-permute-start.7 = (bf16[134,3,128]{2,1,0:T(4,128)(2,1)S(1)}, bf16[134,3,128]{2,1,0:T(4,128)(2,1)S(1)}, u32[]{:S(2)}, u32[]{:S(2)}) collective-permute-start(bf16[134,3,128]{2,1,0:T(4,128)(2,1)S(1)} %pad_maximum_fusion.3), channel_id=1, source_target_pairs={{1,0},{2,1},{3,2},{4,3},{5,4},{6,5},{7,6},{9,8},{10,9},{11,10},{12... | collective-permute-start | bytes 308744 | tf_op jit(solution)/shard_map/ppermute | solution.py:24
  106.6 1.2 collective-permute-done.6.left
  107.8 3.5 %collective-permute-done.7.right = bf16[134,3,128]{2,1,0:T(4,128)(2,1)S(1)} collective-permute-done((bf16[134,3,128]{2,1,0:T(4,128)(2,1)S(1)}, bf16[134,3,128]{2,1,0:T(4,128)(2,1)S(1)}, u32[]{:S(2)}, u32[]{:S(2)}) %collective-permute-start.7) | collective-permute-done | bytes 102944 | tf_op jit(solution)/shard_map/ppermute | solution.py:24
  112.0 22.7 %spread.1 = bf16[8192,128]{1,0:T(8,128)(2,1)} custom-call(bf16[128,64,128]{2,1,0:T(8,128)(2,1)} %bitcast.22, bf16[3,64,128]{2,1,0:T(8,128)(2,1)} %copy-done.5, bf16[3,64,128]{2,1,0:T(8,128)(2,1)} %copy-done.6, bf16[134,3,128]{2,1,0:T(4,128)(2,1)} %copy-done.1, bf16[134,3,128]{2,1,0:T(4,128)(2,1)} %copy-done.2, bf16[8192,128]{1,0:T(8,128)(2,1)} %bitcast.20, ...), custom_call_target="tpu_custom_call" | custom-call | tf_op jit(solution)/shard_map/spread/pallas_call | solution.py:319
  135.5 2.2 %finish.1 = (f32[7,7,128]{2,1,0:T(8,128)}, f32[1,128]{1,0:T(1,128)}, f32[1,128]{1,0:T(1,128)}, f32[1,128]{1,0:T(1,128)}, f32[128,512]{1,0:T(8,128)}, /*index=5*/...) custom-call(bf16[2048,128]{1,0:T(8,128)(2,1)} %bitcast.23, bf16[512,128]{1,0:T(8,128)(2,1)} %wdown_ref.3, ...), custom_call_target="tpu_custom_call" | custom-call | tf_op jit(solution)/shard_map/finish/pallas_call | solution.py:394
  (32 shorter events, 2.8 us)
Async XLA Ops:
  1.5 8.3 %collective-permute-start.1 = (bf16[3,64,128]{2,1,0:T(8,128)(2,1)S(1)}, bf16[3,64,128]{2,1,0:T(8,128)(2,1)S(1)}, u32[]{:S(2)}, u32[]{:S(2)}) collective-permute-start(bf16[3,64,128]{2,1,0:T(8,128)(2,1)S(1)} %get-tuple-element.46), channel_id=1, source_target_pairs={{0,120},{8,0},{16,8},{24,16},{32,24},{40,32},{48,40},{56,48},{64,5... | collective-permute-start | bytes 147464 | tf_op jit(solution)/shard_map/ppermute | solution.py:24
  8.6 6.3 %collective-permute-start = (bf16[3,64,128]{2,1,0:T(8,128)(2,1)S(1)}, bf16[3,64,128]{2,1,0:T(8,128)(2,1)S(1)}, u32[]{:S(2)}, u32[]{:S(2)}) collective-permute-start(bf16[3,64,128]{2,1,0:T(8,128)(2,1)S(1)} %get-tuple-element.47), channel_id=1, source_target_pairs={{0,8},{8,16},{16,24},{24,32},{32,40},{40,48},{48,56},{56,64},{64,7... | collective-permute-start | bytes 147464 | tf_op jit(solution)/shard_map/ppermute | solution.py:24
  9.7 16.8 %copy-start.7 = (bf16[3,64,128]{2,1,0:T(8,128)(2,1)}, bf16[3,64,128]{2,1,0:T(8,128)(2,1)S(1)}, u32[]{:S(2)}) copy-start(bf16[3,64,128]{2,1,0:T(8,128)(2,1)S(1)} %collective-permute-done.1.bottom) | copy-start | bytes 147460
  14.8 11.7 %copy-start.8 = (bf16[3,64,128]{2,1,0:T(8,128)(2,1)}, bf16[3,64,128]{2,1,0:T(8,128)(2,1)S(1)}, u32[]{:S(2)}) copy-start(bf16[3,64,128]{2,1,0:T(8,128)(2,1)S(1)} %collective-permute-done.top) | copy-start | bytes 147460
  14.9 7.2 %collective-permute-start.2 = (bf16[134,3,128]{2,1,0:T(4,128)(2,1)S(1)}, bf16[134,3,128]{2,1,0:T(4,128)(2,1)S(1)}, u32[]{:S(2)}, u32[]{:S(2)}) collective-permute-start(bf16[134,3,128]{2,1,0:T(4,128)(2,1)S(1)} %pad_maximum_fusion), channel_id=1, source_target_pairs={{0,1},{1,2},{2,3},{3,4},{4,5},{5,6},{6,7},{8,9},{9,10},{10,11},{11... | collective-permute-start | bytes 308744 | tf_op jit(solution)/shard_map/ppermute | solution.py:24
  20.2 6.4 %collective-permute-start.3 = (bf16[134,3,128]{2,1,0:T(4,128)(2,1)S(1)}, bf16[134,3,128]{2,1,0:T(4,128)(2,1)S(1)}, u32[]{:S(2)}, u32[]{:S(2)}) collective-permute-start(bf16[134,3,128]{2,1,0:T(4,128)(2,1)S(1)} %pad_maximum_fusion.1), channel_id=1, source_target_pairs={{1,0},{2,1},{3,2},{4,3},{5,4},{6,5},{7,6},{9,8},{10,9},{11,10},{12... | collective-permute-start | bytes 308744 | tf_op jit(solution)/shard_map/ppermute | solution.py:24
  22.1 4.4 %copy-start.3 = (bf16[134,3,128]{2,1,0:T(4,128)(2,1)}, bf16[134,3,128]{2,1,0:T(4,128)(2,1)S(1)}, u32[]{:S(2)}) copy-start(bf16[134,3,128]{2,1,0:T(4,128)(2,1)S(1)} %collective-permute-done.2.left) | copy-start | bytes 308740
  26.5 0.7 copy-start.4
  77.9 17.3 %all-to-all-start = ((bf16[128,16,128]{2,1,0:T(8,128)(2,1)}), bf16[128,16,128]{2,1,0:T(8,128)(2,1)S(1)}, u32[]{:S(2)}, u32[]{:S(2)}) async-start(bf16[128,16,128]{2,1,0:T(8,128)(2,1)} %bitcast.25), calls=%async_computation | async-start | bytes 1048576 | tf_op jit(solution)/shard_map/all_to_all | solution.py:338
  82.4 9.0 %collective-permute-start.4 = (bf16[3,64,128]{2,1,0:T(8,128)(2,1)S(1)}, bf16[3,64,128]{2,1,0:T(8,128)(2,1)S(1)}, u32[]{:S(2)}, u32[]{:S(2)}) collective-permute-start(bf16[3,64,128]{2,1,0:T(8,128)(2,1)S(1)} %bitcast.27), channel_id=1, source_target_pairs={{0,8},{8,16},{16,24},{24,32},{32,40},{40,48},{48,56},{56,64},{64,7... | collective-permute-start | bytes 147464 | tf_op jit(solution)/shard_map/ppermute | solution.py:24
  84.0 16.9 %collective-permute-start.5 = (bf16[3,64,128]{2,1,0:T(8,128)(2,1)S(1)}, bf16[3,64,128]{2,1,0:T(8,128)(2,1)S(1)}, u32[]{:S(2)}, u32[]{:S(2)}) collective-permute-start(bf16[3,64,128]{2,1,0:T(8,128)(2,1)S(1)} %bitcast.26), channel_id=1, source_target_pairs={{0,120},{8,0},{16,8},{24,16},{32,24},{40,32},{48,40},{56,48},{64,5... | collective-permute-start | bytes 147464 | tf_op jit(solution)/shard_map/ppermute | solution.py:24
  91.4 19.9 %copy-start.5 = (bf16[3,64,128]{2,1,0:T(8,128)(2,1)}, bf16[3,64,128]{2,1,0:T(8,128)(2,1)S(1)}, u32[]{:S(2)}) copy-start(bf16[3,64,128]{2,1,0:T(8,128)(2,1)S(1)} %collective-permute-done.4.top) | copy-start | bytes 147460
  96.2 38.4 %all-to-all-start.1 = ((bf16[128,16,128]{2,1,0:T(8,128)(2,1)}), bf16[128,16,128]{2,1,0:T(8,128)(2,1)S(1)}, u32[]{:S(2)}, u32[]{:S(2)}) async-start(bf16[128,16,128]{2,1,0:T(8,128)(2,1)} %broadcast_in_dim.2), calls=%async_computation.1 | async-start | bytes 1048576 | tf_op jit(solution)/shard_map/all_to_all | solution.py:341
  100.9 10.4 %copy-start.6 = (bf16[3,64,128]{2,1,0:T(8,128)(2,1)}, bf16[3,64,128]{2,1,0:T(8,128)(2,1)S(1)}, u32[]{:S(2)}) copy-start(bf16[3,64,128]{2,1,0:T(8,128)(2,1)S(1)} %collective-permute-done.5.bottom) | copy-start | bytes 147460
  101.0 6.8 %collective-permute-start.6 = (bf16[134,3,128]{2,1,0:T(4,128)(2,1)S(1)}, bf16[134,3,128]{2,1,0:T(4,128)(2,1)S(1)}, u32[]{:S(2)}, u32[]{:S(2)}) collective-permute-start(bf16[134,3,128]{2,1,0:T(4,128)(2,1)S(1)} %pad_maximum_fusion.2), channel_id=1, source_target_pairs={{0,1},{1,2},{2,3},{3,4},{4,5},{5,6},{6,7},{8,9},{9,10},{10,11},{11... | collective-permute-start | bytes 308744 | tf_op jit(solution)/shard_map/ppermute | solution.py:24
  104.7 6.6 %collective-permute-start.7 = (bf16[134,3,128]{2,1,0:T(4,128)(2,1)S(1)}, bf16[134,3,128]{2,1,0:T(4,128)(2,1)S(1)}, u32[]{:S(2)}, u32[]{:S(2)}) collective-permute-start(bf16[134,3,128]{2,1,0:T(4,128)(2,1)S(1)} %pad_maximum_fusion.3), channel_id=1, source_target_pairs={{1,0},{2,1},{3,2},{4,3},{5,4},{6,5},{7,6},{9,8},{10,9},{11,10},{12... | collective-permute-start | bytes 308744 | tf_op jit(solution)/shard_map/ppermute | solution.py:24
  107.8 3.5 %copy-start.1 = (bf16[134,3,128]{2,1,0:T(4,128)(2,1)}, bf16[134,3,128]{2,1,0:T(4,128)(2,1)S(1)}, u32[]{:S(2)}) copy-start(bf16[134,3,128]{2,1,0:T(4,128)(2,1)S(1)} %collective-permute-done.6.left) | copy-start | bytes 308740
  111.3 0.7 copy-start.2
  134.7 0.8 copy-start

commit v4 on v3

--- a/solution.py
+++ b/solution.py
@@ -14,6 +14,7 @@
 PAIRS = 4
 OFF = 8
 GRANT = 58 * 2**20
+VECTOR_ROWS = 8
 LANES = 4
 SHARE = 16
 
@@ -210,12 +211,14 @@
     for q in range(2):
         cell_ref[pl.ds(q, count, stride=2), :] = d_conv[q * count : (q + 1) * count]
     dconv_ref[...] = cell_ref[...].astype(jnp.bfloat16)
-    following = jnp.minimum(step + 1, pl.num_programs(0) - 1)
-    conv = conv_pairs(pair_ref, w_ref, following * block_rows, block_rows, half)
-    taps = tap_sums(pad_ref, cell_ref, step * block_rows, block_rows, cols)
-    conv_ref[...] = conv
-    for (a, b), value in taps.items():
-        dkern_ref[a, b] += value
+    @pl.when(step < pl.num_programs(0))
+    def _():
+        following = jnp.minimum(step + 1, pl.num_programs(0) - 1)
+        taps = tap_sums(pad_ref, cell_ref, step * block_rows, block_rows, cols)
+        conv = conv_pairs(pair_ref, w_ref, following * block_rows, block_rows, half)
+        conv_ref[...] = conv
+        for (a, b), value in taps.items():
+            dkern_ref[a, b] += value
 
 
 def layer(x, sides, cotangent, kernel, kbias, gain, shift, wup, bup, wdown, scale):
@@ -290,23 +293,64 @@
     )(*sums)
 
 
+def conv_rows(pad_ref, tap_ref, row0, row_count, cols):
+    out = {}
+    for s in range(0, cols, 8):
+        sums = [jnp.zeros((8, 128), jnp.float32) for _ in range(row_count)]
+        for b in range(TAPS):
+            taps = [tap_ref[(TAPS - 1 - a) * TAPS + TAPS - 1 - b] for a in range(TAPS)]
+            for reached in range(row_count + TAPS - 1):
+                start = OFF - REACH + b + s
+                cells = pad_ref[row0 + reached, start : start + 8, :]
+                for a in range(TAPS):
+                    if 0 <= reached - a < row_count:
+                        sums[reached - a] = sums[reached - a] + cells * taps[a]
+        for r in range(row_count):
+            out[r, s] = sums[r]
+    return out
+
+
 def spread_kernel(
-    block_rows, own, top, bottom, left, right, cot_ref, kern_ref, out_ref, pad_ref, pair_ref, w_ref, cell_ref
+    block_rows,
+    own,
+    top,
+    bottom,
+    left,
+    right,
+    cot_ref,
+    kern_ref,
+    out_ref,
+    pad_ref,
+    pair_ref,
+    w_ref,
+    tap_ref,
+    cell_ref,
 ):
     step = pl.program_id(0)
-    half = own.shape[1] // 2
-    count = block_rows * half
+    cols = own.shape[1]
+    half = cols // 2
+    upper = block_rows - VECTOR_ROWS
+    count = upper * half
 
     @pl.when(step == 0)
     def _():
         fill_weights(kern_ref, w_ref, True)
         fill_padded(own, top, bottom, left, right, pad_ref)
         fill_pairs(pad_ref, pair_ref)
-
-    conv = conv_pairs(pair_ref, w_ref, step * block_rows, block_rows, half)
-    for q in range(2):
-        cell_ref[pl.ds(q, count, stride=2), :] = conv[:, q * 128 : q * 128 + 128]
-    out_ref[...] = (cell_ref[...] + cot_ref[...].astype(jnp.float32)).astype(jnp.bfloat16)
+        for a in range(TAPS):
+            for b in range(TAPS):
+                tap_ref[a * TAPS + b] = jnp.broadcast_to(kern_ref[a, b : b + 1, :], (8, 128))
+
+    @pl.when(step < pl.num_programs(0))
+    def _():
+        rows = conv_rows(pad_ref, tap_ref, step * block_rows + upper, VECTOR_ROWS, cols)
+        conv = conv_pairs(pair_ref, w_ref, step * block_rows, upper, half)
+        for q in range(2):
+            cell_ref[pl.ds(q, count, stride=2), :] = conv[:, q * 128 : q * 128 + 128]
+        for (r, s), value in rows.items():
+            at = (upper + r) * cols + s
+            cell_ref[at : at + 8, :] = value
+        out_ref[...] = (cell_ref[...] + cot_ref[...].astype(jnp.float32)).astype(jnp.bfloat16)
 
 
 def spread(dconv, sides, cotangent, kernel):
@@ -326,6 +370,7 @@
             pltpu.VMEM((padded, cols + 2 * OFF, width), jnp.float32),
             pltpu.VMEM((PAIRS, padded * cols // 2, 2 * width), jnp.bfloat16),
             pltpu.VMEM((TAPS * PAIRS * 2 * width, 2 * width), jnp.bfloat16),
+            pltpu.VMEM((TAPS * TAPS, 8, width), jnp.float32),
             pltpu.VMEM((block, width), jnp.float32),
         ],
         compiler_params=pltpu.CompilerParams(vmem_limit_bytes=GRANT),

time: 138 us -> 127 us (0.920)
  Pallas kernels: 75.6 us -> 64.6 us
    pallas_call x1, Pallas kernels: 22.7 us -> 15.2 us  [spread(): pl.pallas_call(functools.partial(spread_kernel, block_rows), grid=(rows /...]
    pallas_call x1, Pallas kernels: 48.4 us -> 44.9 us  [layer(): pl.pallas_call(functools.partial(layer_kernel, block_rows), grid=(rows //...]
  transfers between devices with their start and end apart: 10 -> 10, of which waited for: 6 -> 6; matrix products, arithmetic and copies ran while one was open for 3% -> 4% of each run, Pallas kernels for 16% -> 12%
where the time goes in v4:
time: 127 us
  Pallas kernels  64.6 us (51%)
  starting transfers between devices  33.6 us (26%)
  waiting for transfers between devices  20.2 us (16%)
  local copies, waits for them, and re-layouts  6.99 us (6%)
    pallas_call x1, Pallas kernels, layer(): pl.pallas_call(functools.partial(layer_kernel, block_rows), grid=(rows //...  44.9 us
    ppermute x8, starting transfers between devices, shifted(): return lax.ppermute(cells, axis, pairs)  25.3 us
    ppermute x8, waiting for transfers between devices, shifted(): return lax.ppermute(cells, axis, pairs)  16.4 us
    pallas_call x1, Pallas kernels, spread(): pl.pallas_call(functools.partial(spread_kernel, block_rows), grid=(rows /...  15.2 us
    all_to_all x1, starting transfers between devices, total(): return lax.all_to_all(copies, axes, split_axis=0, concat_axis=0, tiled=True)  4.6 us
    all_to_all x1, waiting for transfers between devices, total(): share = lax.all_to_all(parts, axes, split_axis=0, concat_axis=0, tiled=True)  3.77 us
    all_to_all x1, starting transfers between devices, total(): share = lax.all_to_all(parts, axes, split_axis=0, concat_axis=0, tiled=True)  3.71 us
  transfers between devices with their start and end apart: 10, of which 6 were waited for; matrix products, arithmetic and copies ran while one was open for 4% of the time, Pallas kernels for 12%

profile of v4, /device:TPU:1, one launch (start us, length us, event | category | flops | bytes accessed | tf_op | source)
XLA Modules:
  0.0 126.7 jit_solution(1136657705527723643)
XLA Ops:
  0.6 0.8 fusion.3
  1.5 7.1 %collective-permute-start.1 = (bf16[3,64,128]{2,1,0:T(8,128)(2,1)S(1)}, bf16[3,64,128]{2,1,0:T(8,128)(2,1)S(1)}, u32[]{:S(2)}, u32[]{:S(2)}) collective-permute-start(bf16[3,64,128]{2,1,0:T(8,128)(2,1)S(1)} %get-tuple-element.46), channel_id=1, source_target_pairs={{0,120},{8,0},{16,8},{24,16},{32,24},{40,32},{48,40},{56,48},{64,5... | collective-permute-start | bytes 147464 | tf_op jit(solution)/shard_map/ppermute | solution.py:25
  8.6 1.1 fusion.2
  9.7 5.1 %collective-permute-done.top = bf16[3,64,128]{2,1,0:T(8,128)(2,1)S(1)} collective-permute-done((bf16[3,64,128]{2,1,0:T(8,128)(2,1)S(1)}, bf16[3,64,128]{2,1,0:T(8,128)(2,1)S(1)}, u32[]{:S(2)}, u32[]{:S(2)}) %collective-permute-start) | collective-permute-done | bytes 49184 | tf_op jit(solution)/shard_map/ppermute | solution.py:25
  14.9 5.1 %collective-permute-start.2 = (bf16[134,3,128]{2,1,0:T(4,128)(2,1)S(1)}, bf16[134,3,128]{2,1,0:T(4,128)(2,1)S(1)}, u32[]{:S(2)}, u32[]{:S(2)}) collective-permute-start(bf16[134,3,128]{2,1,0:T(4,128)(2,1)S(1)} %pad_maximum_fusion), channel_id=1, source_target_pairs={{0,1},{1,2},{2,3},{3,4},{4,5},{5,6},{6,7},{8,9},{9,10},{10,11},{11... | collective-permute-start | bytes 308744 | tf_op jit(solution)/shard_map/ppermute | solution.py:25
  20.2 1.9 %collective-permute-start.3 = (bf16[134,3,128]{2,1,0:T(4,128)(2,1)S(1)}, bf16[134,3,128]{2,1,0:T(4,128)(2,1)S(1)}, u32[]{:S(2)}, u32[]{:S(2)}) collective-permute-start(bf16[134,3,128]{2,1,0:T(4,128)(2,1)S(1)} %pad_maximum_fusion.1), channel_id=1, source_target_pairs={{1,0},{2,1},{3,2},{4,3},{5,4},{6,5},{7,6},{9,8},{10,9},{11,10},{12... | collective-permute-start | bytes 308744 | tf_op jit(solution)/shard_map/ppermute | solution.py:25
  22.1 4.4 %collective-permute-done.3.right = bf16[134,3,128]{2,1,0:T(4,128)(2,1)S(1)} collective-permute-done((bf16[134,3,128]{2,1,0:T(4,128)(2,1)S(1)}, bf16[134,3,128]{2,1,0:T(4,128)(2,1)S(1)}, u32[]{:S(2)}, u32[]{:S(2)}) %collective-permute-start.3) | collective-permute-done | bytes 102944 | tf_op jit(solution)/shard_map/ppermute | solution.py:25
  27.2 44.9 %layer.1 = (bf16[8192,128]{1,0:T(8,128)(2,1)}, f32[128,512]{1,0:T(8,128)}, f32[128,512]{1,0:T(8,128)}, f32[4,8,128]{2,1,0:T(8,128)}, f32[8,512]{1,0:T(8,128)}, /*index=5*/f32[7,7,8,128]{3,2,1,0:T(8,128)}) custom-call(bf16[128,64,128]{2,1,0:T(8,128)(2,1)} %own.1, bf16[3,64,128]{2,1,0:T(8,128)(2,1)} %copy-done.8, bf16[3,64,128]{2,1,0:T(8,128)(2,1)} %copy-done.7, ...), custom_call_target="tpu_custom_call" | custom-call | tf_op jit(solution)/shard_map/layer/pallas_call | solution.py:236
  72.1 2.3 %shares.1 = bf16[2048,128]{1,0:T(8,128)(2,1)} custom-call(f32[128,512]{1,0:T(8,128)} %get-tuple-element.26.dwup_ref, f32[128,512]{1,0:T(8,128)} %get-tuple-element.27.dgt_ref, f32[4,8,128]{2,1,0:T(8,128)} %get-tuple-element.28.sums_ref, f32[8,512]{1,0:T(8,128)} %get-tuple-element.29.dbup_ref, f32[7,7,8,128]{3,2,1,0:T(8,128)} %get-tuple-element.30.dkern_ref), custom_call_target="tpu_custom_call" | custom-call | tf_op jit(solution)/shard_map/shares/pallas_call | solution.py:288
  74.4 3.7 %all-to-all-start = ((bf16[128,16,128]{2,1,0:T(8,128)(2,1)}), bf16[128,16,128]{2,1,0:T(8,128)(2,1)S(1)}, u32[]{:S(2)}, u32[]{:S(2)}) async-start(bf16[128,16,128]{2,1,0:T(8,128)(2,1)} %bitcast.25), calls=%async_computation | async-start | bytes 1048576 | tf_op jit(solution)/shard_map/all_to_all | solution.py:383
  78.2 0.8 fusion.1
  79.0 1.5 %collective-permute-start.4 = (bf16[3,64,128]{2,1,0:T(8,128)(2,1)S(1)}, bf16[3,64,128]{2,1,0:T(8,128)(2,1)S(1)}, u32[]{:S(2)}, u32[]{:S(2)}) collective-permute-start(bf16[3,64,128]{2,1,0:T(8,128)(2,1)S(1)} %bitcast.27), channel_id=1, source_target_pairs={{0,8},{8,16},{16,24},{24,32},{32,40},{40,48},{48,56},{56,64},{64,7... | collective-permute-start | bytes 147464 | tf_op jit(solution)/shard_map/ppermute | solution.py:25
  80.5 4.1 %collective-permute-start.5 = (bf16[3,64,128]{2,1,0:T(8,128)(2,1)S(1)}, bf16[3,64,128]{2,1,0:T(8,128)(2,1)S(1)}, u32[]{:S(2)}, u32[]{:S(2)}) collective-permute-start(bf16[3,64,128]{2,1,0:T(8,128)(2,1)S(1)} %bitcast.26), channel_id=1, source_target_pairs={{0,120},{8,0},{16,8},{24,16},{32,24},{40,32},{48,40},{56,48},{64,5... | collective-permute-start | bytes 147464 | tf_op jit(solution)/shard_map/ppermute | solution.py:25
  84.7 1.1 fusion
  85.8 2.2 %collective-permute-done.4.top = bf16[3,64,128]{2,1,0:T(8,128)(2,1)S(1)} collective-permute-done((bf16[3,64,128]{2,1,0:T(8,128)(2,1)S(1)}, bf16[3,64,128]{2,1,0:T(8,128)(2,1)S(1)}, u32[]{:S(2)}, u32[]{:S(2)}) %collective-permute-start.4) | collective-permute-done | bytes 49184 | tf_op jit(solution)/shard_map/ppermute | solution.py:25
  88.0 3.8 %all-to-all-done = bf16[128,16,128]{2,1,0:T(8,128)(2,1)S(1)} async-done(((bf16[128,16,128]{2,1,0:T(8,128)(2,1)}), bf16[128,16,128]{2,1,0:T(8,128)(2,1)S(1)}, u32[]{:S(2)}, u32[]{:S(2)}) %all-to-all-start) | async-done | bytes 524320 | tf_op jit(solution)/shard_map/all_to_all | solution.py:383
  91.9 0.9 broadcast_in_dim.2
  92.8 4.6 %all-to-all-start.1 = ((bf16[128,16,128]{2,1,0:T(8,128)(2,1)}), bf16[128,16,128]{2,1,0:T(8,128)(2,1)S(1)}, u32[]{:S(2)}, u32[]{:S(2)}) async-start(bf16[128,16,128]{2,1,0:T(8,128)(2,1)} %broadcast_in_dim.2), calls=%async_computation.1 | async-start | bytes 1048576 | tf_op jit(solution)/shard_map/all_to_all | solution.py:386
  97.5 3.5 %collective-permute-start.6 = (bf16[134,3,128]{2,1,0:T(4,128)(2,1)S(1)}, bf16[134,3,128]{2,1,0:T(4,128)(2,1)S(1)}, u32[]{:S(2)}, u32[]{:S(2)}) collective-permute-start(bf16[134,3,128]{2,1,0:T(4,128)(2,1)S(1)} %pad_maximum_fusion.2), channel_id=1, source_target_pairs={{0,1},{1,2},{2,3},{3,4},{4,5},{5,6},{6,7},{8,9},{9,10},{10,11},{11... | collective-permute-start | bytes 308744 | tf_op jit(solution)/shard_map/ppermute | solution.py:25
  101.2 1.9 %collective-permute-start.7 = (bf16[134,3,128]{2,1,0:T(4,128)(2,1)S(1)}, bf16[134,3,128]{2,1,0:T(4,128)(2,1)S(1)}, u32[]{:S(2)}, u32[]{:S(2)}) collective-permute-start(bf16[134,3,128]{2,1,0:T(4,128)(2,1)S(1)} %pad_maximum_fusion.3), channel_id=1, source_target_pairs={{1,0},{2,1},{3,2},{4,3},{5,4},{6,5},{7,6},{9,8},{10,9},{11,10},{12... | collective-permute-start | bytes 308744 | tf_op jit(solution)/shard_map/ppermute | solution.py:25
  103.1 1.2 collective-permute-done.6.left
  104.3 3.5 %collective-permute-done.7.right = bf16[134,3,128]{2,1,0:T(4,128)(2,1)S(1)} collective-permute-done((bf16[134,3,128]{2,1,0:T(4,128)(2,1)S(1)}, bf16[134,3,128]{2,1,0:T(4,128)(2,1)S(1)}, u32[]{:S(2)}, u32[]{:S(2)}) %collective-permute-start.7) | collective-permute-done | bytes 102944 | tf_op jit(solution)/shard_map/ppermute | solution.py:25
  108.5 15.2 %spread.1 = bf16[8192,128]{1,0:T(8,128)(2,1)} custom-call(bf16[128,64,128]{2,1,0:T(8,128)(2,1)} %bitcast.22, bf16[3,64,128]{2,1,0:T(8,128)(2,1)} %copy-done.5, bf16[3,64,128]{2,1,0:T(8,128)(2,1)} %copy-done.6, bf16[134,3,128]{2,1,0:T(4,128)(2,1)} %copy-done.1, bf16[134,3,128]{2,1,0:T(4,128)(2,1)} %copy-done.2, bf16[8192,128]{1,0:T(8,128)(2,1)} %bitcast.20, ...), custom_call_target="tpu_custom_call" | custom-call | tf_op jit(solution)/shard_map/spread/pallas_call | solution.py:363
  124.5 2.2 %finish.1 = (f32[7,7,128]{2,1,0:T(8,128)}, f32[1,128]{1,0:T(1,128)}, f32[1,128]{1,0:T(1,128)}, f32[1,128]{1,0:T(1,128)}, f32[128,512]{1,0:T(8,128)}, /*index=5*/...) custom-call(bf16[2048,128]{1,0:T(8,128)(2,1)} %bitcast.23, bf16[512,128]{1,0:T(8,128)(2,1)} %wdown_ref.3, ...), custom_call_target="tpu_custom_call" | custom-call | tf_op jit(solution)/shard_map/finish/pallas_call | solution.py:439
  (32 shorter events, 2.8 us)
Async XLA Ops:
  1.5 8.3 %collective-permute-start.1 = (bf16[3,64,128]{2,1,0:T(8,128)(2,1)S(1)}, bf16[3,64,128]{2,1,0:T(8,128)(2,1)S(1)}, u32[]{:S(2)}, u32[]{:S(2)}) collective-permute-start(bf16[3,64,128]{2,1,0:T(8,128)(2,1)S(1)} %get-tuple-element.46), channel_id=1, source_target_pairs={{0,120},{8,0},{16,8},{24,16},{32,24},{40,32},{48,40},{56,48},{64,5... | collective-permute-start | bytes 147464 | tf_op jit(solution)/shard_map/ppermute | solution.py:25
  8.6 6.3 %collective-permute-start = (bf16[3,64,128]{2,1,0:T(8,128)(2,1)S(1)}, bf16[3,64,128]{2,1,0:T(8,128)(2,1)S(1)}, u32[]{:S(2)}, u32[]{:S(2)}) collective-permute-start(bf16[3,64,128]{2,1,0:T(8,128)(2,1)S(1)} %get-tuple-element.47), channel_id=1, source_target_pairs={{0,8},{8,16},{16,24},{24,32},{32,40},{40,48},{48,56},{56,64},{64,7... | collective-permute-start | bytes 147464 | tf_op jit(solution)/shard_map/ppermute | solution.py:25
  9.7 16.8 %copy-start.7 = (bf16[3,64,128]{2,1,0:T(8,128)(2,1)}, bf16[3,64,128]{2,1,0:T(8,128)(2,1)S(1)}, u32[]{:S(2)}) copy-start(bf16[3,64,128]{2,1,0:T(8,128)(2,1)S(1)} %collective-permute-done.1.bottom) | copy-start | bytes 147460
  14.8 11.7 %copy-start.8 = (bf16[3,64,128]{2,1,0:T(8,128)(2,1)}, bf16[3,64,128]{2,1,0:T(8,128)(2,1)S(1)}, u32[]{:S(2)}) copy-start(bf16[3,64,128]{2,1,0:T(8,128)(2,1)S(1)} %collective-permute-done.top) | copy-start | bytes 147460
  14.9 7.2 %collective-permute-start.2 = (bf16[134,3,128]{2,1,0:T(4,128)(2,1)S(1)}, bf16[134,3,128]{2,1,0:T(4,128)(2,1)S(1)}, u32[]{:S(2)}, u32[]{:S(2)}) collective-permute-start(bf16[134,3,128]{2,1,0:T(4,128)(2,1)S(1)} %pad_maximum_fusion), channel_id=1, source_target_pairs={{0,1},{1,2},{2,3},{3,4},{4,5},{5,6},{6,7},{8,9},{9,10},{10,11},{11... | collective-permute-start | bytes 308744 | tf_op jit(solution)/shard_map/ppermute | solution.py:25
  20.2 6.4 %collective-permute-start.3 = (bf16[134,3,128]{2,1,0:T(4,128)(2,1)S(1)}, bf16[134,3,128]{2,1,0:T(4,128)(2,1)S(1)}, u32[]{:S(2)}, u32[]{:S(2)}) collective-permute-start(bf16[134,3,128]{2,1,0:T(4,128)(2,1)S(1)} %pad_maximum_fusion.1), channel_id=1, source_target_pairs={{1,0},{2,1},{3,2},{4,3},{5,4},{6,5},{7,6},{9,8},{10,9},{11,10},{12... | collective-permute-start | bytes 308744 | tf_op jit(solution)/shard_map/ppermute | solution.py:25
  22.1 4.4 %copy-start.3 = (bf16[134,3,128]{2,1,0:T(4,128)(2,1)}, bf16[134,3,128]{2,1,0:T(4,128)(2,1)S(1)}, u32[]{:S(2)}) copy-start(bf16[134,3,128]{2,1,0:T(4,128)(2,1)S(1)} %collective-permute-done.2.left) | copy-start | bytes 308740
  26.5 0.7 copy-start.4
  74.4 17.3 %all-to-all-start = ((bf16[128,16,128]{2,1,0:T(8,128)(2,1)}), bf16[128,16,128]{2,1,0:T(8,128)(2,1)S(1)}, u32[]{:S(2)}, u32[]{:S(2)}) async-start(bf16[128,16,128]{2,1,0:T(8,128)(2,1)} %bitcast.25), calls=%async_computation | async-start | bytes 1048576 | tf_op jit(solution)/shard_map/all_to_all | solution.py:383
  79.0 9.0 %collective-permute-start.4 = (bf16[3,64,128]{2,1,0:T(8,128)(2,1)S(1)}, bf16[3,64,128]{2,1,0:T(8,128)(2,1)S(1)}, u32[]{:S(2)}, u32[]{:S(2)}) collective-permute-start(bf16[3,64,128]{2,1,0:T(8,128)(2,1)S(1)} %bitcast.27), channel_id=1, source_target_pairs={{0,8},{8,16},{16,24},{24,32},{32,40},{40,48},{48,56},{56,64},{64,7... | collective-permute-start | bytes 147464 | tf_op jit(solution)/shard_map/ppermute | solution.py:25
  80.5 16.9 %collective-permute-start.5 = (bf16[3,64,128]{2,1,0:T(8,128)(2,1)S(1)}, bf16[3,64,128]{2,1,0:T(8,128)(2,1)S(1)}, u32[]{:S(2)}, u32[]{:S(2)}) collective-permute-start(bf16[3,64,128]{2,1,0:T(8,128)(2,1)S(1)} %bitcast.26), channel_id=1, source_target_pairs={{0,120},{8,0},{16,8},{24,16},{32,24},{40,32},{48,40},{56,48},{64,5... | collective-permute-start | bytes 147464 | tf_op jit(solution)/shard_map/ppermute | solution.py:25
  88.0 19.9 %copy-start.5 = (bf16[3,64,128]{2,1,0:T(8,128)(2,1)}, bf16[3,64,128]{2,1,0:T(8,128)(2,1)S(1)}, u32[]{:S(2)}) copy-start(bf16[3,64,128]{2,1,0:T(8,128)(2,1)S(1)} %collective-permute-done.4.top) | copy-start | bytes 147460
  92.8 30.9 %all-to-all-start.1 = ((bf16[128,16,128]{2,1,0:T(8,128)(2,1)}), bf16[128,16,128]{2,1,0:T(8,128)(2,1)S(1)}, u32[]{:S(2)}, u32[]{:S(2)}) async-start(bf16[128,16,128]{2,1,0:T(8,128)(2,1)} %broadcast_in_dim.2), calls=%async_computation.1 | async-start | bytes 1048576 | tf_op jit(solution)/shard_map/all_to_all | solution.py:386
  97.4 10.4 %copy-start.6 = (bf16[3,64,128]{2,1,0:T(8,128)(2,1)}, bf16[3,64,128]{2,1,0:T(8,128)(2,1)S(1)}, u32[]{:S(2)}) copy-start(bf16[3,64,128]{2,1,0:T(8,128)(2,1)S(1)} %collective-permute-done.5.bottom) | copy-start | bytes 147460
  97.5 6.8 %collective-permute-start.6 = (bf16[134,3,128]{2,1,0:T(4,128)(2,1)S(1)}, bf16[134,3,128]{2,1,0:T(4,128)(2,1)S(1)}, u32[]{:S(2)}, u32[]{:S(2)}) collective-permute-start(bf16[134,3,128]{2,1,0:T(4,128)(2,1)S(1)} %pad_maximum_fusion.2), channel_id=1, source_target_pairs={{0,1},{1,2},{2,3},{3,4},{4,5},{5,6},{6,7},{8,9},{9,10},{10,11},{11... | collective-permute-start | bytes 308744 | tf_op jit(solution)/shard_map/ppermute | solution.py:25
  101.2 6.6 %collective-permute-start.7 = (bf16[134,3,128]{2,1,0:T(4,128)(2,1)S(1)}, bf16[134,3,128]{2,1,0:T(4,128)(2,1)S(1)}, u32[]{:S(2)}, u32[]{:S(2)}) collective-permute-start(bf16[134,3,128]{2,1,0:T(4,128)(2,1)S(1)} %pad_maximum_fusion.3), channel_id=1, source_target_pairs={{1,0},{2,1},{3,2},{4,3},{5,4},{6,5},{7,6},{9,8},{10,9},{11,10},{12... | collective-permute-start | bytes 308744 | tf_op jit(solution)/shard_map/ppermute | solution.py:25
  104.3 3.5 %copy-start.1 = (bf16[134,3,128]{2,1,0:T(4,128)(2,1)}, bf16[134,3,128]{2,1,0:T(4,128)(2,1)S(1)}, u32[]{:S(2)}) copy-start(bf16[134,3,128]{2,1,0:T(4,128)(2,1)S(1)} %collective-permute-done.6.left) | copy-start | bytes 308740
  107.9 0.7 copy-start.2
  123.7 0.8 copy-start

commit v5 on v4

--- a/solution.py
+++ b/solution.py
@@ -7,6 +7,7 @@
 from jax.experimental import pallas as pl
 from jax.experimental.pallas import tpu as pltpu
 from jax.sharding import PartitionSpec as P
+
 
 EPSILON = 1e-06
 REACH = 3
@@ -34,8 +35,9 @@
         cut = [part[:, start : start + REACH] for part in (top, cells, bottom)]
         return jnp.concatenate(cut, axis=0)
 
-    left = shifted(edge(cols - REACH), "gy", 1, False)
-    right = shifted(edge(0), "gy", -1, False)
+    ends = edge(cols - REACH), edge(0)
+    left = shifted(ends[0], "gy", 1, False)
+    right = shifted(ends[1], "gy", -1, False)
     return top, bottom, left, right
 
 
@@ -211,6 +213,7 @@
     for q in range(2):
         cell_ref[pl.ds(q, count, stride=2), :] = d_conv[q * count : (q + 1) * count]
     dconv_ref[...] = cell_ref[...].astype(jnp.bfloat16)
+
     @pl.when(step < pl.num_programs(0))
     def _():
         following = jnp.minimum(step + 1, pl.num_programs(0) - 1)
@@ -464,7 +467,8 @@
     )
     dconv = dconv.reshape(rows, cols, width)
     d_features = spread(dconv, halo(dconv), cotangent, kernel)
-    summed = total(shares(*sums).reshape(devices, SHARE, width)).reshape(devices * SHARE, width)
+    parts = shares(*sums)
+    summed = total(parts.reshape(devices, SHARE, width)).reshape(devices * SHARE, width)
     factor = 1.0 / math.sqrt(rows * cols * devices)
     grads = finish(summed, w_down, b_down, layer_scale, factor)
     return (d_features,) + tuple(g.reshape(-1) if g.shape[0] == 1 else g for g in grads)

time: 127 us -> 127 us (level)
  no operation moved by 1% of the time
where the time goes in v5:
time: 127 us
  Pallas kernels  64.6 us (51%)
  starting transfers between devices  33.6 us (26%)
  waiting for transfers between devices  20.2 us (16%)
  local copies, waits for them, and re-layouts  6.99 us (6%)
    pallas_call x1, Pallas kernels, layer(): pl.pallas_call(functools.partial(layer_kernel, block_rows), grid=(rows //...  44.9 us
    ppermute x8, starting transfers between devices, shifted(): return lax.ppermute(cells, axis, pairs)  25.3 us
    ppermute x8, waiting for transfers between devices, shifted(): return lax.ppermute(cells, axis, pairs)  16.4 us
    pallas_call x1, Pallas kernels, spread(): pl.pallas_call(functools.partial(spread_kernel, block_rows), grid=(rows /...  15.2 us
    all_to_all x1, starting transfers between devices, total(): return lax.all_to_all(copies, axes, split_axis=0, concat_axis=0, tiled=True)  4.6 us
    all_to_all x1, waiting for transfers between devices, total(): share = lax.all_to_all(parts, axes, split_axis=0, concat_axis=0, tiled=True)  3.77 us
    all_to_all x1, starting transfers between devices, total(): share = lax.all_to_all(parts, axes, split_axis=0, concat_axis=0, tiled=True)  3.71 us
  transfers between devices with their start and end apart: 10, of which 6 were waited for; matrix products, arithmetic and copies ran while one was open for 4% of the time, Pallas kernels for 12%

profile of v5, /device:TPU:1, one launch (start us, length us, event | category | flops | bytes accessed | tf_op | source)
XLA Modules:
  0.0 126.7 jit_solution(1136657705527723643)
XLA Ops:
  0.6 0.8 fusion.3
  1.5 7.1 %collective-permute-start.1 = (bf16[3,64,128]{2,1,0:T(8,128)(2,1)S(1)}, bf16[3,64,128]{2,1,0:T(8,128)(2,1)S(1)}, u32[]{:S(2)}, u32[]{:S(2)}) collective-permute-start(bf16[3,64,128]{2,1,0:T(8,128)(2,1)S(1)} %get-tuple-element.46), channel_id=1, source_target_pairs={{0,120},{8,0},{16,8},{24,16},{32,24},{40,32},{48,40},{56,48},{64,5... | collective-permute-start | bytes 147464 | tf_op jit(solution)/shard_map/ppermute | solution.py:26
  8.6 1.1 fusion.2
  9.7 5.1 %collective-permute-done.top = bf16[3,64,128]{2,1,0:T(8,128)(2,1)S(1)} collective-permute-done((bf16[3,64,128]{2,1,0:T(8,128)(2,1)S(1)}, bf16[3,64,128]{2,1,0:T(8,128)(2,1)S(1)}, u32[]{:S(2)}, u32[]{:S(2)}) %collective-permute-start) | collective-permute-done | bytes 49184 | tf_op jit(solution)/shard_map/ppermute | solution.py:26
  14.9 5.1 %collective-permute-start.2 = (bf16[134,3,128]{2,1,0:T(4,128)(2,1)S(1)}, bf16[134,3,128]{2,1,0:T(4,128)(2,1)S(1)}, u32[]{:S(2)}, u32[]{:S(2)}) collective-permute-start(bf16[134,3,128]{2,1,0:T(4,128)(2,1)S(1)} %pad_maximum_fusion), channel_id=1, source_target_pairs={{0,1},{1,2},{2,3},{3,4},{4,5},{5,6},{6,7},{8,9},{9,10},{10,11},{11... | collective-permute-start | bytes 308744 | tf_op jit(solution)/shard_map/ppermute | solution.py:26
  20.2 1.9 %collective-permute-start.3 = (bf16[134,3,128]{2,1,0:T(4,128)(2,1)S(1)}, bf16[134,3,128]{2,1,0:T(4,128)(2,1)S(1)}, u32[]{:S(2)}, u32[]{:S(2)}) collective-permute-start(bf16[134,3,128]{2,1,0:T(4,128)(2,1)S(1)} %pad_maximum_fusion.1), channel_id=1, source_target_pairs={{1,0},{2,1},{3,2},{4,3},{5,4},{6,5},{7,6},{9,8},{10,9},{11,10},{12... | collective-permute-start | bytes 308744 | tf_op jit(solution)/shard_map/ppermute | solution.py:26
  22.1 4.4 %collective-permute-done.3.right = bf16[134,3,128]{2,1,0:T(4,128)(2,1)S(1)} collective-permute-done((bf16[134,3,128]{2,1,0:T(4,128)(2,1)S(1)}, bf16[134,3,128]{2,1,0:T(4,128)(2,1)S(1)}, u32[]{:S(2)}, u32[]{:S(2)}) %collective-permute-start.3) | collective-permute-done | bytes 102944 | tf_op jit(solution)/shard_map/ppermute | solution.py:26
  27.2 44.9 %layer.1 = (bf16[8192,128]{1,0:T(8,128)(2,1)}, f32[128,512]{1,0:T(8,128)}, f32[128,512]{1,0:T(8,128)}, f32[4,8,128]{2,1,0:T(8,128)}, f32[8,512]{1,0:T(8,128)}, /*index=5*/f32[7,7,8,128]{3,2,1,0:T(8,128)}) custom-call(bf16[128,64,128]{2,1,0:T(8,128)(2,1)} %own.1, bf16[3,64,128]{2,1,0:T(8,128)(2,1)} %copy-done.8, bf16[3,64,128]{2,1,0:T(8,128)(2,1)} %copy-done.7, ...), custom_call_target="tpu_custom_call" | custom-call | tf_op jit(solution)/shard_map/layer/pallas_call | solution.py:239
  72.1 2.3 %shares.1 = bf16[2048,128]{1,0:T(8,128)(2,1)} custom-call(f32[128,512]{1,0:T(8,128)} %get-tuple-element.26.dwup_ref, f32[128,512]{1,0:T(8,128)} %get-tuple-element.27.dgt_ref, f32[4,8,128]{2,1,0:T(8,128)} %get-tuple-element.28.sums_ref, f32[8,512]{1,0:T(8,128)} %get-tuple-element.29.dbup_ref, f32[7,7,8,128]{3,2,1,0:T(8,128)} %get-tuple-element.30.dkern_ref), custom_call_target="tpu_custom_call" | custom-call | tf_op jit(solution)/shard_map/shares/pallas_call | solution.py:291
  74.4 3.7 %all-to-all-start = ((bf16[128,16,128]{2,1,0:T(8,128)(2,1)}), bf16[128,16,128]{2,1,0:T(8,128)(2,1)S(1)}, u32[]{:S(2)}, u32[]{:S(2)}) async-start(bf16[128,16,128]{2,1,0:T(8,128)(2,1)} %bitcast.25), calls=%async_computation | async-start | bytes 1048576 | tf_op jit(solution)/shard_map/all_to_all | solution.py:386
  78.2 0.8 fusion.1
  79.0 1.5 %collective-permute-start.4 = (bf16[3,64,128]{2,1,0:T(8,128)(2,1)S(1)}, bf16[3,64,128]{2,1,0:T(8,128)(2,1)S(1)}, u32[]{:S(2)}, u32[]{:S(2)}) collective-permute-start(bf16[3,64,128]{2,1,0:T(8,128)(2,1)S(1)} %bitcast.27), channel_id=1, source_target_pairs={{0,8},{8,16},{16,24},{24,32},{32,40},{40,48},{48,56},{56,64},{64,7... | collective-permute-start | bytes 147464 | tf_op jit(solution)/shard_map/ppermute | solution.py:26
  80.5 4.1 %collective-permute-start.5 = (bf16[3,64,128]{2,1,0:T(8,128)(2,1)S(1)}, bf16[3,64,128]{2,1,0:T(8,128)(2,1)S(1)}, u32[]{:S(2)}, u32[]{:S(2)}) collective-permute-start(bf16[3,64,128]{2,1,0:T(8,128)(2,1)S(1)} %bitcast.26), channel_id=1, source_target_pairs={{0,120},{8,0},{16,8},{24,16},{32,24},{40,32},{48,40},{56,48},{64,5... | collective-permute-start | bytes 147464 | tf_op jit(solution)/shard_map/ppermute | solution.py:26
  84.7 1.1 fusion
  85.8 2.2 %collective-permute-done.4.top = bf16[3,64,128]{2,1,0:T(8,128)(2,1)S(1)} collective-permute-done((bf16[3,64,128]{2,1,0:T(8,128)(2,1)S(1)}, bf16[3,64,128]{2,1,0:T(8,128)(2,1)S(1)}, u32[]{:S(2)}, u32[]{:S(2)}) %collective-permute-start.4) | collective-permute-done | bytes 49184 | tf_op jit(solution)/shard_map/ppermute | solution.py:26
  88.0 3.8 %all-to-all-done = bf16[128,16,128]{2,1,0:T(8,128)(2,1)S(1)} async-done(((bf16[128,16,128]{2,1,0:T(8,128)(2,1)}), bf16[128,16,128]{2,1,0:T(8,128)(2,1)S(1)}, u32[]{:S(2)}, u32[]{:S(2)}) %all-to-all-start) | async-done | bytes 524320 | tf_op jit(solution)/shard_map/all_to_all | solution.py:386
  91.9 0.9 broadcast_in_dim.2
  92.8 4.6 %all-to-all-start.1 = ((bf16[128,16,128]{2,1,0:T(8,128)(2,1)}), bf16[128,16,128]{2,1,0:T(8,128)(2,1)S(1)}, u32[]{:S(2)}, u32[]{:S(2)}) async-start(bf16[128,16,128]{2,1,0:T(8,128)(2,1)} %broadcast_in_dim.2), calls=%async_computation.1 | async-start | bytes 1048576 | tf_op jit(solution)/shard_map/all_to_all | solution.py:389
  97.5 3.5 %collective-permute-start.6 = (bf16[134,3,128]{2,1,0:T(4,128)(2,1)S(1)}, bf16[134,3,128]{2,1,0:T(4,128)(2,1)S(1)}, u32[]{:S(2)}, u32[]{:S(2)}) collective-permute-start(bf16[134,3,128]{2,1,0:T(4,128)(2,1)S(1)} %pad_maximum_fusion.2), channel_id=1, source_target_pairs={{0,1},{1,2},{2,3},{3,4},{4,5},{5,6},{6,7},{8,9},{9,10},{10,11},{11... | collective-permute-start | bytes 308744 | tf_op jit(solution)/shard_map/ppermute | solution.py:26
  101.2 1.9 %collective-permute-start.7 = (bf16[134,3,128]{2,1,0:T(4,128)(2,1)S(1)}, bf16[134,3,128]{2,1,0:T(4,128)(2,1)S(1)}, u32[]{:S(2)}, u32[]{:S(2)}) collective-permute-start(bf16[134,3,128]{2,1,0:T(4,128)(2,1)S(1)} %pad_maximum_fusion.3), channel_id=1, source_target_pairs={{1,0},{2,1},{3,2},{4,3},{5,4},{6,5},{7,6},{9,8},{10,9},{11,10},{12... | collective-permute-start | bytes 308744 | tf_op jit(solution)/shard_map/ppermute | solution.py:26
  103.1 1.2 collective-permute-done.6.left
  104.3 3.5 %collective-permute-done.7.right = bf16[134,3,128]{2,1,0:T(4,128)(2,1)S(1)} collective-permute-done((bf16[134,3,128]{2,1,0:T(4,128)(2,1)S(1)}, bf16[134,3,128]{2,1,0:T(4,128)(2,1)S(1)}, u32[]{:S(2)}, u32[]{:S(2)}) %collective-permute-start.7) | collective-permute-done | bytes 102944 | tf_op jit(solution)/shard_map/ppermute | solution.py:26
  108.5 15.2 %spread.1 = bf16[8192,128]{1,0:T(8,128)(2,1)} custom-call(bf16[128,64,128]{2,1,0:T(8,128)(2,1)} %bitcast.22, bf16[3,64,128]{2,1,0:T(8,128)(2,1)} %copy-done.5, bf16[3,64,128]{2,1,0:T(8,128)(2,1)} %copy-done.6, bf16[134,3,128]{2,1,0:T(4,128)(2,1)} %copy-done.1, bf16[134,3,128]{2,1,0:T(4,128)(2,1)} %copy-done.2, bf16[8192,128]{1,0:T(8,128)(2,1)} %bitcast.20, ...), custom_call_target="tpu_custom_call" | custom-call | tf_op jit(solution)/shard_map/spread/pallas_call | solution.py:366
  124.5 2.2 %finish.1 = (f32[7,7,128]{2,1,0:T(8,128)}, f32[1,128]{1,0:T(1,128)}, f32[1,128]{1,0:T(1,128)}, f32[1,128]{1,0:T(1,128)}, f32[128,512]{1,0:T(8,128)}, /*index=5*/...) custom-call(bf16[2048,128]{1,0:T(8,128)(2,1)} %bitcast.23, bf16[512,128]{1,0:T(8,128)(2,1)} %wdown_ref.3, ...), custom_call_target="tpu_custom_call" | custom-call | tf_op jit(solution)/shard_map/finish/pallas_call | solution.py:442
  (32 shorter events, 2.8 us)
Async XLA Ops:
  1.5 8.3 %collective-permute-start.1 = (bf16[3,64,128]{2,1,0:T(8,128)(2,1)S(1)}, bf16[3,64,128]{2,1,0:T(8,128)(2,1)S(1)}, u32[]{:S(2)}, u32[]{:S(2)}) collective-permute-start(bf16[3,64,128]{2,1,0:T(8,128)(2,1)S(1)} %get-tuple-element.46), channel_id=1, source_target_pairs={{0,120},{8,0},{16,8},{24,16},{32,24},{40,32},{48,40},{56,48},{64,5... | collective-permute-start | bytes 147464 | tf_op jit(solution)/shard_map/ppermute | solution.py:26
  8.6 6.3 %collective-permute-start = (bf16[3,64,128]{2,1,0:T(8,128)(2,1)S(1)}, bf16[3,64,128]{2,1,0:T(8,128)(2,1)S(1)}, u32[]{:S(2)}, u32[]{:S(2)}) collective-permute-start(bf16[3,64,128]{2,1,0:T(8,128)(2,1)S(1)} %get-tuple-element.47), channel_id=1, source_target_pairs={{0,8},{8,16},{16,24},{24,32},{32,40},{40,48},{48,56},{56,64},{64,7... | collective-permute-start | bytes 147464 | tf_op jit(solution)/shard_map/ppermute | solution.py:26
  9.7 16.8 %copy-start.7 = (bf16[3,64,128]{2,1,0:T(8,128)(2,1)}, bf16[3,64,128]{2,1,0:T(8,128)(2,1)S(1)}, u32[]{:S(2)}) copy-start(bf16[3,64,128]{2,1,0:T(8,128)(2,1)S(1)} %collective-permute-done.1.bottom) | copy-start | bytes 147460
  14.8 11.7 %copy-start.8 = (bf16[3,64,128]{2,1,0:T(8,128)(2,1)}, bf16[3,64,128]{2,1,0:T(8,128)(2,1)S(1)}, u32[]{:S(2)}) copy-start(bf16[3,64,128]{2,1,0:T(8,128)(2,1)S(1)} %collective-permute-done.top) | copy-start | bytes 147460
  14.9 7.2 %collective-permute-start.2 = (bf16[134,3,128]{2,1,0:T(4,128)(2,1)S(1)}, bf16[134,3,128]{2,1,0:T(4,128)(2,1)S(1)}, u32[]{:S(2)}, u32[]{:S(2)}) collective-permute-start(bf16[134,3,128]{2,1,0:T(4,128)(2,1)S(1)} %pad_maximum_fusion), channel_id=1, source_target_pairs={{0,1},{1,2},{2,3},{3,4},{4,5},{5,6},{6,7},{8,9},{9,10},{10,11},{11... | collective-permute-start | bytes 308744 | tf_op jit(solution)/shard_map/ppermute | solution.py:26
  20.2 6.4 %collective-permute-start.3 = (bf16[134,3,128]{2,1,0:T(4,128)(2,1)S(1)}, bf16[134,3,128]{2,1,0:T(4,128)(2,1)S(1)}, u32[]{:S(2)}, u32[]{:S(2)}) collective-permute-start(bf16[134,3,128]{2,1,0:T(4,128)(2,1)S(1)} %pad_maximum_fusion.1), channel_id=1, source_target_pairs={{1,0},{2,1},{3,2},{4,3},{5,4},{6,5},{7,6},{9,8},{10,9},{11,10},{12... | collective-permute-start | bytes 308744 | tf_op jit(solution)/shard_map/ppermute | solution.py:26
  22.1 4.4 %copy-start.3 = (bf16[134,3,128]{2,1,0:T(4,128)(2,1)}, bf16[134,3,128]{2,1,0:T(4,128)(2,1)S(1)}, u32[]{:S(2)}) copy-start(bf16[134,3,128]{2,1,0:T(4,128)(2,1)S(1)} %collective-permute-done.2.left) | copy-start | bytes 308740
  26.5 0.7 copy-start.4
  74.4 17.3 %all-to-all-start = ((bf16[128,16,128]{2,1,0:T(8,128)(2,1)}), bf16[128,16,128]{2,1,0:T(8,128)(2,1)S(1)}, u32[]{:S(2)}, u32[]{:S(2)}) async-start(bf16[128,16,128]{2,1,0:T(8,128)(2,1)} %bitcast.25), calls=%async_computation | async-start | bytes 1048576 | tf_op jit(solution)/shard_map/all_to_all | solution.py:386
  79.0 9.0 %collective-permute-start.4 = (bf16[3,64,128]{2,1,0:T(8,128)(2,1)S(1)}, bf16[3,64,128]{2,1,0:T(8,128)(2,1)S(1)}, u32[]{:S(2)}, u32[]{:S(2)}) collective-permute-start(bf16[3,64,128]{2,1,0:T(8,128)(2,1)S(1)} %bitcast.27), channel_id=1, source_target_pairs={{0,8},{8,16},{16,24},{24,32},{32,40},{40,48},{48,56},{56,64},{64,7... | collective-permute-start | bytes 147464 | tf_op jit(solution)/shard_map/ppermute | solution.py:26
  80.5 16.9 %collective-permute-start.5 = (bf16[3,64,128]{2,1,0:T(8,128)(2,1)S(1)}, bf16[3,64,128]{2,1,0:T(8,128)(2,1)S(1)}, u32[]{:S(2)}, u32[]{:S(2)}) collective-permute-start(bf16[3,64,128]{2,1,0:T(8,128)(2,1)S(1)} %bitcast.26), channel_id=1, source_target_pairs={{0,120},{8,0},{16,8},{24,16},{32,24},{40,32},{48,40},{56,48},{64,5... | collective-permute-start | bytes 147464 | tf_op jit(solution)/shard_map/ppermute | solution.py:26
  88.0 19.9 %copy-start.5 = (bf16[3,64,128]{2,1,0:T(8,128)(2,1)}, bf16[3,64,128]{2,1,0:T(8,128)(2,1)S(1)}, u32[]{:S(2)}) copy-start(bf16[3,64,128]{2,1,0:T(8,128)(2,1)S(1)} %collective-permute-done.4.top) | copy-start | bytes 147460
  92.8 30.9 %all-to-all-start.1 = ((bf16[128,16,128]{2,1,0:T(8,128)(2,1)}), bf16[128,16,128]{2,1,0:T(8,128)(2,1)S(1)}, u32[]{:S(2)}, u32[]{:S(2)}) async-start(bf16[128,16,128]{2,1,0:T(8,128)(2,1)} %broadcast_in_dim.2), calls=%async_computation.1 | async-start | bytes 1048576 | tf_op jit(solution)/shard_map/all_to_all | solution.py:389
  97.4 10.4 %copy-start.6 = (bf16[3,64,128]{2,1,0:T(8,128)(2,1)}, bf16[3,64,128]{2,1,0:T(8,128)(2,1)S(1)}, u32[]{:S(2)}) copy-start(bf16[3,64,128]{2,1,0:T(8,128)(2,1)S(1)} %collective-permute-done.5.bottom) | copy-start | bytes 147460
  97.5 6.8 %collective-permute-start.6 = (bf16[134,3,128]{2,1,0:T(4,128)(2,1)S(1)}, bf16[134,3,128]{2,1,0:T(4,128)(2,1)S(1)}, u32[]{:S(2)}, u32[]{:S(2)}) collective-permute-start(bf16[134,3,128]{2,1,0:T(4,128)(2,1)S(1)} %pad_maximum_fusion.2), channel_id=1, source_target_pairs={{0,1},{1,2},{2,3},{3,4},{4,5},{5,6},{6,7},{8,9},{9,10},{10,11},{11... | collective-permute-start | bytes 308744 | tf_op jit(solution)/shard_map/ppermute | solution.py:26
  101.2 6.6 %collective-permute-start.7 = (bf16[134,3,128]{2,1,0:T(4,128)(2,1)S(1)}, bf16[134,3,128]{2,1,0:T(4,128)(2,1)S(1)}, u32[]{:S(2)}, u32[]{:S(2)}) collective-permute-start(bf16[134,3,128]{2,1,0:T(4,128)(2,1)S(1)} %pad_maximum_fusion.3), channel_id=1, source_target_pairs={{1,0},{2,1},{3,2},{4,3},{5,4},{6,5},{7,6},{9,8},{10,9},{11,10},{12... | collective-permute-start | bytes 308744 | tf_op jit(solution)/shard_map/ppermute | solution.py:26
  104.3 3.5 %copy-start.1 = (bf16[134,3,128]{2,1,0:T(4,128)(2,1)}, bf16[134,3,128]{2,1,0:T(4,128)(2,1)S(1)}, u32[]{:S(2)}) copy-start(bf16[134,3,128]{2,1,0:T(4,128)(2,1)S(1)} %collective-permute-done.6.left) | copy-start | bytes 308740
  107.9 0.7 copy-start.2
  123.7 0.8 copy-start

commit v6 on v5

--- a/solution.py
+++ b/solution.py
@@ -58,7 +58,10 @@
         pad_ref[r, OFF + cols : OFF + cols + REACH, :] = right[r].astype(jnp.float32)
         return carry
 
-    lax.fori_loop(0, rows + 2 * REACH, sides, 0, unroll=2)
+    span = rows + 2 * REACH
+    lax.fori_loop(0, span // 8, lambda i, carry: [sides(8 * i + k, carry) for k in range(8)][0], 0)
+    for r in range(span // 8 * 8, span):
+        sides(r, 0)
 
 
 def fill_pairs(pad_ref, pair_ref):
@@ -74,7 +77,10 @@
                 )
         return carry
 
-    lax.fori_loop(0, pad_ref.shape[0], body, 0, unroll=2)
+    count = pad_ref.shape[0]
+    lax.fori_loop(0, count // 8, lambda i, carry: [body(8 * i + k, carry) for k in range(8)][0], 0)
+    for r in range(count // 8 * 8, count):
+        body(r, 0)
 
 
 def fill_weights(kern_ref, w_ref, flip):
@@ -197,7 +203,8 @@
     cell_ref[...] = cot_ref[...].astype(jnp.float32)
     cot = jnp.concatenate([cell_ref[pl.ds(q, count, stride=2), :] for q in range(2)], axis=0)
     d_output = (cot * scale_ref[...]).astype(jnp.bfloat16)
-    d_hidden = (dot(d_output, wdown_ref[...], ((1,), (1,))) * slope).astype(jnp.bfloat16)
+    d_wide = dot(d_output, wdown_ref[...], ((1,), (1,))) * slope
+    d_hidden = d_wide.astype(jnp.bfloat16)
     d_normal = dot(d_hidden, wup_ref[...], ((1,), (1,)))
     d_normed = d_normal * gain
     first = jnp.mean(d_normed, axis=-1, keepdims=True)
@@ -207,7 +214,7 @@
     sums_ref[1] += fold(d_normal * normed)
     sums_ref[2] += fold(d_normal)
     sums_ref[3] += fold(cot)
-    dbup_ref[...] += fold(d_hidden.astype(jnp.float32))
+    dbup_ref[...] += fold(d_wide)
     dwup_ref[...] += dot(normal, d_hidden, ((0,), (0,)))
     dgt_ref[...] += dot(cot.astype(jnp.bfloat16), active, ((0,), (0,)))
     for q in range(2):

time: 127 us -> 126 us (level)
  no operation moved by 1% of the time
where the time goes in v6:
time: 126 us; the launch traced here: 125 us
  Pallas kernels  63.4 us (50%)
  starting transfers between devices  33.6 us (27%)
  waiting for transfers between devices  20.2 us (16%)
  local copies, waits for them, and re-layouts  6.99 us (6%)
    pallas_call x1, Pallas kernels, layer(): pl.pallas_call(functools.partial(layer_kernel, block_rows), grid=(rows //...  44.1 us
    ppermute x8, starting transfers between devices, shifted(): return lax.ppermute(cells, axis, pairs)  25.3 us
    ppermute x8, waiting for transfers between devices, shifted(): return lax.ppermute(cells, axis, pairs)  16.4 us
    pallas_call x1, Pallas kernels, spread(): pl.pallas_call(functools.partial(spread_kernel, block_rows), grid=(rows /...  14.8 us
    all_to_all x1, starting transfers between devices, total(): return lax.all_to_all(copies, axes, split_axis=0, concat_axis=0, tiled=True)  4.6 us
    all_to_all x1, waiting for transfers between devices, total(): share = lax.all_to_all(parts, axes, split_axis=0, concat_axis=0, tiled=True)  3.77 us
    all_to_all x1, starting transfers between devices, total(): share = lax.all_to_all(parts, axes, split_axis=0, concat_axis=0, tiled=True)  3.71 us
  transfers between devices with their start and end apart: 10, of which 6 were waited for; matrix products, arithmetic and copies ran while one was open for 4% of the time, Pallas kernels for 12%

profile of v6, /device:TPU:1, one launch (start us, length us, event | category | flops | bytes accessed | tf_op | source)
XLA Modules:
  0.0 125.4 jit_solution(15492107260923366581)
XLA Ops:
  0.6 0.8 fusion.3
  1.5 7.1 %collective-permute-start.1 = (bf16[3,64,128]{2,1,0:T(8,128)(2,1)S(1)}, bf16[3,64,128]{2,1,0:T(8,128)(2,1)S(1)}, u32[]{:S(2)}, u32[]{:S(2)}) collective-permute-start(bf16[3,64,128]{2,1,0:T(8,128)(2,1)S(1)} %get-tuple-element.46), channel_id=1, source_target_pairs={{0,120},{8,0},{16,8},{24,16},{32,24},{40,32},{48,40},{56,48},{64,5... | collective-permute-start | bytes 147464 | tf_op jit(solution)/shard_map/ppermute | solution.py:26
  8.6 1.1 fusion.2
  9.7 5.1 %collective-permute-done.top = bf16[3,64,128]{2,1,0:T(8,128)(2,1)S(1)} collective-permute-done((bf16[3,64,128]{2,1,0:T(8,128)(2,1)S(1)}, bf16[3,64,128]{2,1,0:T(8,128)(2,1)S(1)}, u32[]{:S(2)}, u32[]{:S(2)}) %collective-permute-start) | collective-permute-done | bytes 49184 | tf_op jit(solution)/shard_map/ppermute | solution.py:26
  14.9 5.1 %collective-permute-start.2 = (bf16[134,3,128]{2,1,0:T(4,128)(2,1)S(1)}, bf16[134,3,128]{2,1,0:T(4,128)(2,1)S(1)}, u32[]{:S(2)}, u32[]{:S(2)}) collective-permute-start(bf16[134,3,128]{2,1,0:T(4,128)(2,1)S(1)} %pad_maximum_fusion), channel_id=1, source_target_pairs={{0,1},{1,2},{2,3},{3,4},{4,5},{5,6},{6,7},{8,9},{9,10},{10,11},{11... | collective-permute-start | bytes 308744 | tf_op jit(solution)/shard_map/ppermute | solution.py:26
  20.2 1.9 %collective-permute-start.3 = (bf16[134,3,128]{2,1,0:T(4,128)(2,1)S(1)}, bf16[134,3,128]{2,1,0:T(4,128)(2,1)S(1)}, u32[]{:S(2)}, u32[]{:S(2)}) collective-permute-start(bf16[134,3,128]{2,1,0:T(4,128)(2,1)S(1)} %pad_maximum_fusion.1), channel_id=1, source_target_pairs={{1,0},{2,1},{3,2},{4,3},{5,4},{6,5},{7,6},{9,8},{10,9},{11,10},{12... | collective-permute-start | bytes 308744 | tf_op jit(solution)/shard_map/ppermute | solution.py:26
  22.1 4.4 %collective-permute-done.3.right = bf16[134,3,128]{2,1,0:T(4,128)(2,1)S(1)} collective-permute-done((bf16[134,3,128]{2,1,0:T(4,128)(2,1)S(1)}, bf16[134,3,128]{2,1,0:T(4,128)(2,1)S(1)}, u32[]{:S(2)}, u32[]{:S(2)}) %collective-permute-start.3) | collective-permute-done | bytes 102944 | tf_op jit(solution)/shard_map/ppermute | solution.py:26
  27.2 44.1 %layer.1 = (bf16[8192,128]{1,0:T(8,128)(2,1)}, f32[128,512]{1,0:T(8,128)}, f32[128,512]{1,0:T(8,128)}, f32[4,8,128]{2,1,0:T(8,128)}, f32[8,512]{1,0:T(8,128)}, /*index=5*/f32[7,7,8,128]{3,2,1,0:T(8,128)}) custom-call(bf16[128,64,128]{2,1,0:T(8,128)(2,1)} %own.1, bf16[3,64,128]{2,1,0:T(8,128)(2,1)} %copy-done.8, bf16[3,64,128]{2,1,0:T(8,128)(2,1)} %copy-done.7, ...), custom_call_target="tpu_custom_call" | custom-call | tf_op jit(solution)/shard_map/layer/pallas_call | solution.py:246
  71.3 2.3 %shares.1 = bf16[2048,128]{1,0:T(8,128)(2,1)} custom-call(f32[128,512]{1,0:T(8,128)} %get-tuple-element.26.dwup_ref, f32[128,512]{1,0:T(8,128)} %get-tuple-element.27.dgt_ref, f32[4,8,128]{2,1,0:T(8,128)} %get-tuple-element.28.sums_ref, f32[8,512]{1,0:T(8,128)} %get-tuple-element.29.dbup_ref, f32[7,7,8,128]{3,2,1,0:T(8,128)} %get-tuple-element.30.dkern_ref), custom_call_target="tpu_custom_call" | custom-call | tf_op jit(solution)/shard_map/shares/pallas_call | solution.py:298
  73.6 3.7 %all-to-all-start = ((bf16[128,16,128]{2,1,0:T(8,128)(2,1)}), bf16[128,16,128]{2,1,0:T(8,128)(2,1)S(1)}, u32[]{:S(2)}, u32[]{:S(2)}) async-start(bf16[128,16,128]{2,1,0:T(8,128)(2,1)} %bitcast.25), calls=%async_computation | async-start | bytes 1048576 | tf_op jit(solution)/shard_map/all_to_all | solution.py:393
  77.3 0.8 fusion.1
  78.2 1.5 %collective-permute-start.4 = (bf16[3,64,128]{2,1,0:T(8,128)(2,1)S(1)}, bf16[3,64,128]{2,1,0:T(8,128)(2,1)S(1)}, u32[]{:S(2)}, u32[]{:S(2)}) collective-permute-start(bf16[3,64,128]{2,1,0:T(8,128)(2,1)S(1)} %bitcast.27), channel_id=1, source_target_pairs={{0,8},{8,16},{16,24},{24,32},{32,40},{40,48},{48,56},{56,64},{64,7... | collective-permute-start | bytes 147464 | tf_op jit(solution)/shard_map/ppermute | solution.py:26
  79.7 4.1 %collective-permute-start.5 = (bf16[3,64,128]{2,1,0:T(8,128)(2,1)S(1)}, bf16[3,64,128]{2,1,0:T(8,128)(2,1)S(1)}, u32[]{:S(2)}, u32[]{:S(2)}) collective-permute-start(bf16[3,64,128]{2,1,0:T(8,128)(2,1)S(1)} %bitcast.26), channel_id=1, source_target_pairs={{0,120},{8,0},{16,8},{24,16},{32,24},{40,32},{48,40},{56,48},{64,5... | collective-permute-start | bytes 147464 | tf_op jit(solution)/shard_map/ppermute | solution.py:26
  83.9 1.1 fusion
  85.0 2.2 %collective-permute-done.4.top = bf16[3,64,128]{2,1,0:T(8,128)(2,1)S(1)} collective-permute-done((bf16[3,64,128]{2,1,0:T(8,128)(2,1)S(1)}, bf16[3,64,128]{2,1,0:T(8,128)(2,1)S(1)}, u32[]{:S(2)}, u32[]{:S(2)}) %collective-permute-start.4) | collective-permute-done | bytes 49184 | tf_op jit(solution)/shard_map/ppermute | solution.py:26
  87.2 3.8 %all-to-all-done = bf16[128,16,128]{2,1,0:T(8,128)(2,1)S(1)} async-done(((bf16[128,16,128]{2,1,0:T(8,128)(2,1)}), bf16[128,16,128]{2,1,0:T(8,128)(2,1)S(1)}, u32[]{:S(2)}, u32[]{:S(2)}) %all-to-all-start) | async-done | bytes 524320 | tf_op jit(solution)/shard_map/all_to_all | solution.py:393
  91.1 0.9 broadcast_in_dim.2
  92.0 4.6 %all-to-all-start.1 = ((bf16[128,16,128]{2,1,0:T(8,128)(2,1)}), bf16[128,16,128]{2,1,0:T(8,128)(2,1)S(1)}, u32[]{:S(2)}, u32[]{:S(2)}) async-start(bf16[128,16,128]{2,1,0:T(8,128)(2,1)} %broadcast_in_dim.2), calls=%async_computation.1 | async-start | bytes 1048576 | tf_op jit(solution)/shard_map/all_to_all | solution.py:396
  96.7 3.5 %collective-permute-start.6 = (bf16[134,3,128]{2,1,0:T(4,128)(2,1)S(1)}, bf16[134,3,128]{2,1,0:T(4,128)(2,1)S(1)}, u32[]{:S(2)}, u32[]{:S(2)}) collective-permute-start(bf16[134,3,128]{2,1,0:T(4,128)(2,1)S(1)} %pad_maximum_fusion.2), channel_id=1, source_target_pairs={{0,1},{1,2},{2,3},{3,4},{4,5},{5,6},{6,7},{8,9},{9,10},{10,11},{11... | collective-permute-start | bytes 308744 | tf_op jit(solution)/shard_map/ppermute | solution.py:26
  100.4 1.9 %collective-permute-start.7 = (bf16[134,3,128]{2,1,0:T(4,128)(2,1)S(1)}, bf16[134,3,128]{2,1,0:T(4,128)(2,1)S(1)}, u32[]{:S(2)}, u32[]{:S(2)}) collective-permute-start(bf16[134,3,128]{2,1,0:T(4,128)(2,1)S(1)} %pad_maximum_fusion.3), channel_id=1, source_target_pairs={{1,0},{2,1},{3,2},{4,3},{5,4},{6,5},{7,6},{9,8},{10,9},{11,10},{12... | collective-permute-start | bytes 308744 | tf_op jit(solution)/shard_map/ppermute | solution.py:26
  102.3 1.2 collective-permute-done.6.left
  103.5 3.5 %collective-permute-done.7.right = bf16[134,3,128]{2,1,0:T(4,128)(2,1)S(1)} collective-permute-done((bf16[134,3,128]{2,1,0:T(4,128)(2,1)S(1)}, bf16[134,3,128]{2,1,0:T(4,128)(2,1)S(1)}, u32[]{:S(2)}, u32[]{:S(2)}) %collective-permute-start.7) | collective-permute-done | bytes 102944 | tf_op jit(solution)/shard_map/ppermute | solution.py:26
  107.7 14.8 %spread.1 = bf16[8192,128]{1,0:T(8,128)(2,1)} custom-call(bf16[128,64,128]{2,1,0:T(8,128)(2,1)} %bitcast.22, bf16[3,64,128]{2,1,0:T(8,128)(2,1)} %copy-done.5, bf16[3,64,128]{2,1,0:T(8,128)(2,1)} %copy-done.6, bf16[134,3,128]{2,1,0:T(4,128)(2,1)} %copy-done.1, bf16[134,3,128]{2,1,0:T(4,128)(2,1)} %copy-done.2, bf16[8192,128]{1,0:T(8,128)(2,1)} %bitcast.20, ...), custom_call_target="tpu_custom_call" | custom-call | tf_op jit(solution)/shard_map/spread/pallas_call | solution.py:373
  123.3 2.2 %finish.1 = (f32[7,7,128]{2,1,0:T(8,128)}, f32[1,128]{1,0:T(1,128)}, f32[1,128]{1,0:T(1,128)}, f32[1,128]{1,0:T(1,128)}, f32[128,512]{1,0:T(8,128)}, /*index=5*/...) custom-call(bf16[2048,128]{1,0:T(8,128)(2,1)} %bitcast.23, bf16[512,128]{1,0:T(8,128)(2,1)} %wdown_ref.3, ...), custom_call_target="tpu_custom_call" | custom-call | tf_op jit(solution)/shard_map/finish/pallas_call | solution.py:449
  (32 shorter events, 2.8 us)
Async XLA Ops:
  1.5 8.3 %collective-permute-start.1 = (bf16[3,64,128]{2,1,0:T(8,128)(2,1)S(1)}, bf16[3,64,128]{2,1,0:T(8,128)(2,1)S(1)}, u32[]{:S(2)}, u32[]{:S(2)}) collective-permute-start(bf16[3,64,128]{2,1,0:T(8,128)(2,1)S(1)} %get-tuple-element.46), channel_id=1, source_target_pairs={{0,120},{8,0},{16,8},{24,16},{32,24},{40,32},{48,40},{56,48},{64,5... | collective-permute-start | bytes 147464 | tf_op jit(solution)/shard_map/ppermute | solution.py:26
  8.6 6.3 %collective-permute-start = (bf16[3,64,128]{2,1,0:T(8,128)(2,1)S(1)}, bf16[3,64,128]{2,1,0:T(8,128)(2,1)S(1)}, u32[]{:S(2)}, u32[]{:S(2)}) collective-permute-start(bf16[3,64,128]{2,1,0:T(8,128)(2,1)S(1)} %get-tuple-element.47), channel_id=1, source_target_pairs={{0,8},{8,16},{16,24},{24,32},{32,40},{40,48},{48,56},{56,64},{64,7... | collective-permute-start | bytes 147464 | tf_op jit(solution)/shard_map/ppermute | solution.py:26
  9.7 16.8 %copy-start.7 = (bf16[3,64,128]{2,1,0:T(8,128)(2,1)}, bf16[3,64,128]{2,1,0:T(8,128)(2,1)S(1)}, u32[]{:S(2)}) copy-start(bf16[3,64,128]{2,1,0:T(8,128)(2,1)S(1)} %collective-permute-done.1.bottom) | copy-start | bytes 147460
  14.8 11.7 %copy-start.8 = (bf16[3,64,128]{2,1,0:T(8,128)(2,1)}, bf16[3,64,128]{2,1,0:T(8,128)(2,1)S(1)}, u32[]{:S(2)}) copy-start(bf16[3,64,128]{2,1,0:T(8,128)(2,1)S(1)} %collective-permute-done.top) | copy-start | bytes 147460
  14.9 7.2 %collective-permute-start.2 = (bf16[134,3,128]{2,1,0:T(4,128)(2,1)S(1)}, bf16[134,3,128]{2,1,0:T(4,128)(2,1)S(1)}, u32[]{:S(2)}, u32[]{:S(2)}) collective-permute-start(bf16[134,3,128]{2,1,0:T(4,128)(2,1)S(1)} %pad_maximum_fusion), channel_id=1, source_target_pairs={{0,1},{1,2},{2,3},{3,4},{4,5},{5,6},{6,7},{8,9},{9,10},{10,11},{11... | collective-permute-start | bytes 308744 | tf_op jit(solution)/shard_map/ppermute | solution.py:26
  20.2 6.4 %collective-permute-start.3 = (bf16[134,3,128]{2,1,0:T(4,128)(2,1)S(1)}, bf16[134,3,128]{2,1,0:T(4,128)(2,1)S(1)}, u32[]{:S(2)}, u32[]{:S(2)}) collective-permute-start(bf16[134,3,128]{2,1,0:T(4,128)(2,1)S(1)} %pad_maximum_fusion.1), channel_id=1, source_target_pairs={{1,0},{2,1},{3,2},{4,3},{5,4},{6,5},{7,6},{9,8},{10,9},{11,10},{12... | collective-permute-start | bytes 308744 | tf_op jit(solution)/shard_map/ppermute | solution.py:26
  22.1 4.4 %copy-start.3 = (bf16[134,3,128]{2,1,0:T(4,128)(2,1)}, bf16[134,3,128]{2,1,0:T(4,128)(2,1)S(1)}, u32[]{:S(2)}) copy-start(bf16[134,3,128]{2,1,0:T(4,128)(2,1)S(1)} %collective-permute-done.2.left) | copy-start | bytes 308740
  26.5 0.7 copy-start.4
  73.6 17.3 %all-to-all-start = ((bf16[128,16,128]{2,1,0:T(8,128)(2,1)}), bf16[128,16,128]{2,1,0:T(8,128)(2,1)S(1)}, u32[]{:S(2)}, u32[]{:S(2)}) async-start(bf16[128,16,128]{2,1,0:T(8,128)(2,1)} %bitcast.25), calls=%async_computation | async-start | bytes 1048576 | tf_op jit(solution)/shard_map/all_to_all | solution.py:393
  78.2 9.0 %collective-permute-start.4 = (bf16[3,64,128]{2,1,0:T(8,128)(2,1)S(1)}, bf16[3,64,128]{2,1,0:T(8,128)(2,1)S(1)}, u32[]{:S(2)}, u32[]{:S(2)}) collective-permute-start(bf16[3,64,128]{2,1,0:T(8,128)(2,1)S(1)} %bitcast.27), channel_id=1, source_target_pairs={{0,8},{8,16},{16,24},{24,32},{32,40},{40,48},{48,56},{56,64},{64,7... | collective-permute-start | bytes 147464 | tf_op jit(solution)/shard_map/ppermute | solution.py:26
  79.7 16.9 %collective-permute-start.5 = (bf16[3,64,128]{2,1,0:T(8,128)(2,1)S(1)}, bf16[3,64,128]{2,1,0:T(8,128)(2,1)S(1)}, u32[]{:S(2)}, u32[]{:S(2)}) collective-permute-start(bf16[3,64,128]{2,1,0:T(8,128)(2,1)S(1)} %bitcast.26), channel_id=1, source_target_pairs={{0,120},{8,0},{16,8},{24,16},{32,24},{40,32},{48,40},{56,48},{64,5... | collective-permute-start | bytes 147464 | tf_op jit(solution)/shard_map/ppermute | solution.py:26
  87.2 19.9 %copy-start.5 = (bf16[3,64,128]{2,1,0:T(8,128)(2,1)}, bf16[3,64,128]{2,1,0:T(8,128)(2,1)S(1)}, u32[]{:S(2)}) copy-start(bf16[3,64,128]{2,1,0:T(8,128)(2,1)S(1)} %collective-permute-done.4.top) | copy-start | bytes 147460
  92.0 30.5 %all-to-all-start.1 = ((bf16[128,16,128]{2,1,0:T(8,128)(2,1)}), bf16[128,16,128]{2,1,0:T(8,128)(2,1)S(1)}, u32[]{:S(2)}, u32[]{:S(2)}) async-start(bf16[128,16,128]{2,1,0:T(8,128)(2,1)} %broadcast_in_dim.2), calls=%async_computation.1 | async-start | bytes 1048576 | tf_op jit(solution)/shard_map/all_to_all | solution.py:396
  96.6 10.4 %copy-start.6 = (bf16[3,64,128]{2,1,0:T(8,128)(2,1)}, bf16[3,64,128]{2,1,0:T(8,128)(2,1)S(1)}, u32[]{:S(2)}) copy-start(bf16[3,64,128]{2,1,0:T(8,128)(2,1)S(1)} %collective-permute-done.5.bottom) | copy-start | bytes 147460
  96.7 6.8 %collective-permute-start.6 = (bf16[134,3,128]{2,1,0:T(4,128)(2,1)S(1)}, bf16[134,3,128]{2,1,0:T(4,128)(2,1)S(1)}, u32[]{:S(2)}, u32[]{:S(2)}) collective-permute-start(bf16[134,3,128]{2,1,0:T(4,128)(2,1)S(1)} %pad_maximum_fusion.2), channel_id=1, source_target_pairs={{0,1},{1,2},{2,3},{3,4},{4,5},{5,6},{6,7},{8,9},{9,10},{10,11},{11... | collective-permute-start | bytes 308744 | tf_op jit(solution)/shard_map/ppermute | solution.py:26
  100.4 6.6 %collective-permute-start.7 = (bf16[134,3,128]{2,1,0:T(4,128)(2,1)S(1)}, bf16[134,3,128]{2,1,0:T(4,128)(2,1)S(1)}, u32[]{:S(2)}, u32[]{:S(2)}) collective-permute-start(bf16[134,3,128]{2,1,0:T(4,128)(2,1)S(1)} %pad_maximum_fusion.3), channel_id=1, source_target_pairs={{1,0},{2,1},{3,2},{4,3},{5,4},{6,5},{7,6},{9,8},{10,9},{11,10},{12... | collective-permute-start | bytes 308744 | tf_op jit(solution)/shard_map/ppermute | solution.py:26
  103.5 3.5 %copy-start.1 = (bf16[134,3,128]{2,1,0:T(4,128)(2,1)}, bf16[134,3,128]{2,1,0:T(4,128)(2,1)S(1)}, u32[]{:S(2)}) copy-start(bf16[134,3,128]{2,1,0:T(4,128)(2,1)S(1)} %collective-permute-done.6.left) | copy-start | bytes 308740
  107.0 0.7 copy-start.2
  122.5 0.8 copy-start
